TPU v7x, 256 devices: a whole 4x4x8 slice. The times are simulated.
256 devices in a mesh: seq: 128 (over x_hi, y, z, core), fsdp: 2 (over x_lo).
Axes of the slice: x: 4 (x_hi: 2, x_lo: 2; x = x_hi * 2 + x_lo), y: 4, z: 8, core: 2. Of those that a mesh axis runs over, the one named last changes fastest.
Arguments:
- dna_embed: bfloat16 [2, 32768, 1024], P('fsdp', 'seq'), may hold values from -60 to 60
- site_owner: int32 [2, 32768, 1], P('fsdp', 'seq'), may hold values from 0 to 127; in each aligned block of 256 rows (0 to 255, 256 to 511, ..., all dimensions but the last counted through in order) at most 4 rows name the same one
- site_row: int32 [2, 32768], P('fsdp', 'seq'), may hold values from 0 to 2047
- variant_table: bfloat16 [262144, 1024], P('seq'), may hold values from -6 to 6
- norm_gain: float32 [1024], replicated, may hold values from 0.1 to 1.9
- conv_weight: bfloat16 [7, 1024], replicated, may hold values from -2.390625 to 2.390625
- qkv_weight: bfloat16 [1024, 3072], P(None, 'fsdp'), may hold values from -4 to 4
- out_weight: bfloat16 [1024, 1024], P(None, 'fsdp'), may hold values from -0.1875 to 0.1875
- attn_gain: float32 [1024], replicated, may hold values from 0.1 to 1.9
Outputs:
- mixed: bfloat16 [2, 32768, 1024], P('fsdp', 'seq')
Inputs may be any that keep to these rules, and one draw needn't show every extreme that they name: `site_owner`: in each haplotype the 256 positions of one device name one site range at most 4 times, and some site range exactly 4 times.
All inputs are finite; a program needn't handle non-finite values.
Results may differ from a plain program's by a relative error of at most 0.0075.
The roundings to bfloat16 on the way count: a program that leaves them out, or rounds other values in their place, can miss the bound.
Values may be sent and summed in bfloat16 or wider, within the bound.
No kernel may reach another device: no remote copies, remote signals or barrier semaphores. Data moves between devices by JAX's collectives and lax.ppermute only.
A program may use at most 128 MiB of HBM per device.

v0:
```python
import jax
import jax.numpy as jnp
from jax import lax
from jax.sharding import PartitionSpec as P

HEAD = 64
WINDOW = 2048


EPSILON = 1e-05


def shifted(value, axis, steps):
    count = lax.axis_size(axis)
    first, last = (max(0, -steps), min(count, count - steps))
    return lax.ppermute(value, axis, [(source, source + steps) for source in range(first, last)])


def rms_scale(values, gain):
    return values * lax.rsqrt(jnp.mean(values * values, axis=-1, keepdims=True) + EPSILON) * gain


def local(
    dna_embed,
    site_owner,
    site_row,
    variant_table,
    norm_gain,
    conv_weight,
    qkv_weight,
    out_weight,
    attn_gain,
):
    seq_rank = lax.axis_index("seq")
    seq_count = lax.axis_size("seq")
    tok_rows = dna_embed.shape[1]
    model_width = dna_embed.shape[2]
    slot_count = max(2, 2 * tok_rows // seq_count)
    owner_ids = site_owner[0, :, 0]
    wanted_rows = site_row[0]
    owner_onehot = (owner_ids[:, None] == jnp.arange(seq_count, dtype=jnp.int32)[None, :]).astype(
        jnp.int32
    )
    earlier_same = jnp.cumsum(owner_onehot, axis=0) - owner_onehot
    rank_within = jnp.sum(earlier_same * owner_onehot, axis=1)
    slot_index = owner_ids * slot_count + rank_within
    request_table = jnp.zeros((seq_count * slot_count,), jnp.int32).at[slot_index].set(wanted_rows)
    request_table = request_table.reshape(seq_count, slot_count)
    found = variant_table[
        lax.all_to_all(request_table, "seq", split_axis=0, concat_axis=0, tiled=True)
    ]
    fetched = lax.all_to_all(found, "seq", split_axis=0, concat_axis=0, tiled=True)
    site_embed = fetched.reshape(seq_count * slot_count, model_width)[slot_index]
    resid = dna_embed[0].astype(jnp.float32) + site_embed.astype(jnp.float32)
    normed = rms_scale(resid, norm_gain).astype(jnp.bfloat16)
    taps = conv_weight.shape[0]
    rim_rows = shifted(normed[tok_rows - (taps - 1) :], "seq", 1)
    padded = jnp.concatenate([rim_rows, normed], axis=0)
    conv_sum = jnp.zeros((tok_rows, model_width), jnp.float32)
    for tap in range(taps):
        conv_sum = conv_sum + conv_weight[tap].astype(jnp.float32) * padded[
            taps - 1 - tap : taps - 1 - tap + tok_rows
        ].astype(jnp.float32)
    conv_out = conv_sum.astype(jnp.bfloat16)
    full_qkv, full_out = (
        lax.all_gather(qkv_weight, "fsdp", axis=1, tiled=True),
        lax.all_gather(out_weight, "fsdp", axis=1, tiled=True),
    )
    qkv = jnp.dot(conv_out, full_qkv, preferred_element_type=jnp.float32).astype(jnp.bfloat16)
    query = qkv[:, :model_width]
    local_kv = qkv[:, model_width:]
    reach_count = WINDOW // tok_rows
    earlier = [shifted(local_kv, "seq", reach_count - offset) for offset in range(reach_count)]
    keys_all = jnp.concatenate(earlier + [local_kv], axis=0)
    key_total = keys_all.shape[0]
    q_where = seq_rank * tok_rows + jnp.arange(tok_rows, dtype=jnp.int32)
    k_where = seq_rank * tok_rows - reach_count * tok_rows + jnp.arange(key_total, dtype=jnp.int32)
    allowed = (
        (k_where[None, :] <= q_where[:, None])
        & (k_where[None, :] > q_where[:, None] - WINDOW)
        & (k_where[None, :] >= 0)
    )
    head_count = model_width // HEAD
    group_heads = min(4, head_count)
    group_count = head_count // group_heads
    span = group_heads * HEAD

    def head_group(group_index):
        first_col = group_index * span
        q_group = lax.dynamic_slice_in_dim(query, first_col, span, 1).reshape(
            tok_rows, group_heads, HEAD
        )
        k_group = lax.dynamic_slice_in_dim(keys_all, first_col, span, 1).reshape(
            key_total, group_heads, HEAD
        )
        v_group = lax.dynamic_slice_in_dim(keys_all, model_width + first_col, span, 1).reshape(
            key_total, group_heads, HEAD
        )
        scores = jnp.einsum(
            "qhd,khd->hqk", q_group, k_group, preferred_element_type=jnp.float32
        ) * HEAD ** (-0.5)
        scores = jnp.where(allowed[None, :, :], scores, -jnp.inf)
        highest = jnp.max(scores, axis=-1, keepdims=True)
        expo = jnp.exp(scores - highest)
        probs = (expo / jnp.sum(expo, axis=-1, keepdims=True)).astype(jnp.bfloat16)
        attended = jnp.einsum("hqk,khd->qhd", probs, v_group, preferred_element_type=jnp.float32)
        return attended.reshape(tok_rows, span)

    grouped = lax.map(head_group, jnp.arange(group_count, dtype=jnp.int32))
    attended = jnp.moveaxis(grouped, 0, 1).reshape(tok_rows, model_width)
    attn_normed = rms_scale(attended, attn_gain).astype(jnp.bfloat16)
    mixed = jnp.dot(attn_normed, full_out, preferred_element_type=jnp.float32).astype(jnp.bfloat16)
    return mixed[None, :, :]


def solution(mesh):
    in_specs = (
        P("fsdp", "seq", None),
        P("fsdp", "seq", None),
        P("fsdp", "seq"),
        P("seq", None),
        P(),
        P(),
        P(None, "fsdp"),
        P(None, "fsdp"),
        P(),
    )
    out_specs = P("fsdp", "seq", None)
    return jax.shard_map(local, mesh=mesh, in_specs=in_specs, out_specs=out_specs, check_vma=False)
```

profile of v0, /device:TPU:25, one launch (start us, length us, event | category | flops | bytes accessed | tf_op | source)
XLA Modules:
  0.0 536.0 jit_solution(8549622350062569202)
XLA Ops:
  9.9 1.6 scatter_custom_fusion
  11.6 25.6 %all_to_all.17 = s32[128,1,4]{2,1,0:T(1,128)S(1)} all-to-all(s32[128,1,4]{2,1,0:T(1,128)S(1)} %bitcast.93), channel_id=1, replica_groups=mesh['seq'=128,'fsdp'=2] {'seq'}, dimensions={0} | all-to-all | bytes 4096 | tf_op jit(solution)/shard_map/all_to_all | solution.py:50
  37.3 5.5 %gather_fusion = bf16[512,1024]{1,0:T(8,128)(2,1)S(1)} fusion(bf16[2048,1024]{1,0:T(8,128)(2,1)} %param.14, s32[1024]{0:T(1024)S(1)} %pad_clamp_fusion.1), kind=kCustom, calls=%fused_computation | custom fusion | bytes 2099200 | tf_op jit(solution)/shard_map/gather | solution.py:49
  42.9 1.2 reshape.156
  44.1 7.9 %all-to-all-start.1 = ((bf16[128,4,1024]{2,1,0:T(4,128)(2,1)}), bf16[128,4,1024]{2,1,0:T(4,128)(2,1)S(1)}, u32[]{:S(2)}, u32[]{:S(2)}) async-start(bf16[128,4,1024]{2,1,0:T(4,128)(2,1)} %reshape.156), calls=%async_computation.1 | async-start | bytes 2097152 | tf_op jit(solution)/shard_map/all_to_all | solution.py:52
  52.1 29.8 %all-to-all-done.1 = bf16[128,4,1024]{2,1,0:T(4,128)(2,1)S(1)} async-done(((bf16[128,4,1024]{2,1,0:T(4,128)(2,1)}), bf16[128,4,1024]{2,1,0:T(4,128)(2,1)S(1)}, u32[]{:S(2)}, u32[]{:S(2)}) %all-to-all-start.1) | async-done | bytes 1048608 | tf_op jit(solution)/shard_map/all_to_all | solution.py:52
  82.1 1.2 gather_fusion.1
  83.8 1.9 collective-permute-start
  86.9 22.2 %all-gather.3.cloned.1.call-done = bf16[1024,3072]{1,0:T(8,128)(2,1)} async-done(((bf16[1024,1536]{1,0:T(8,128)(2,1)}), bf16[1024,3072]{1,0:T(8,128)(2,1)}) %all-gather.3.cloned.1.call-update) | async-done | bytes 6291472 | tf_op jit(solution)/shard_map/all_gather | solution.py:66
  109.1 5.3 convolution_convert_fusion
  114.5 6.6 %collective-permute-start.1 = (bf16[256,2048]{1,0:T(8,128)(2,1)S(1)}, bf16[256,2048]{1,0:T(8,128)(2,1)}, u32[]{:S(2)}, u32[]{:S(2)}) collective-permute-start(bf16[256,2048]{1,0:T(8,128)(2,1)S(1)} %slice.88), channel_id=1, source_target_pairs={{0,16},{2,18},{4,20},{6,22},{8,24},{10,26},{12,28},{14,30},{16,32}... | collective-permute-start | bytes 3145736 | tf_op jit(solution)/shard_map/ppermute | solution.py:16
  121.1 5.5 %collective-permute-start.2 = (bf16[256,2048]{1,0:T(8,128)(2,1)S(1)}, bf16[256,2048]{1,0:T(8,128)(2,1)}, u32[]{:S(2)}, u32[]{:S(2)}) collective-permute-start(bf16[256,2048]{1,0:T(8,128)(2,1)S(1)} %slice.88), channel_id=1, source_target_pairs={{0,14},{2,16},{4,18},{6,20},{8,22},{10,24},{12,26},{14,28},{16,30}... | collective-permute-start | bytes 3145736 | tf_op jit(solution)/shard_map/ppermute | solution.py:16
  126.6 5.0 collective-permute-start.3
  131.6 4.0 collective-permute-start.4
  135.7 2.5 collective-permute-start.5
  139.0 17.8 %collective-permute-done.1 = bf16[256,2048]{1,0:T(8,128)(2,1)} collective-permute-done((bf16[256,2048]{1,0:T(8,128)(2,1)S(1)}, bf16[256,2048]{1,0:T(8,128)(2,1)}, u32[]{:S(2)}, u32[]{:S(2)}) %collective-permute-start.1) | collective-permute-done | bytes 1048608 | tf_op jit(solution)/shard_map/ppermute | solution.py:16
  156.9 21.0 %collective-permute-start.6 = (bf16[256,2048]{1,0:T(8,128)(2,1)S(1)}, bf16[256,2048]{1,0:T(8,128)(2,1)S(1)}, u32[]{:S(2)}, u32[]{:S(2)}) collective-permute-start(bf16[256,2048]{1,0:T(8,128)(2,1)S(1)} %slice.88), channel_id=1, source_target_pairs={{0,6},{2,8},{4,10},{6,12},{8,14},{10,16},{12,18},{14,20},{16,22},{... | collective-permute-start | bytes 3145736 | tf_op jit(solution)/shard_map/ppermute | solution.py:16
  177.8 2.3 constant_dynamic-update-slice_fusion.9
  180.1 76.4 %collective-permute-done.2 = bf16[256,2048]{1,0:T(8,128)(2,1)} collective-permute-done((bf16[256,2048]{1,0:T(8,128)(2,1)S(1)}, bf16[256,2048]{1,0:T(8,128)(2,1)}, u32[]{:S(2)}, u32[]{:S(2)}) %collective-permute-start.2) | collective-permute-done | bytes 1048608 | tf_op jit(solution)/shard_map/ppermute | solution.py:16
  256.5 2.1 collective-permute-start.7
  258.6 2.3 constant_dynamic-update-slice_fusion.8
  260.9 21.8 %collective-permute-done.3 = bf16[256,2048]{1,0:T(8,128)(2,1)} collective-permute-done((bf16[256,2048]{1,0:T(8,128)(2,1)S(1)}, bf16[256,2048]{1,0:T(8,128)(2,1)}, u32[]{:S(2)}, u32[]{:S(2)}) %collective-permute-start.3) | collective-permute-done | bytes 1048608 | tf_op jit(solution)/shard_map/ppermute | solution.py:16
  282.8 57.0 %collective-permute-start.8 = (bf16[256,2048]{1,0:T(8,128)(2,1)S(1)}, bf16[256,2048]{1,0:T(8,128)(2,1)S(1)}, u32[]{:S(2)}, u32[]{:S(2)}) collective-permute-start(bf16[256,2048]{1,0:T(8,128)(2,1)S(1)} %slice.88), channel_id=1, source_target_pairs={{0,2},{2,4},{4,6},{6,8},{8,10},{10,12},{12,14},{14,16},{16,18},{18... | collective-permute-start | bytes 3145736 | tf_op jit(solution)/shard_map/ppermute | solution.py:16
  339.8 2.3 constant_dynamic-update-slice_fusion.7
  342.1 2.4 constant_dynamic-update-slice_fusion.6
  344.5 16.0 %collective-permute-done.5 = bf16[256,2048]{1,0:T(8,128)(2,1)} collective-permute-done((bf16[256,2048]{1,0:T(8,128)(2,1)S(1)}, bf16[256,2048]{1,0:T(8,128)(2,1)}, u32[]{:S(2)}, u32[]{:S(2)}) %collective-permute-start.5) | collective-permute-done | bytes 1048608 | tf_op jit(solution)/shard_map/ppermute | solution.py:16
  360.5 2.3 constant_dynamic-update-slice_fusion.5
  362.8 75.1 %collective-permute-done.6 = bf16[256,2048]{1,0:T(8,128)(2,1)S(1)} collective-permute-done((bf16[256,2048]{1,0:T(8,128)(2,1)S(1)}, bf16[256,2048]{1,0:T(8,128)(2,1)S(1)}, u32[]{:S(2)}, u32[]{:S(2)}) %collective-permute-start.6) | collective-permute-done | bytes 1048608 | tf_op jit(solution)/shard_map/ppermute | solution.py:16
  439.0 7.5 %collective-permute-done.7 = bf16[256,2048]{1,0:T(8,128)(2,1)S(1)} collective-permute-done((bf16[256,2048]{1,0:T(8,128)(2,1)S(1)}, bf16[256,2048]{1,0:T(8,128)(2,1)S(1)}, u32[]{:S(2)}, u32[]{:S(2)}) %collective-permute-start.7) | collective-permute-done | bytes 1048608 | tf_op jit(solution)/shard_map/ppermute | solution.py:16
  447.6 11.5 %collective-permute-done.8 = bf16[256,2048]{1,0:T(8,128)(2,1)S(1)} collective-permute-done((bf16[256,2048]{1,0:T(8,128)(2,1)S(1)}, bf16[256,2048]{1,0:T(8,128)(2,1)S(1)}, u32[]{:S(2)}, u32[]{:S(2)}) %collective-permute-start.8) | collective-permute-done | bytes 1048608 | tf_op jit(solution)/shard_map/ppermute | solution.py:16
  460.1 1.1 constant_dynamic-update-slice_fusion.1
  461.2 12.2 %copy.20 = bf16[2304,2048]{0,1:T(8,128)(2,1)} copy(bf16[2304,2048]{1,0:T(8,128)(2,1)} %constant_dynamic-update-slice_fusion.1) | data formatting | bytes 18874368
  473.4 49.8 %while.13 = (s32[]{:T(128)}, f32[4,256,256]{1,2,0:T(8,128)}, s32[4]{0:T(128)S(1)}, bf16[2304,2048]{0,1:T(8,128)(2,1)}, bf16[256,1024]{1,0:T(8,128)(2,1)}, /*inde...) while((s32[]{:T(128)}, f32[4,256,256]{1,2,0:T(8,128)}, ...), condition=%wide.region_8.9_spmd.clone, body=%wide.region_5.8_spmd.clone.sunk | while | flops 929568256 | bytes 11622414 | solution.py:109
  474.7 1.8 constant_dynamic-slice_fusion.5
  478.1 3.5 fusion.70
  481.6 3.5 fusion.71
  487.1 1.8 constant_dynamic-slice_fusion.5
  490.6 3.5 fusion.70
  494.1 3.5 fusion.71
  499.6 1.8 constant_dynamic-slice_fusion.5
  503.0 3.5 fusion.70
  506.5 3.5 fusion.71
  512.0 1.8 constant_dynamic-slice_fusion.5
  515.5 3.5 fusion.70
  519.0 3.5 fusion.71
  523.2 1.4 fusion.19
  524.6 1.4 fusion.18
  526.1 3.1 fusion.16
  (67 shorter events, 21.7 us)
Async XLA Ops:
  6.5 102.6 %all-gather.3.cloned.1.call-start = ((), (), s32[]{:S(2)}) async-start(), calls=%async_computation.2 | async-start | bytes 9437184 | tf_op jit(solution)/shard_map/all_gather | solution.py:66
  37.3 46.0 %copy-start = (bf16[1,256,1024]{2,1,0:T(8,128)(2,1)S(1)}, bf16[1,256,1024]{2,1,0:T(8,128)(2,1)}, u32[]{:S(2)}) copy-start(bf16[1,256,1024]{2,1,0:T(8,128)(2,1)} %param.11) | copy-start | bytes 1572868
  37.3 46.2 %copy-start.2 = (f32[1024]{0:T(1024)S(1)}, f32[1024]{0:T(1024)}, u32[]{:S(2)}) copy-start(f32[1024]{0:T(1024)} %param.15) | copy-start | bytes 12292
  37.3 48.4 %copy-start.1 = (bf16[7,1024]{1,0:T(8,128)(2,1)S(1)}, bf16[7,1024]{1,0:T(8,128)(2,1)}, u32[]{:S(2)}) copy-start(bf16[7,1024]{1,0:T(8,128)(2,1)} %param.16) | copy-start | bytes 43012
  44.1 37.7 %all-to-all-start.1 = ((bf16[128,4,1024]{2,1,0:T(4,128)(2,1)}), bf16[128,4,1024]{2,1,0:T(4,128)(2,1)S(1)}, u32[]{:S(2)}, u32[]{:S(2)}) async-start(bf16[128,4,1024]{2,1,0:T(4,128)(2,1)} %reshape.156), calls=%async_computation.1 | async-start | bytes 2097152 | tf_op jit(solution)/shard_map/all_to_all | solution.py:52
  52.0 474.1 %all-gather.5.cloned.1.call-start = ((), (), s32[]{:S(2)}) async-start(), calls=%async_computation.3 | async-start | bytes 3145728 | tf_op jit(solution)/shard_map/all_gather | solution.py:67
  83.8 3.1 collective-permute-start
  114.5 42.4 %collective-permute-start.1 = (bf16[256,2048]{1,0:T(8,128)(2,1)S(1)}, bf16[256,2048]{1,0:T(8,128)(2,1)}, u32[]{:S(2)}, u32[]{:S(2)}) collective-permute-start(bf16[256,2048]{1,0:T(8,128)(2,1)S(1)} %slice.88), channel_id=1, source_target_pairs={{0,16},{2,18},{4,20},{6,22},{8,24},{10,26},{12,28},{14,30},{16,32}... | collective-permute-start | bytes 3145736 | tf_op jit(solution)/shard_map/ppermute | solution.py:16
  121.1 135.4 %collective-permute-start.2 = (bf16[256,2048]{1,0:T(8,128)(2,1)S(1)}, bf16[256,2048]{1,0:T(8,128)(2,1)}, u32[]{:S(2)}, u32[]{:S(2)}) collective-permute-start(bf16[256,2048]{1,0:T(8,128)(2,1)S(1)} %slice.88), channel_id=1, source_target_pairs={{0,14},{2,16},{4,18},{6,20},{8,22},{10,24},{12,26},{14,28},{16,30}... | collective-permute-start | bytes 3145736 | tf_op jit(solution)/shard_map/ppermute | solution.py:16
  126.6 156.2 %collective-permute-start.3 = (bf16[256,2048]{1,0:T(8,128)(2,1)S(1)}, bf16[256,2048]{1,0:T(8,128)(2,1)}, u32[]{:S(2)}, u32[]{:S(2)}) collective-permute-start(bf16[256,2048]{1,0:T(8,128)(2,1)S(1)} %slice.88), channel_id=1, source_target_pairs={{0,12},{2,14},{4,16},{6,18},{8,20},{10,22},{12,24},{14,26},{16,28}... | collective-permute-start | bytes 3145736 | tf_op jit(solution)/shard_map/ppermute | solution.py:16
  131.6 210.5 %collective-permute-start.4 = (bf16[256,2048]{1,0:T(8,128)(2,1)S(1)}, bf16[256,2048]{1,0:T(8,128)(2,1)}, u32[]{:S(2)}, u32[]{:S(2)}) collective-permute-start(bf16[256,2048]{1,0:T(8,128)(2,1)S(1)} %slice.88), channel_id=1, source_target_pairs={{0,10},{2,12},{4,14},{6,16},{8,18},{10,20},{12,22},{14,24},{16,26}... | collective-permute-start | bytes 3145736 | tf_op jit(solution)/shard_map/ppermute | solution.py:16
  135.7 224.9 %collective-permute-start.5 = (bf16[256,2048]{1,0:T(8,128)(2,1)S(1)}, bf16[256,2048]{1,0:T(8,128)(2,1)}, u32[]{:S(2)}, u32[]{:S(2)}) collective-permute-start(bf16[256,2048]{1,0:T(8,128)(2,1)S(1)} %slice.88), channel_id=1, source_target_pairs={{0,8},{2,10},{4,12},{6,14},{8,16},{10,18},{12,20},{14,22},{16,24},... | collective-permute-start | bytes 3145736 | tf_op jit(solution)/shard_map/ppermute | solution.py:16
  156.9 281.1 %collective-permute-start.6 = (bf16[256,2048]{1,0:T(8,128)(2,1)S(1)}, bf16[256,2048]{1,0:T(8,128)(2,1)S(1)}, u32[]{:S(2)}, u32[]{:S(2)}) collective-permute-start(bf16[256,2048]{1,0:T(8,128)(2,1)S(1)} %slice.88), channel_id=1, source_target_pairs={{0,6},{2,8},{4,10},{6,12},{8,14},{10,16},{12,18},{14,20},{16,22},{... | collective-permute-start | bytes 3145736 | tf_op jit(solution)/shard_map/ppermute | solution.py:16
  256.5 190.0 %collective-permute-start.7 = (bf16[256,2048]{1,0:T(8,128)(2,1)S(1)}, bf16[256,2048]{1,0:T(8,128)(2,1)S(1)}, u32[]{:S(2)}, u32[]{:S(2)}) collective-permute-start(bf16[256,2048]{1,0:T(8,128)(2,1)S(1)} %slice.88), channel_id=1, source_target_pairs={{0,4},{2,6},{4,8},{6,10},{8,12},{10,14},{12,16},{14,18},{16,20},{1... | collective-permute-start | bytes 3145736 | tf_op jit(solution)/shard_map/ppermute | solution.py:16
  282.8 176.3 %collective-permute-start.8 = (bf16[256,2048]{1,0:T(8,128)(2,1)S(1)}, bf16[256,2048]{1,0:T(8,128)(2,1)S(1)}, u32[]{:S(2)}, u32[]{:S(2)}) collective-permute-start(bf16[256,2048]{1,0:T(8,128)(2,1)S(1)} %slice.88), channel_id=1, source_target_pairs={{0,2},{2,4},{4,6},{6,8},{8,10},{10,12},{12,14},{14,16},{16,18},{18... | collective-permute-start | bytes 3145736 | tf_op jit(solution)/shard_map/ppermute | solution.py:16
  473.4 51.2 %copy-start.3 = (f32[1024]{0:T(1024)S(1)}, f32[1024]{0:T(1024)}, u32[]{:S(2)}) copy-start(f32[1024]{0:T(1024)} %param.19) | copy-start | bytes 12292
Sparse Core Ops, SparseCore 0:
  9.1 99.9 all-gather.2
  131.7 48.2 all-gather.4
where the time goes:
time: 543 us; the launch traced here: 536 us
  waiting for transfers between devices  280 us (52%)
  starting transfers between devices  114 us (21%)
  local copies, waits for them, and re-layouts  56.4 us (10%)
  matrix products  36.3 us (7%)
  blocking collectives  25.6 us (5%)
  between operations  13.7 us (3%)
  other arithmetic  7.74 us (1%)
    ppermute x9, waiting for transfers between devices, shifted(): lax.ppermute(value, axis, [(source, source + steps) for source in range(f...  227 us
    ppermute x9, starting transfers between devices, shifted(): lax.ppermute(value, axis, [(source, source + steps) for source in range(f...  106 us
    all_to_all x1, waiting for transfers between devices, local(): lax.all_to_all(found, 'seq', split_axis=0, concat_axis=0, tiled=True)  29.8 us
    unnamed x18, local copies, waits for them, and re-layouts  27 us
    all_to_all x1, blocking collectives, local(): lax.all_to_all(request_table, 'seq', split_axis=0, concat_axis=0, tiled=T...  25.6 us
    all_gather x1, waiting for transfers between devices, local(): lax.all_gather(qkv_weight, 'fsdp', axis=1, tiled=True)  22.2 us
    sub x4, matrix products, head_group(): expo = jnp.exp(scores - highest)  14 us
    dot_general x4, matrix products, head_group(): jnp.einsum('hqk,khd->qhd', probs, v_group, preferred_element_type=jnp.flo...  13.9 us
  transfers between devices with their start and end apart: 12, of which 10 were waited for; matrix products, arithmetic and copies ran while one was open for 17% of the time, Pallas kernels for 0%

commit v1 on v0

v1 whole, which is shorter than its diff:
```python
import jax
import jax.numpy as jnp
from jax import lax
from jax.experimental import pallas as pl
from jax.experimental.pallas import tpu as pltpu
from jax.sharding import PartitionSpec as P

HEAD = 64
WINDOW = 2048
EPSILON = 1e-05
ROWS = 256
D = 1024
HALF = 512
OWNERS = 128
SLOTS = 4
HOPS = 4
BLOCKS = 2 * (HOPS + 1)
SPAN = WINDOW // ROWS + 1
LOG2E = 1.4426950408889634

bf16 = jnp.bfloat16
f32 = jnp.float32


def vmem():
    return pl.BlockSpec(memory_space=pltpu.VMEM)


def anywhere():
    return pl.BlockSpec(memory_space=pl.ANY)


def cost(flops, moved):
    return pl.CostEstimate(flops=flops, bytes_accessed=moved, transcendentals=0)


def request_kernel(owner_col, owner_row, row_row, table, slot):
    oc, orow = owner_col[...], owner_row[...]
    later = lax.broadcasted_iota(jnp.int32, (ROWS, ROWS), 0) < lax.broadcasted_iota(jnp.int32, (ROWS, ROWS), 1)
    rank = jnp.sum(jnp.where((oc == orow) & later, 1, 0), axis=0, keepdims=True)
    mine = lax.broadcasted_iota(jnp.int32, (OWNERS, ROWS), 0) == orow
    lane = lax.broadcasted_iota(jnp.int32, (OWNERS, 128), 1)
    out = jnp.zeros((OWNERS, 128), jnp.int32)
    for k in range(SLOTS):
        column = jnp.sum(jnp.where(mine & (rank == k), row_row[...], 0), axis=1, keepdims=True)
        out = jnp.where(lane == k, column, out)
    table[...] = out
    slot[...] = orow * SLOTS + rank


def norm_kernel(fetched, slot, dna, gain, normed):
    index = slot[...]
    pick = (lax.broadcasted_iota(jnp.int32, (OWNERS * SLOTS, ROWS), 0) == index).astype(f32).astype(bf16)
    site = lax.dot_general(pick, fetched[...], (((0,), (0,)), ((), ())), preferred_element_type=f32)
    resid = dna[...].astype(f32) + site
    mean = jnp.mean(resid * resid, axis=1, keepdims=True)
    normed[...] = (resid * lax.rsqrt(mean + EPSILON) * gain[...]).astype(bf16)


def conv_kernel(normed, rim, taps, out, padded):
    padded[pl.ds(2, 6), :] = rim[...].astype(f32)
    padded[pl.ds(8, ROWS), :] = normed[...].astype(f32)
    total = jnp.zeros((ROWS, D), f32)
    for tap in range(7):
        total = total + taps[pl.ds(tap, 1), :].astype(f32) * padded[pl.ds(8 - tap, ROWS), :]
    out[...] = total.astype(bf16)


def attend_kernel(*refs):
    own, other = refs[0 : HOPS + 1], refs[HOPS + 1 : 2 * HOPS + 2]
    wq, wk, wv, mine, theirs, xs, qs, ks, vs, mask, sc0, sc1, sems = refs[2 * HOPS + 2 :]
    seq = lax.axis_index("seq")
    par = lax.rem(seq, 2)
    chip = seq // 2
    copies = []
    for k in range(HOPS + 1):
        base = 2 * (HOPS - k) * ROWS
        here = pl.multiple_of(base + par * ROWS, ROWS)
        there = pl.multiple_of(base + (1 - par) * ROWS, ROWS)
        copies.append(pltpu.make_async_copy(own[k], xs.at[pl.ds(here, ROWS), :], sems.at[2 * k]))
        copies.append(pltpu.make_async_copy(other[k], xs.at[pl.ds(there, ROWS), :], sems.at[2 * k + 1]))
    for copy in copies:
        copy.start()
    row = lax.broadcasted_iota(jnp.int32, (ROWS, ROWS), 0)
    col = lax.broadcasted_iota(jnp.int32, (ROWS, ROWS), 1)
    for qb in range(2):
        for kb in range(SPAN):
            live = chip * 2 - 2 * HOPS + qb + kb >= 0
            ok = jnp.broadcast_to(live, (ROWS, ROWS))
            if kb == 0:
                ok = ok & (col > row)
            if kb == SPAN - 1:
                ok = col <= row
            mask[qb, :, pl.ds(kb * ROWS, ROWS)] = jnp.where(ok, 0.0, -jnp.inf).astype(f32)
    for copy in copies:
        copy.wait()

    def project(b, carry):
        at = pl.ds(pl.multiple_of(b * ROWS, ROWS), ROWS)
        x = xs[at, :]
        ks[at, :] = jnp.dot(x, wk[...], preferred_element_type=f32).astype(bf16)
        vs[at, :] = jnp.dot(x, wv[...], preferred_element_type=f32).astype(bf16)
        return carry

    lax.fori_loop(0, BLOCKS, project, 0)

    def project_q(b, carry):
        at = pl.ds(pl.multiple_of(b * ROWS, ROWS), ROWS)
        x = xs[pl.ds(pl.multiple_of((b + 2 * HOPS) * ROWS, ROWS), ROWS), :]
        qs[at, :] = jnp.dot(x, wq[...], preferred_element_type=f32).astype(bf16)
        return carry

    lax.fori_loop(0, 2, project_q, 0)

    lane = lax.broadcasted_iota(jnp.int32, (ROWS, 128), 1)

    def pair(step, carry):
        qb, hp = step // 4, lax.rem(step, 4)
        lanes = pl.ds(pl.multiple_of(hp * 128, 128), 128)
        q = qs[pl.ds(pl.multiple_of(qb * ROWS, ROWS), ROWS), lanes]
        outs = []
        for h, sc in ((0, sc0), (1, sc1)):
            qh = jnp.where((lane < HEAD) == (h == 0), q, jnp.zeros_like(q))
            top = None
            for kb in range(SPAN):
                at = pl.ds(pl.multiple_of((qb + kb) * ROWS, ROWS), ROWS)
                s = lax.dot_general(qh, ks[at, lanes], (((1,), (1,)), ((), ())), preferred_element_type=f32)
                s = s + mask[qb, :, pl.ds(kb * ROWS, ROWS)]
                sc[:, pl.ds(kb * ROWS, ROWS)] = s
                part = jnp.maximum(s[:, :128], s[:, 128:])
                top = part if top is None else jnp.maximum(top, part)
            top = jnp.max(top, axis=1, keepdims=True)
            total = None
            for kb in range(SPAN):
                e = jnp.exp2((sc[:, pl.ds(kb * ROWS, ROWS)] - top) * (LOG2E * HEAD ** (-0.5)))
                sc[:, pl.ds(kb * ROWS, ROWS)] = e
                part = e[:, :128] + e[:, 128:]
                total = part if total is None else total + part
            inverse = 1.0 / jnp.sum(total, axis=1, keepdims=True)
            acc = None
            for kb in range(SPAN):
                at = pl.ds(pl.multiple_of((qb + kb) * ROWS, ROWS), ROWS)
                p = (sc[:, pl.ds(kb * ROWS, ROWS)] * inverse).astype(bf16)
                part = jnp.dot(p, vs[at, lanes], preferred_element_type=f32)
                acc = part if acc is None else acc + part
            outs.append(acc)
        both = jnp.where(lane < HEAD, outs[0], outs[1])

        @pl.when(qb == par)
        def _():
            mine[:, lanes] = both

        @pl.when(qb != par)
        def _():
            theirs[:, lanes] = both

        return carry

    lax.fori_loop(0, 8, pair, 0)


def out_kernel(mine, received, gain, w_here, w_there, out):
    par = lax.rem(lax.axis_index("seq"), 2)
    f = lax.axis_index("fsdp")
    a, b = mine[...], received[...]
    mean = (jnp.sum(a * a, axis=1, keepdims=True) + jnp.sum(b * b, axis=1, keepdims=True)) / D
    scale = lax.rsqrt(mean + EPSILON)
    at_a = pl.ds(pl.multiple_of(par * HALF, HALF), HALF)
    at_b = pl.ds(pl.multiple_of((1 - par) * HALF, HALF), HALF)
    na = (a * scale * gain[:, at_a]).astype(bf16)
    nb = (b * scale * gain[:, at_b]).astype(bf16)
    for w, side in ((w_here, f), (w_there, 1 - f)):
        y = jnp.dot(na, w[at_a, :], preferred_element_type=f32) + jnp.dot(nb, w[at_b, :], preferred_element_type=f32)
        out[:, pl.ds(pl.multiple_of(side * HALF, HALF), HALF)] = y.astype(bf16)


def local(dna_embed, site_owner, site_row, variant_table, norm_gain, conv_weight, qkv_weight, out_weight, attn_gain):
    count = lax.axis_size("seq")
    par = lax.rem(lax.axis_index("seq"), 2)
    f = lax.axis_index("fsdp")
    across = [(0, 1), (1, 0)]
    swap = [(i, i ^ 1) for i in range(count)]
    ahead = [(i, i + 2) for i in range(count - 2)]

    main = lax.dynamic_slice_in_dim(qkv_weight, HALF * (par + f), HALF, 1)
    aux = lax.dynamic_slice_in_dim(qkv_weight, D * (1 - f) + 256 * par, 256, 1)
    main_in = lax.ppermute(main, "fsdp", across)
    aux_in = lax.ppermute(aux, "fsdp", across)
    aux_pair = lax.ppermute(aux_in, "seq", swap)
    out_half = lax.dynamic_slice_in_dim(out_weight, HALF * par, HALF, 0)
    out_in = lax.ppermute(out_half, "fsdp", across)
    out_pair = lax.ppermute(out_in, "seq", swap)

    table, slot = pl.pallas_call(
        request_kernel,
        out_shape=(jax.ShapeDtypeStruct((OWNERS, 128), jnp.int32), jax.ShapeDtypeStruct((1, ROWS), jnp.int32)),
        in_specs=[vmem()] * 3,
        out_specs=(vmem(), vmem()),
        name="requests",
    )(site_owner[0], site_owner.reshape(1, ROWS), site_row)
    wanted = lax.all_to_all(table, "seq", split_axis=0, concat_axis=0, tiled=True)
    found = variant_table[wanted[:, :SLOTS].reshape(OWNERS * SLOTS)]
    fetched = lax.all_to_all(found, "seq", split_axis=0, concat_axis=0, tiled=True)
    normed = pl.pallas_call(
        norm_kernel,
        out_shape=jax.ShapeDtypeStruct((ROWS, D), bf16),
        in_specs=[vmem()] * 4,
        out_specs=vmem(),
        name="norm",
    )(fetched, slot, dna_embed[0], norm_gain.reshape(1, D))
    rim = lax.ppermute(normed[ROWS - 6 :], "seq", [(i, i + 1) for i in range(count - 1)])
    x = pl.pallas_call(
        conv_kernel,
        out_shape=jax.ShapeDtypeStruct((ROWS, D), bf16),
        in_specs=[vmem()] * 3,
        out_specs=vmem(),
        scratch_shapes=[pltpu.VMEM((ROWS + 8, D), f32)],
        name="conv",
    )(normed, rim, conv_weight)
    own = [x]
    for _ in range(HOPS):
        own.append(lax.ppermute(own[-1], "seq", ahead))
    other = [lax.ppermute(value, "seq", swap) for value in own]

    first = f == 0
    wq = jnp.where(first, main, main_in)
    wv = jnp.where(first, main_in, main)
    k_here = lax.dynamic_slice_in_dim(qkv_weight, D * (1 - f), HALF, 1)
    lower = jnp.where(par == 0, aux_in, aux_pair)
    upper = jnp.where(par == 0, aux_pair, aux_in)
    wk = jnp.where(par == f, k_here, jnp.concatenate([lower, upper], axis=1))
    mine, theirs = pl.pallas_call(
        attend_kernel,
        out_shape=(jax.ShapeDtypeStruct((ROWS, HALF), f32), jax.ShapeDtypeStruct((ROWS, HALF), f32)),
        in_specs=[anywhere()] * BLOCKS + [vmem()] * 3,
        out_specs=(vmem(), vmem()),
        scratch_shapes=[
            pltpu.VMEM((BLOCKS * ROWS, D), bf16),
            pltpu.VMEM((2 * ROWS, HALF), bf16),
            pltpu.VMEM((BLOCKS * ROWS, HALF), bf16),
            pltpu.VMEM((BLOCKS * ROWS, HALF), bf16),
            pltpu.VMEM((2, ROWS, SPAN * ROWS), f32),
            pltpu.VMEM((ROWS, SPAN * ROWS), f32),
            pltpu.VMEM((ROWS, SPAN * ROWS), f32),
            pltpu.SemaphoreType.DMA((BLOCKS,)),
        ],
        compiler_params=pltpu.CompilerParams(vmem_limit_bytes=48 * 2**20),
        cost_estimate=cost(12 * 10**9, 10 * 2**20),
        name="attend",
    )(*own, *other, wq, wk, wv)
    received = lax.ppermute(theirs, "seq", swap)
    w_there = jnp.concatenate(
        [jnp.where(par == 0, out_in, out_pair), jnp.where(par == 0, out_pair, out_in)], axis=0
    )
    mixed = pl.pallas_call(
        out_kernel,
        out_shape=jax.ShapeDtypeStruct((ROWS, D), bf16),
        in_specs=[vmem()] * 5,
        out_specs=vmem(),
        name="project",
    )(mine, received, attn_gain.reshape(1, D), out_weight, w_there)
    return mixed[None]


def solution(mesh):
    in_specs = (
        P("fsdp", "seq", None),
        P("fsdp", "seq", None),
        P("fsdp", "seq"),
        P("seq", None),
        P(),
        P(),
        P(None, "fsdp"),
        P(None, "fsdp"),
        P(),
    )
    return jax.shard_map(local, mesh=mesh, in_specs=in_specs, out_specs=P("fsdp", "seq", None), check_vma=False)
```

time: 543 us -> 221 us (0.41); the launches traced: 536 us -> 220 us
  waiting for transfers between devices: 280 us -> 95.2 us
  starting transfers between devices: 114 us -> 33.5 us
  Pallas kernels: 0 us -> 44.8 us
  local copies, waits for them, and re-layouts: 56.4 us -> 12.8 us
  matrix products: 36.3 us -> 0 us
  between operations: 13.7 us -> 0.24 us
    ppermute x9 -> x16, waiting for transfers between devices: 227 us -> 66.9 us  [the longest x1 41.3 us: local(): out_in = lax.ppermute(out_half, 'fsdp', across)]
    ppermute x9 -> x16, starting transfers between devices: 106 us -> 25.6 us  [the longest x4 16 us: local(): own.append(lax.ppermute(own[-1], 'seq', ahead))]
    pallas_call x0 -> x5, Pallas kernels: none -> 44.8 us  [the longest x1 33.2 us: local(): pl.pallas_call(attend_kernel, out_shape=(jax.ShapeDtypeStruct((ROWS, HALF...]
    unnamed x18 -> x14, local copies, waits for them, and re-layouts: 27 us -> 1.61 us
    dot_general x6 -> x0, matrix products: 22.3 us -> none  [the longest x4 13.9 us: head_group(): jnp.einsum('hqk,khd->qhd', probs, v_group, preferred_element_type=jnp.flo...]
    all_gather x2 -> x0, waiting for transfers between devices: 22.2 us -> none  [the longest x1 22.2 us: local(): lax.all_gather(qkv_weight, 'fsdp', axis=1, tiled=True)]
    sub x4 -> x0, matrix products: 14 us -> none  [head_group(): expo = jnp.exp(scores - highest)]
    dynamic_slice x16 -> x2, local copies, waits for them, and re-layouts: 13.7 us -> 1.12 us  [the longest x1 1.08 us: local(): aux = lax.dynamic_slice_in_dim(qkv_weight, D * (1 - f) + 256 * par, 256, 1)]
  transfers between devices with their start and end apart: 12 -> 17, of which waited for: 10 -> 7; matrix products, arithmetic and copies ran while one was open for 17% -> 4% of each run, Pallas kernels for 0% -> 18%
where the time goes in v1:
time: 221 us; the launch traced here: 220 us
  waiting for transfers between devices  95.2 us (43%)
  Pallas kernels  44.8 us (20%)
  starting transfers between devices  33.5 us (15%)
  blocking collectives  25.8 us (12%)
  local copies, waits for them, and re-layouts  12.8 us (6%)
  other arithmetic  7.62 us (3%)
    ppermute x1, waiting for transfers between devices, local(): out_in = lax.ppermute(out_half, 'fsdp', across)  41.3 us
    pallas_call x1, Pallas kernels, local(): pl.pallas_call(attend_kernel, out_shape=(jax.ShapeDtypeStruct((ROWS, HALF...  33.2 us
    all_to_all x1, waiting for transfers between devices, local(): lax.all_to_all(found, 'seq', split_axis=0, concat_axis=0, tiled=True)  28.3 us
    all_to_all x1, blocking collectives, local(): lax.all_to_all(table, 'seq', split_axis=0, concat_axis=0, tiled=True)  25.8 us
    ppermute x4, waiting for transfers between devices, local(): own.append(lax.ppermute(own[-1], 'seq', ahead))  24.2 us
    ppermute x4, starting transfers between devices, local(): own.append(lax.ppermute(own[-1], 'seq', ahead))  16 us
    all_to_all x1, starting transfers between devices, local(): lax.all_to_all(found, 'seq', split_axis=0, concat_axis=0, tiled=True)  7.88 us
    gather x1, local copies, waits for them, and re-layouts, local(): found = variant_table[wanted[:, :SLOTS].reshape(OWNERS * SLOTS)]  5.46 us
  transfers between devices with their start and end apart: 17, of which 7 were waited for; matrix products, arithmetic and copies ran while one was open for 4% of the time, Pallas kernels for 18%

profile of v1, /device:TPU:25, one launch (start us, length us, event | category | flops | bytes accessed | tf_op | source)
XLA Modules:
  0.0 219.9 jit_solution(797278063181471026)
XLA Ops:
  0.0 1.5 copy.11.owner_col
  1.5 1.9 requests.1
  3.4 25.8 %all_to_all.23 = s32[128,1,128]{2,1,0:T(1,128)S(1)} all-to-all(s32[128,1,128]{2,1,0:T(1,128)} %bitcast.14), channel_id=1, replica_groups=mesh['seq'=128,'fsdp'=2] {'seq'}, dimensions={0} | all-to-all | bytes 131072 | tf_op jit(solution)/shard_map/all_to_all | solution.py:201
  29.1 0.1 reshape.45
  29.3 5.5 %gather_fusion = bf16[512,1024]{1,0:T(8,128)(2,1)S(1)} fusion(bf16[2048,1024]{1,0:T(8,128)(2,1)} %param.12, s32[1024]{0:T(1024)S(1)} %pad_clamp_fusion), kind=kCustom, calls=%fused_computation | custom fusion | bytes 2099200 | tf_op jit(solution)/shard_map/gather | solution.py:202
  34.7 1.2 all_to_all.18
  36.0 7.9 %all-to-all-start.1 = ((bf16[128,4,1024]{2,1,0:T(4,128)(2,1)}), bf16[128,4,1024]{2,1,0:T(4,128)(2,1)S(1)}, u32[]{:S(2)}, u32[]{:S(2)}) async-start(bf16[128,4,1024]{2,1,0:T(4,128)(2,1)} %all_to_all.18), calls=%async_computation.1 | async-start | bytes 2097152 | tf_op jit(solution)/shard_map/all_to_all | solution.py:203
  43.9 1.1 constant_dynamic-slice_fusion.1
  45.0 0.4 collective-permute-start.11
  45.4 28.3 %all-to-all-done.1 = bf16[128,4,1024]{2,1,0:T(4,128)(2,1)S(1)} async-done(((bf16[128,4,1024]{2,1,0:T(4,128)(2,1)}), bf16[128,4,1024]{2,1,0:T(4,128)(2,1)S(1)}, u32[]{:S(2)}, u32[]{:S(2)}) %all-to-all-start.1) | async-done | bytes 1048608 | tf_op jit(solution)/shard_map/all_to_all | solution.py:203
  73.6 1.1 all_to_all.20.fetched
  74.7 2.8 %norm.1.normed = bf16[256,1024]{1,0:T(8,128)(2,1)} custom-call(bf16[512,1024]{1,0:T(8,128)(2,1)} %all_to_all.20.fetched, s32[1,256]{1,0:T(1,128)} %get-tuple-element.10.slot, bf16[256,1024]{1,0:T(8,128)(2,1)} %bitcast.12, f32[1,1024]{1,0:T(1,128)} %bitcast.16), custom_call_target="tpu_custom_call" | custom-call | tf_op jit(solution)/shard_map/norm/pallas_call | solution.py:204
  77.5 0.7 slice.11
  78.2 2.0 collective-permute-start
  80.2 1.1 collective-permute-done.rim
  81.3 0.6 copy-done.6
  81.9 3.5 %conv.1.refs_0_ = bf16[256,1024]{1,0:T(8,128)(2,1)} custom-call(bf16[256,1024]{1,0:T(8,128)(2,1)} %norm.1.normed, bf16[6,1024]{1,0:T(8,128)(2,1)} %copy-done.6, bf16[7,1024]{1,0:T(8,128)(2,1)} %taps.1), custom_call_target="tpu_custom_call" | custom-call | tf_op jit(solution)/shard_map/conv/pallas_call | solution.py:212
  85.4 3.8 %collective-permute-start.1 = (bf16[256,1024]{1,0:T(8,128)(2,1)}, bf16[256,1024]{1,0:T(8,128)(2,1)S(1)}, u32[]{:S(2)}, u32[]{:S(2)}) collective-permute-start(bf16[256,1024]{1,0:T(8,128)(2,1)} %conv.1.refs_0_), channel_id=1, source_target_pairs={{0,4},{2,6},{4,8},{6,10},{8,12},{10,14},{12,16},{14,18},{16,20},{1... | collective-permute-start | bytes 1572872 | tf_op jit(solution)/shard_map/ppermute | solution.py:222
  89.2 1.2 collective-permute-start.12
  90.3 9.7 %collective-permute-done.1.refs_1_ = bf16[256,1024]{1,0:T(8,128)(2,1)S(1)} collective-permute-done((bf16[256,1024]{1,0:T(8,128)(2,1)}, bf16[256,1024]{1,0:T(8,128)(2,1)S(1)}, u32[]{:S(2)}, u32[]{:S(2)}) %collective-permute-start.1) | collective-permute-done | bytes 524320 | tf_op jit(solution)/shard_map/ppermute | solution.py:222
  100.1 3.8 %collective-permute-start.2 = (bf16[256,1024]{1,0:T(8,128)(2,1)S(1)}, bf16[256,1024]{1,0:T(8,128)(2,1)S(1)}, u32[]{:S(2)}, u32[]{:S(2)}) collective-permute-start(bf16[256,1024]{1,0:T(8,128)(2,1)S(1)} %collective-permute-done.1.refs_1_), channel_id=1, source_target_pairs={{0,4},{2,6},{4,8},{6,10},{8,12},{10,14},{12,16},{14,18},{16,20},{1... | collective-permute-start | bytes 1572872 | tf_op jit(solution)/shard_map/ppermute | solution.py:222
  103.9 0.0 collective-permute-done.12
  104.0 0.1 broadcast_select_fusion.5
  104.0 0.0 copy-start.2
  104.1 3.3 %maximum_select_fusion = (bf16[1024,512]{1,0:T(8,128)(2,1)}, bf16[1024,512]{1,0:T(8,128)(2,1)}) fusion(bf16[1024,256]{1,0:T(8,128)(2,1)S(1)} %get-tuple-element.20, bf16[1024,256]{1,0:T(8,128)(2,1)S(1)} %get-tuple-element.19, bf16[1024,1536]{1,0:T(8,128)(2,1)} %param.15, s32[]{:T(128)S(6)} %select_n.69, pred[]{:T(512)S(6)} %eq.13, s32[]{:T(128)S(6)} %select_n.66), kind=kLoop, calls=%fused_computation.1 | loop fusion | flops 2621440 | bytes 5242889 | tf_op jit(solution)/shard_map/jit(_where)/select_n | solution.py:231
  107.4 0.3 collective-permute-start.10
  107.7 6.1 %collective-permute-done.2.refs_2_ = bf16[256,1024]{1,0:T(8,128)(2,1)S(1)} collective-permute-done((bf16[256,1024]{1,0:T(8,128)(2,1)S(1)}, bf16[256,1024]{1,0:T(8,128)(2,1)S(1)}, u32[]{:S(2)}, u32[]{:S(2)}) %collective-permute-start.2) | collective-permute-done | bytes 524320 | tf_op jit(solution)/shard_map/ppermute | solution.py:222
  113.7 4.0 %collective-permute-start.3 = (bf16[256,1024]{1,0:T(8,128)(2,1)S(1)}, bf16[256,1024]{1,0:T(8,128)(2,1)S(1)}, u32[]{:S(2)}, u32[]{:S(2)}) collective-permute-start(bf16[256,1024]{1,0:T(8,128)(2,1)S(1)} %collective-permute-done.2.refs_2_), channel_id=1, source_target_pairs={{0,4},{2,6},{4,8},{6,10},{8,12},{10,14},{12,16},{14,18},{16,20},{1... | collective-permute-start | bytes 1572872 | tf_op jit(solution)/shard_map/ppermute | solution.py:222
  117.8 0.4 collective-permute-start.14
  118.2 8.4 %collective-permute-done.3.refs_3_ = bf16[256,1024]{1,0:T(8,128)(2,1)S(1)} collective-permute-done((bf16[256,1024]{1,0:T(8,128)(2,1)S(1)}, bf16[256,1024]{1,0:T(8,128)(2,1)S(1)}, u32[]{:S(2)}, u32[]{:S(2)}) %collective-permute-start.3) | collective-permute-done | bytes 524320 | tf_op jit(solution)/shard_map/ppermute | solution.py:222
  126.6 4.4 %collective-permute-start.4 = (bf16[256,1024]{1,0:T(8,128)(2,1)S(1)}, bf16[256,1024]{1,0:T(8,128)(2,1)S(1)}, u32[]{:S(2)}, u32[]{:S(2)}) collective-permute-start(bf16[256,1024]{1,0:T(8,128)(2,1)S(1)} %collective-permute-done.3.refs_3_), channel_id=1, source_target_pairs={{0,4},{2,6},{4,8},{6,10},{8,12},{10,14},{12,16},{14,18},{16,20},{1... | collective-permute-start | bytes 1572872 | tf_op jit(solution)/shard_map/ppermute | solution.py:222
  131.0 3.5 %collective-permute-start.5 = (bf16[256,1024]{1,0:T(8,128)(2,1)S(1)}, bf16[256,1024]{1,0:T(8,128)(2,1)S(1)}, u32[]{:S(2)}, u32[]{:S(2)}) collective-permute-start(bf16[256,1024]{1,0:T(8,128)(2,1)S(1)} %copy-done), channel_id=1, source_target_pairs={{0,2},{2,0},{4,6},{6,4},{8,10},{10,8},{12,14},{14,12},{16,18},{18,... | collective-permute-start | bytes 1572872 | tf_op jit(solution)/shard_map/ppermute | solution.py:223
  134.5 0.1 collective-permute-start.6
  134.6 41.3 %collective-permute-done.14 = bf16[512,512]{1,0:T(8,128)(2,1)S(1)} collective-permute-done((bf16[512,512]{1,0:T(8,128)(2,1)S(1)}, bf16[512,512]{1,0:T(8,128)(2,1)S(1)}, u32[]{:S(2)}, u32[]{:S(2)}) %collective-permute-start.14) | collective-permute-done | bytes 524320 | tf_op jit(solution)/shard_map/ppermute | solution.py:191
  175.9 0.5 collective-permute-start.7
  176.4 0.1 collective-permute-start.8
  176.5 0.0 collective-permute-done.4.refs_4_
  176.5 0.2 copy-done.3
  176.7 0.5 collective-permute-start.9
  177.2 3.1 %broadcast_select_fusion = (bf16[1024,512]{1,0:T(8,128)(2,1)}, bf16[1024,512]{1,0:T(8,128)(2,1)}) fusion(bf16[1024,512]{1,0:T(8,128)(2,1)} %collective-permute-done.10, bf16[1024,512]{1,0:T(8,128)(2,1)} %get-tuple-element.14, pred[]{:T(512)S(6)} %eq.12), kind=kLoop, calls=%fused_computation.3 | loop fusion | flops 1048576 | bytes 4194305 | tf_op jit(solution)/shard_map/jit(_where)/select_n | solution.py:227
  180.3 0.0 collective-permute-start.15
  180.3 33.2 %attend.1 = (f32[256,512]{1,0:T(8,128)S(1)}, f32[256,512]{1,0:T(8,128)S(1)}) custom-call(bf16[256,1024]{1,0:T(8,128)(2,1)S(1)} %copy-done, bf16[256,1024]{1,0:T(8,128)(2,1)S(1)} %collective-permute-done.1.refs_1_, bf16[256,1024]{1,0:T(8,128)(2,1)S(1)} %collective-permute-done.2.refs_2_, bf16[256,1024]{1,0:T(8,128)(2,1)S(1)} %collective-permute-done.3.refs_3_, ...), custom_call_target="tpu_custom_call" | custom-call | flops 12000000000 | bytes 10485760 | tf_op jit(solution)/shard_map/attend/pallas_call | solution.py:232
  213.5 0.6 collective-permute-start.13
  214.1 0.1 broadcast_select_fusion.3
  214.2 1.1 pad_maximum_fusion.w_there
  215.2 0.4 collective-permute-done.13.received
  215.6 0.8 copy-done.5
  216.4 3.5 %project.1 = bf16[256,1024]{1,0:T(8,128)(2,1)} custom-call(f32[256,512]{1,0:T(8,128)} %copy-done.1, f32[256,512]{1,0:T(8,128)} %copy-done.5, f32[1,1024]{1,0:T(1,128)} %bitcast.19, bf16[1024,512]{1,0:T(8,128)(2,1)} %w_here.1, bf16[1024,512]{1,0:T(8,128)(2,1)} %pad_maximum_fusion.w_there), custom_call_target="tpu_custom_call" | custom-call | tf_op jit(solution)/shard_map/project/pallas_call | solution.py:255
  (21 shorter events, 0.1 us)
Async XLA Ops:
  36.0 37.7 %all-to-all-start.1 = ((bf16[128,4,1024]{2,1,0:T(4,128)(2,1)}), bf16[128,4,1024]{2,1,0:T(4,128)(2,1)S(1)}, u32[]{:S(2)}, u32[]{:S(2)}) async-start(bf16[128,4,1024]{2,1,0:T(4,128)(2,1)} %all_to_all.18), calls=%async_computation.1 | async-start | bytes 2097152 | tf_op jit(solution)/shard_map/all_to_all | solution.py:203
  45.0 44.2 %collective-permute-start.11 = (bf16[1024,256]{1,0:T(8,128)(2,1)S(1)}, bf16[1024,256]{1,0:T(8,128)(2,1)S(1)}, u32[]{:S(2)}, u32[]{:S(2)}) collective-permute-start(bf16[1024,256]{1,0:T(8,128)(2,1)S(1)} %constant_dynamic-slice_fusion.1), channel_id=1, source_target_pairs={{0,1},{1,0},{2,3},{3,2},{4,5},{5,4},{6,7},{7,6},{8,9},{9,8},{10,11... | collective-permute-start | bytes 1572872 | tf_op jit(solution)/shard_map/ppermute | solution.py:188
  78.2 3.1 %collective-permute-start = (bf16[6,1024]{1,0:T(8,128)(2,1)S(1)}, bf16[6,1024]{1,0:T(8,128)(2,1)S(1)}, u32[]{:S(2)}, u32[]{:S(2)}) collective-permute-start(bf16[6,1024]{1,0:T(8,128)(2,1)S(1)} %slice.11), channel_id=1, source_target_pairs={{0,2},{2,4},{4,6},{6,8},{8,10},{10,12},{12,14},{14,16},{16,18},{18... | collective-permute-start | bytes 36872 | tf_op jit(solution)/shard_map/ppermute | solution.py:211
  81.3 0.6 copy-start.6
  85.4 14.7 %collective-permute-start.1 = (bf16[256,1024]{1,0:T(8,128)(2,1)}, bf16[256,1024]{1,0:T(8,128)(2,1)S(1)}, u32[]{:S(2)}, u32[]{:S(2)}) collective-permute-start(bf16[256,1024]{1,0:T(8,128)(2,1)} %conv.1.refs_0_), channel_id=1, source_target_pairs={{0,4},{2,6},{4,8},{6,10},{8,12},{10,14},{12,16},{14,18},{16,20},{1... | collective-permute-start | bytes 1572872 | tf_op jit(solution)/shard_map/ppermute | solution.py:222
  89.2 14.8 %collective-permute-start.12 = (bf16[1024,256]{1,0:T(8,128)(2,1)S(1)}, bf16[1024,256]{1,0:T(8,128)(2,1)S(1)}, u32[]{:S(2)}, u32[]{:S(2)}) collective-permute-start(bf16[1024,256]{1,0:T(8,128)(2,1)S(1)} %collective-permute-done.11), channel_id=1, source_target_pairs={{0,2},{2,0},{4,6},{6,4},{8,10},{10,8},{12,14},{14,12},{16,18},{18,... | collective-permute-start | bytes 1572872 | tf_op jit(solution)/shard_map/ppermute | solution.py:189
  100.1 13.7 %collective-permute-start.2 = (bf16[256,1024]{1,0:T(8,128)(2,1)S(1)}, bf16[256,1024]{1,0:T(8,128)(2,1)S(1)}, u32[]{:S(2)}, u32[]{:S(2)}) collective-permute-start(bf16[256,1024]{1,0:T(8,128)(2,1)S(1)} %collective-permute-done.1.refs_1_), channel_id=1, source_target_pairs={{0,4},{2,6},{4,8},{6,10},{8,12},{10,14},{12,16},{14,18},{16,20},{1... | collective-permute-start | bytes 1572872 | tf_op jit(solution)/shard_map/ppermute | solution.py:222
  104.0 13.7 %copy-start.2 = (bf16[1024,512]{1,0:T(8,128)(2,1)S(1)}, bf16[1024,512]{1,0:T(8,128)(2,1)}, u32[]{:S(2)}) copy-start(bf16[1024,512]{1,0:T(8,128)(2,1)} %w_here.1) | copy-start | bytes 3145732
  104.0 26.9 %copy-start = (bf16[256,1024]{1,0:T(8,128)(2,1)S(1)}, bf16[256,1024]{1,0:T(8,128)(2,1)}, u32[]{:S(2)}) copy-start(bf16[256,1024]{1,0:T(8,128)(2,1)} %conv.1.refs_0_) | copy-start | bytes 1572868
  107.4 69.0 %collective-permute-start.10 = (bf16[1024,512]{1,0:T(8,128)(2,1)}, bf16[1024,512]{1,0:T(8,128)(2,1)}, u32[]{:S(2)}, u32[]{:S(2)}) collective-permute-start(bf16[1024,512]{1,0:T(8,128)(2,1)} %get-tuple-element.14), channel_id=1, source_target_pairs={{0,1},{1,0},{2,3},{3,2},{4,5},{5,4},{6,7},{7,6},{8,9},{9,8},{10,11... | collective-permute-start | bytes 3145736 | tf_op jit(solution)/shard_map/ppermute | solution.py:187
  113.7 12.8 %collective-permute-start.3 = (bf16[256,1024]{1,0:T(8,128)(2,1)S(1)}, bf16[256,1024]{1,0:T(8,128)(2,1)S(1)}, u32[]{:S(2)}, u32[]{:S(2)}) collective-permute-start(bf16[256,1024]{1,0:T(8,128)(2,1)S(1)} %collective-permute-done.2.refs_2_), channel_id=1, source_target_pairs={{0,4},{2,6},{4,8},{6,10},{8,12},{10,14},{12,16},{14,18},{16,20},{1... | collective-permute-start | bytes 1572872 | tf_op jit(solution)/shard_map/ppermute | solution.py:222
  117.8 58.1 %collective-permute-start.14 = (bf16[512,512]{1,0:T(8,128)(2,1)S(1)}, bf16[512,512]{1,0:T(8,128)(2,1)S(1)}, u32[]{:S(2)}, u32[]{:S(2)}) collective-permute-start(bf16[512,512]{1,0:T(8,128)(2,1)S(1)} %constant_dynamic-slice_fusion), channel_id=1, source_target_pairs={{0,1},{1,0},{2,3},{3,2},{4,5},{5,4},{6,7},{7,6},{8,9},{9,8},{10,11... | collective-permute-start | bytes 1572872 | tf_op jit(solution)/shard_map/ppermute | solution.py:191
  126.6 49.9 %collective-permute-start.4 = (bf16[256,1024]{1,0:T(8,128)(2,1)S(1)}, bf16[256,1024]{1,0:T(8,128)(2,1)S(1)}, u32[]{:S(2)}, u32[]{:S(2)}) collective-permute-start(bf16[256,1024]{1,0:T(8,128)(2,1)S(1)} %collective-permute-done.3.refs_3_), channel_id=1, source_target_pairs={{0,4},{2,6},{4,8},{6,10},{8,12},{10,14},{12,16},{14,18},{16,20},{1... | collective-permute-start | bytes 1572872 | tf_op jit(solution)/shard_map/ppermute | solution.py:222
  131.0 49.3 %collective-permute-start.5 = (bf16[256,1024]{1,0:T(8,128)(2,1)S(1)}, bf16[256,1024]{1,0:T(8,128)(2,1)S(1)}, u32[]{:S(2)}, u32[]{:S(2)}) collective-permute-start(bf16[256,1024]{1,0:T(8,128)(2,1)S(1)} %copy-done), channel_id=1, source_target_pairs={{0,2},{2,0},{4,6},{6,4},{8,10},{10,8},{12,14},{14,12},{16,18},{18,... | collective-permute-start | bytes 1572872 | tf_op jit(solution)/shard_map/ppermute | solution.py:223
  134.5 45.8 %collective-permute-start.6 = (bf16[256,1024]{1,0:T(8,128)(2,1)S(1)}, bf16[256,1024]{1,0:T(8,128)(2,1)}, u32[]{:S(2)}, u32[]{:S(2)}) collective-permute-start(bf16[256,1024]{1,0:T(8,128)(2,1)S(1)} %collective-permute-done.1.refs_1_), channel_id=1, source_target_pairs={{0,2},{2,0},{4,6},{6,4},{8,10},{10,8},{12,14},{14,12},{16,18},{18,... | collective-permute-start | bytes 1572872 | tf_op jit(solution)/shard_map/ppermute | solution.py:223
  175.9 0.8 copy-start.3
  175.9 4.4 %collective-permute-start.7 = (bf16[256,1024]{1,0:T(8,128)(2,1)S(1)}, bf16[256,1024]{1,0:T(8,128)(2,1)}, u32[]{:S(2)}, u32[]{:S(2)}) collective-permute-start(bf16[256,1024]{1,0:T(8,128)(2,1)S(1)} %collective-permute-done.2.refs_2_), channel_id=1, source_target_pairs={{0,2},{2,0},{4,6},{6,4},{8,10},{10,8},{12,14},{14,12},{16,18},{18,... | collective-permute-start | bytes 1572872 | tf_op jit(solution)/shard_map/ppermute | solution.py:223
  176.4 3.9 %collective-permute-start.8 = (bf16[256,1024]{1,0:T(8,128)(2,1)S(1)}, bf16[256,1024]{1,0:T(8,128)(2,1)}, u32[]{:S(2)}, u32[]{:S(2)}) collective-permute-start(bf16[256,1024]{1,0:T(8,128)(2,1)S(1)} %collective-permute-done.3.refs_3_), channel_id=1, source_target_pairs={{0,2},{2,0},{4,6},{6,4},{8,10},{10,8},{12,14},{14,12},{16,18},{18,... | collective-permute-start | bytes 1572872 | tf_op jit(solution)/shard_map/ppermute | solution.py:223
  176.7 3.6 %collective-permute-start.9 = (bf16[256,1024]{1,0:T(8,128)(2,1)S(1)}, bf16[256,1024]{1,0:T(8,128)(2,1)}, u32[]{:S(2)}, u32[]{:S(2)}) collective-permute-start(bf16[256,1024]{1,0:T(8,128)(2,1)S(1)} %collective-permute-done.4.refs_4_), channel_id=1, source_target_pairs={{0,2},{2,0},{4,6},{6,4},{8,10},{10,8},{12,14},{14,12},{16,18},{18,... | collective-permute-start | bytes 1572872 | tf_op jit(solution)/shard_map/ppermute | solution.py:223
  177.2 3.1 %copy-start.4 = (bf16[512,512]{1,0:T(8,128)(2,1)S(1)}, bf16[512,512]{1,0:T(8,128)(2,1)}, u32[]{:S(2)}) copy-start(bf16[512,512]{1,0:T(8,128)(2,1)} %copy-done.3) | copy-start | bytes 1572868
  180.3 33.8 %collective-permute-start.15 = (bf16[512,512]{1,0:T(8,128)(2,1)S(1)}, bf16[512,512]{1,0:T(8,128)(2,1)S(1)}, u32[]{:S(2)}, u32[]{:S(2)}) collective-permute-start(bf16[512,512]{1,0:T(8,128)(2,1)S(1)} %copy-done.4), channel_id=1, source_target_pairs={{0,2},{2,0},{4,6},{6,4},{8,10},{10,8},{12,14},{14,12},{16,18},{18,... | collective-permute-start | bytes 1572872 | tf_op jit(solution)/shard_map/ppermute | solution.py:192
  213.5 1.7 copy-start.1
  213.5 2.1 collective-permute-start.13
  215.6 0.8 copy-start.5

commit v2 on v1

v2 whole, which is shorter than its diff:
```python
import jax
import jax.numpy as jnp
from jax import lax
from jax.experimental import pallas as pl
from jax.experimental.pallas import tpu as pltpu
from jax.sharding import PartitionSpec as P

HEAD = 64
WINDOW = 2048
EPSILON = 1e-05
ROWS = 256
D = 1024
HALF = 512
OWNERS = 128
SLOTS = 4
HOPS = 4
SPAN = WINDOW // ROWS + 1
LOG2E = 1.4426950408889634

bf16 = jnp.bfloat16
f32 = jnp.float32


def vmem():
    return pl.BlockSpec(memory_space=pltpu.VMEM)


def anywhere():
    return pl.BlockSpec(memory_space=pltpu.HBM)


def limit(mib):
    return pltpu.CompilerParams(vmem_limit_bytes=mib * 2**20)


def cost(flops, moved):
    return pl.CostEstimate(flops=flops, bytes_accessed=moved, transcendentals=0)


def slab_kernel(qkv, out, main, aux, half, sems):
    par = lax.rem(lax.axis_index("seq"), 2)
    f = lax.axis_index("fsdp")
    copies = (
        pltpu.make_async_copy(qkv.at[:, pl.ds(pl.multiple_of(HALF * (par + f), HALF), HALF)], main, sems.at[0]),
        pltpu.make_async_copy(qkv.at[:, pl.ds(pl.multiple_of(D * (1 - f) + 256 * par, 256), 256)], aux, sems.at[1]),
        pltpu.make_async_copy(out.at[pl.ds(pl.multiple_of(HALF * par, HALF), HALF), :], half, sems.at[2]),
    )
    for copy in copies:
        copy.start()
    for copy in copies:
        copy.wait()


def weight_kernel(qkv, main, main_in, aux_in, aux_pair, wq, wk, wv, sem):
    par = lax.rem(lax.axis_index("seq"), 2)
    f = lax.axis_index("fsdp")

    @pl.when(par == f)
    def _():
        copy = pltpu.make_async_copy(qkv.at[:, pl.ds(pl.multiple_of(D * (1 - f), D), HALF)], wk, sem)
        copy.start()
        copy.wait()

    @pl.when(par != f)
    def _():
        wk[:, pl.ds(pl.multiple_of(par * 256, 256), 256)] = aux_in[...]
        wk[:, pl.ds(pl.multiple_of((1 - par) * 256, 256), 256)] = aux_pair[...]

    @pl.when(f == 0)
    def _():
        wq[...] = main[...]
        wv[...] = main_in[...]

    @pl.when(f == 1)
    def _():
        wq[...] = main_in[...]
        wv[...] = main[...]


def request_kernel(owner, rows, table, slot):
    orow = owner[...]
    above = lax.broadcasted_iota(jnp.int32, (ROWS, ROWS), 0)
    along = lax.broadcasted_iota(jnp.int32, (ROWS, ROWS), 1)
    ocol = jnp.sum(jnp.where(above == along, orow, 0), axis=1, keepdims=True)
    same = ocol == orow
    rank = jnp.sum(jnp.where(same & (above < along), 1, 0), axis=0, keepdims=True)
    rank_col = jnp.sum(jnp.where(same & (along < above), 1, 0), axis=1, keepdims=True)
    mine = lax.broadcasted_iota(jnp.int32, (OWNERS, ROWS), 0) == orow
    lane = lax.broadcasted_iota(jnp.int32, (OWNERS, 128), 1)
    out = jnp.zeros((OWNERS, 128), jnp.int32)
    for k in range(SLOTS):
        column = jnp.sum(jnp.where(mine & (rank == k), rows[...], 0), axis=1, keepdims=True)
        out = jnp.where(lane == k, column, out)
    table[...] = out
    slot[...] = ocol * SLOTS + rank_col


def norm_kernel(fetched, slot, dna, gain, normed, rim):
    pick = (lax.broadcasted_iota(jnp.int32, (ROWS, OWNERS * SLOTS), 1) == slot[...]).astype(f32).astype(bf16)
    site = jnp.dot(pick, fetched[...], preferred_element_type=f32)
    resid = dna[...].astype(f32) + site
    mean = jnp.mean(resid * resid, axis=1, keepdims=True)
    out = (resid * lax.rsqrt(mean + EPSILON) * gain[...]).astype(bf16)
    normed[...] = out
    rim[...] = out[ROWS - 8 :]


def conv_kernel(normed, rim, taps, out, padded):
    padded[pl.ds(0, 8), :] = rim[...].astype(f32)
    padded[pl.ds(8, ROWS), :] = normed[...].astype(f32)

    def column(c, carry):
        lanes = pl.ds(pl.multiple_of(c * 128, 128), 128)
        weight = taps[:, lanes].astype(f32)
        for part in range(2):
            total = jnp.zeros((128, 128), f32)
            for tap in range(7):
                total = total + weight[tap : tap + 1] * padded[pl.ds(part * 128 + 8 - tap, 128), lanes]
            out[pl.ds(part * 128, 128), lanes] = total.astype(bf16)
        return carry

    lax.fori_loop(0, D // 128, column, 0)


def kv_kernel(own, other, wk, wv, kv):
    par = lax.rem(lax.axis_index("seq"), 2)
    for x, side in ((own, par), (other, 1 - par)):
        at = pl.ds(pl.multiple_of(side * ROWS, ROWS), ROWS)
        kv[at, :HALF] = jnp.dot(x[...], wk[...], preferred_element_type=f32).astype(bf16)
        kv[at, HALF:] = jnp.dot(x[...], wv[...], preferred_element_type=f32).astype(bf16)


def q_kernel(own, other, wq, q):
    par = lax.rem(lax.axis_index("seq"), 2)
    for x, side in ((own, par), (other, 1 - par)):
        at = pl.ds(pl.multiple_of(side * ROWS, ROWS), ROWS)
        q[at, :] = jnp.dot(x[...], wq[...], preferred_element_type=f32).astype(bf16)


def attend_kernel(q_ref, kv0, kv1, kv2, kv3, kv4, mine, theirs, edge, bias, sc0, sc1, done):
    kv = (kv0, kv1, kv2, kv3, kv4)
    seq = lax.axis_index("seq")
    par = lax.rem(seq, 2)
    chip = seq // 2
    row = lax.broadcasted_iota(jnp.int32, (ROWS, ROWS), 0)
    col = lax.broadcasted_iota(jnp.int32, (ROWS, ROWS), 1)
    edge[0] = jnp.where(col > row, 0.0, -jnp.inf).astype(f32)
    edge[1] = jnp.where(col <= row, 0.0, -jnp.inf).astype(f32)
    block = lax.broadcasted_iota(jnp.int32, (16, ROWS), 0)
    bias[...] = jnp.where(block + 2 * (chip - HOPS) >= 0, 0.0, -jnp.inf).astype(f32)
    lane = lax.broadcasted_iota(jnp.int32, (ROWS, 128), 1)

    def place(h, b, value):
        lanes = pl.ds(pl.multiple_of(value * HALF + (h // 2) * 128, 128), 128)
        return kv[HOPS - b // 2][(b % 2) * ROWS : (b % 2 + 1) * ROWS, lanes]

    def scores(qb, h, sc):
        lanes = pl.ds(pl.multiple_of((h // 2) * 128, 128), 128)
        q = q_ref[qb * ROWS : (qb + 1) * ROWS, lanes]
        q = jnp.where((lane // HEAD) == lax.rem(h, 2), q, jnp.zeros_like(q))
        top = None
        for kb in range(SPAN):
            s = lax.dot_general(q, place(h, qb + kb, 0), (((1,), (1,)), ((), ())), preferred_element_type=f32)
            if kb < SPAN - 1:
                s = s + bias[qb + kb : qb + kb + 1, :]
            if kb == 0:
                s = s + edge[0]
            if kb == SPAN - 1:
                s = s + edge[1]
            sc[:, kb * ROWS : (kb + 1) * ROWS] = s
            part = jnp.maximum(s[:, :128], s[:, 128:])
            top = part if top is None else jnp.maximum(top, part)
        return jnp.max(top, axis=1, keepdims=True)

    def weigh(qb, h, sc, top):
        total = None
        for kb in range(SPAN):
            e = jnp.exp2((sc[:, kb * ROWS : (kb + 1) * ROWS] - top) * (LOG2E * HEAD ** (-0.5)))
            sc[:, kb * ROWS : (kb + 1) * ROWS] = e
            part = e[:, :128] + e[:, 128:]
            total = part if total is None else total + part
        inverse = 1.0 / jnp.sum(total, axis=1, keepdims=True)
        acc = None
        for kb in range(SPAN):
            p = (sc[:, kb * ROWS : (kb + 1) * ROWS] * inverse).astype(bf16)
            part = jnp.dot(p, place(h, qb + kb, 1), preferred_element_type=f32)
            acc = part if acc is None else acc + part
        lanes = pl.ds(pl.multiple_of((h // 2) * 128, 128), 128)
        old = done[qb, :, lanes]
        done[qb, :, lanes] = jnp.where((lane // HEAD) == lax.rem(h, 2), acc, old)

    def head(h, top0):
        top1 = scores(1, h, sc1)
        weigh(0, h, sc0, top0)
        after = scores(0, jnp.minimum(h + 1, 7), sc0)
        weigh(1, h, sc1, top1)
        return after

    lax.fori_loop(0, 8, head, scores(0, 0, sc0))
    mine[...] = done[par]
    theirs[...] = done[1 - par]


def out_kernel(mine, received, gain, w_here, w_mine, w_other, out):
    par = lax.rem(lax.axis_index("seq"), 2)
    f = lax.axis_index("fsdp")
    a, b = mine[...], received[...]
    mean = (jnp.sum(a * a, axis=1, keepdims=True) + jnp.sum(b * b, axis=1, keepdims=True)) / D
    scale = lax.rsqrt(mean + EPSILON)
    at_a = pl.ds(pl.multiple_of(par * HALF, HALF), HALF)
    at_b = pl.ds(pl.multiple_of((1 - par) * HALF, HALF), HALF)
    na = (a * scale * gain[:, at_a]).astype(bf16)
    nb = (b * scale * gain[:, at_b]).astype(bf16)
    here = jnp.dot(na, w_here[at_a, :], preferred_element_type=f32)
    here = here + jnp.dot(nb, w_here[at_b, :], preferred_element_type=f32)
    there = jnp.dot(na, w_mine[...], preferred_element_type=f32)
    there = there + jnp.dot(nb, w_other[...], preferred_element_type=f32)
    out[:, pl.ds(pl.multiple_of(f * HALF, HALF), HALF)] = here.astype(bf16)
    out[:, pl.ds(pl.multiple_of((1 - f) * HALF, HALF), HALF)] = there.astype(bf16)


def local(dna_embed, site_owner, site_row, variant_table, norm_gain, conv_weight, qkv_weight, out_weight, attn_gain):
    count = lax.axis_size("seq")
    across = [(0, 1), (1, 0)]
    swap = [(i, i ^ 1) for i in range(count)]
    ahead = [(i, i + 2) for i in range(count - 2)]

    main, aux, half = pl.pallas_call(
        slab_kernel,
        out_shape=(
            jax.ShapeDtypeStruct((D, HALF), bf16),
            jax.ShapeDtypeStruct((D, 256), bf16),
            jax.ShapeDtypeStruct((HALF, HALF), bf16),
        ),
        in_specs=[anywhere()] * 2,
        out_specs=(vmem(), vmem(), vmem()),
        scratch_shapes=[pltpu.SemaphoreType.DMA((3,))],
        compiler_params=limit(4),
        name="slabs",
    )(qkv_weight, out_weight)
    main_in = lax.ppermute(main, "fsdp", across)
    aux_in = lax.ppermute(aux, "fsdp", across)
    out_in = lax.ppermute(half, "fsdp", across)
    aux_pair = lax.ppermute(aux_in, "seq", swap)
    out_pair = lax.ppermute(out_in, "seq", swap)

    table, slot = pl.pallas_call(
        request_kernel,
        out_shape=(jax.ShapeDtypeStruct((OWNERS, 128), jnp.int32), jax.ShapeDtypeStruct((ROWS, 1), jnp.int32)),
        in_specs=[vmem()] * 2,
        out_specs=(vmem(), vmem()),
        compiler_params=limit(4),
        name="requests",
    )(site_owner.reshape(1, ROWS), site_row)
    wanted = lax.all_to_all(table, "seq", split_axis=0, concat_axis=0, tiled=True)
    found = variant_table[wanted[:, :SLOTS].reshape(OWNERS * SLOTS)]
    fetched = lax.all_to_all(found, "seq", split_axis=0, concat_axis=0, tiled=True)
    normed, edge = pl.pallas_call(
        norm_kernel,
        out_shape=(jax.ShapeDtypeStruct((ROWS, D), bf16), jax.ShapeDtypeStruct((8, D), bf16)),
        in_specs=[vmem()] * 4,
        out_specs=(vmem(), vmem()),
        compiler_params=limit(10),
    name="norm",
    )(fetched, slot, dna_embed[0], norm_gain.reshape(1, D))
    rim = lax.ppermute(edge, "seq", [(i, i + 1) for i in range(count - 1)])
    x = pl.pallas_call(
        conv_kernel,
        out_shape=jax.ShapeDtypeStruct((ROWS, D), bf16),
        in_specs=[vmem()] * 3,
        out_specs=vmem(),
        scratch_shapes=[pltpu.VMEM((ROWS + 8, D), f32)],
        compiler_params=limit(6),
        name="conv",
    )(normed, rim, conv_weight)
    own = [x]
    for _ in range(HOPS):
        own.append(lax.ppermute(own[-1], "seq", ahead))
    other = []
    for hop in range(HOPS + 1):
        other.append(lax.ppermute(own[hop], "seq", swap))

    wq, wk, wv = pl.pallas_call(
        weight_kernel,
        out_shape=(jax.ShapeDtypeStruct((D, HALF), bf16),) * 3,
        in_specs=[anywhere()] + [vmem()] * 4,
        out_specs=(vmem(), vmem(), vmem()),
        scratch_shapes=[pltpu.SemaphoreType.DMA],
        compiler_params=limit(8),
        cost_estimate=cost(10**6, 6 * 2**20),
        name="weights",
    )(qkv_weight, main, main_in, aux_in, aux_pair)
    q = pl.pallas_call(
        q_kernel,
        out_shape=jax.ShapeDtypeStruct((2 * ROWS, HALF), bf16),
        in_specs=[vmem()] * 3,
        out_specs=vmem(),
        cost_estimate=cost(2 * 512 * D * HALF, 3 * 2**20),
        compiler_params=limit(6),
    name="queries",
    )(own[0], other[0], wq)
    kv = []
    for hop in range(HOPS + 1):
        kv.append(
            pl.pallas_call(
                kv_kernel,
                out_shape=jax.ShapeDtypeStruct((2 * ROWS, D), bf16),
                in_specs=[vmem()] * 4,
                out_specs=vmem(),
                cost_estimate=cost(2 * 512 * D * D, 4 * 2**20),
                compiler_params=limit(8),
    name="keys",
            )(own[hop], other[hop], wk, wv)
        )
    mine, theirs = pl.pallas_call(
        attend_kernel,
        out_shape=(jax.ShapeDtypeStruct((ROWS, HALF), f32), jax.ShapeDtypeStruct((ROWS, HALF), f32)),
        in_specs=[vmem()] * 6,
        out_specs=(vmem(), vmem()),
        scratch_shapes=[
            pltpu.VMEM((2, ROWS, ROWS), f32),
            pltpu.VMEM((16, ROWS), f32),
            pltpu.VMEM((ROWS, SPAN * ROWS), f32),
            pltpu.VMEM((ROWS, SPAN * ROWS), f32),
            pltpu.VMEM((2, ROWS, HALF), f32),
        ],
        cost_estimate=cost(5 * 10**9, 6 * 2**20),
        compiler_params=limit(16),
    name="attend",
    )(q, *kv)
    received = lax.ppermute(theirs, "seq", swap)
    mixed = pl.pallas_call(
        out_kernel,
        out_shape=jax.ShapeDtypeStruct((ROWS, D), bf16),
        in_specs=[vmem()] * 6,
        out_specs=vmem(),
        compiler_params=limit(10),
        name="project",
    )(mine, received, attn_gain.reshape(1, D), out_weight, out_in, out_pair)
    return mixed[None]


def solution(mesh):
    in_specs = (
        P("fsdp", "seq", None),
        P("fsdp", "seq", None),
        P("fsdp", "seq"),
        P("seq", None),
        P(),
        P(),
        P(None, "fsdp"),
        P(None, "fsdp"),
        P(),
    )

    return jax.shard_map(local, mesh=mesh, in_specs=in_specs, out_specs=P("fsdp", "seq", None), check_vma=False)
```

time: 221 us -> 224 us (1.014)
  blocking collectives: 25.8 us -> 64.2 us
  Pallas kernels: 44.8 us -> 30.4 us
  starting transfers between devices: 33.5 us -> 21.9 us
  other arithmetic: 7.62 us -> 0.01 us
  waiting for transfers between devices: 95.2 us -> 91.2 us
  local copies, waits for them, and re-layouts: 12.8 us -> 15.7 us
    ppermute x1, waiting for transfers between devices: 0.01 us -> 57 us  [local(): aux_in = lax.ppermute(aux, 'fsdp', across)]
    all_to_all x0 -> x1, blocking collectives: none -> 38.6 us  [local(): lax.all_to_all(found, 'seq', split_axis=0, concat_axis=0, tiled=True)]
    ppermute x7, waiting for transfers between devices: 42.3 us -> 8.85 us  [the longest x1 7.78 us: local(): out_in = lax.ppermute(half, 'fsdp', across)]
    all_to_all x1 -> x0, waiting for transfers between devices: 28.3 us -> none  [local(): lax.all_to_all(found, 'seq', split_axis=0, concat_axis=0, tiled=True)]
    pallas_call x1, Pallas kernels: 33.2 us -> 19.4 us  [local(): pl.pallas_call(attend_kernel, out_shape=(jax.ShapeDtypeStruct((ROWS, HALF...]
    all_to_all x1 -> x0, starting transfers between devices: 7.88 us -> none  [local(): lax.all_to_all(found, 'seq', split_axis=0, concat_axis=0, tiled=True)]
    select_n x4 -> x0, other arithmetic: 6.55 us -> none  [the longest x1 3.31 us: local(): wk = jnp.where(par == f, k_here, jnp.concatenate([lower, upper], axis=1))]
    pallas_call x1 -> x9, Pallas kernels: 2.76 us -> 8 us  [the longest x5 6.23 us: local(): pl.pallas_call(kv_kernel, out_shape=jax.ShapeDtypeStruct((2 * ROWS, D), b...]
  transfers between devices with their start and end apart: 17 -> 16, of which waited for: 7 -> 7; matrix products, arithmetic and copies ran while one was open for 4% -> 0% of each run, Pallas kernels for 18% -> 12%
where the time goes in v2:
time: 224 us
  waiting for transfers between devices  91.2 us (41%)
  blocking collectives  64.2 us (29%)
  Pallas kernels  30.4 us (14%)
  starting transfers between devices  21.9 us (10%)
  local copies, waits for them, and re-layouts  15.7 us (7%)
    ppermute x1, waiting for transfers between devices, local(): aux_in = lax.ppermute(aux, 'fsdp', across)  57 us
    all_to_all x1, blocking collectives, local(): lax.all_to_all(found, 'seq', split_axis=0, concat_axis=0, tiled=True)  38.6 us
    all_to_all x1, blocking collectives, local(): lax.all_to_all(table, 'seq', split_axis=0, concat_axis=0, tiled=True)  25.6 us
    ppermute x4, waiting for transfers between devices, local(): own.append(lax.ppermute(own[-1], 'seq', ahead))  23.8 us
    pallas_call x1, Pallas kernels, local(): pl.pallas_call(attend_kernel, out_shape=(jax.ShapeDtypeStruct((ROWS, HALF...  19.4 us
    ppermute x4, starting transfers between devices, local(): own.append(lax.ppermute(own[-1], 'seq', ahead))  13.4 us
    ppermute x1, waiting for transfers between devices, local(): out_in = lax.ppermute(half, 'fsdp', across)  7.78 us
    pallas_call x5, Pallas kernels, local(): pl.pallas_call(kv_kernel, out_shape=jax.ShapeDtypeStruct((2 * ROWS, D), b...  6.23 us
  transfers between devices with their start and end apart: 16, of which 7 were waited for; matrix products, arithmetic and copies ran while one was open for 0% of the time, Pallas kernels for 12%

profile of v2, /device:TPU:25, one launch (start us, length us, event | category | flops | bytes accessed | tf_op | source)
XLA Modules:
  0.0 223.6 jit_solution(6205928992129332106)
XLA Ops:
  0.0 0.7 copy-done.8
  0.7 0.7 copy-done.9
  1.4 0.4 requests.1
  1.8 25.6 %all_to_all.23 = s32[128,1,128]{2,1,0:T(1,128)S(1)} all-to-all(s32[128,1,128]{2,1,0:T(1,128)S(1)} %bitcast.12), channel_id=1, replica_groups=mesh['seq'=128,'fsdp'=2] {'seq'}, dimensions={0} | all-to-all | bytes 131072 | tf_op jit(solution)/shard_map/all_to_all | solution.py:255
  27.4 0.1 reshape.45
  27.5 6.2 %gather_fusion = bf16[512,1024]{1,0:T(8,128)(2,1)} fusion(bf16[2048,1024]{1,0:T(8,128)(2,1)} %param.12, s32[1024]{0:T(1024)S(1)} %pad_clamp_fusion), kind=kCustom, calls=%fused_computation | custom fusion | bytes 2099200 | tf_op jit(solution)/shard_map/gather | solution.py:256
  33.7 2.4 %all_to_all.18 = bf16[128,4,1024]{2,1,0:T(4,128)(2,1)} reshape(bf16[512,1024]{1,0:T(8,128)(2,1)} %gather_fusion) | data formatting | bytes 2097152 | tf_op jit(solution)/shard_map/all_to_all | solution.py:257
  36.1 38.6 %all_to_all.24 = bf16[128,4,1024]{2,1,0:T(4,128)(2,1)} all-to-all(bf16[128,4,1024]{2,1,0:T(4,128)(2,1)} %all_to_all.18), channel_id=1, replica_groups=mesh['seq'=128,'fsdp'=2] {'seq'}, dimensions={0} | all-to-all | bytes 2097152 | tf_op jit(solution)/shard_map/all_to_all | solution.py:257
  74.7 2.2 all_to_all.20.fetched
  76.8 1.2 copy-done.1
  78.0 1.0 copy-done.4
  79.1 0.6 norm.1
  79.7 2.0 collective-permute-start
  81.7 1.1 collective-permute-done.rim
  82.8 1.0 conv.1.own
  83.8 3.8 %collective-permute-start.5 = (bf16[256,1024]{1,0:T(8,128)(2,1)S(1)}, bf16[256,1024]{1,0:T(8,128)(2,1)S(1)}, u32[]{:S(2)}, u32[]{:S(2)}) collective-permute-start(bf16[256,1024]{1,0:T(8,128)(2,1)S(1)} %conv.1.own), channel_id=1, source_target_pairs={{0,4},{2,6},{4,8},{6,10},{8,12},{10,14},{12,16},{14,18},{16,20},{1... | collective-permute-start | bytes 1572872 | tf_op jit(solution)/shard_map/ppermute | solution.py:278
  87.6 10.7 %collective-permute-done.5.own = bf16[256,1024]{1,0:T(8,128)(2,1)S(1)} collective-permute-done((bf16[256,1024]{1,0:T(8,128)(2,1)S(1)}, bf16[256,1024]{1,0:T(8,128)(2,1)S(1)}, u32[]{:S(2)}, u32[]{:S(2)}) %collective-permute-start.5) | collective-permute-done | bytes 524320 | tf_op jit(solution)/shard_map/ppermute | solution.py:278
  98.4 3.8 %collective-permute-start.7 = (bf16[256,1024]{1,0:T(8,128)(2,1)S(1)}, bf16[256,1024]{1,0:T(8,128)(2,1)S(1)}, u32[]{:S(2)}, u32[]{:S(2)}) collective-permute-start(bf16[256,1024]{1,0:T(8,128)(2,1)S(1)} %collective-permute-done.5.own), channel_id=1, source_target_pairs={{0,4},{2,6},{4,8},{6,10},{8,12},{10,14},{12,16},{14,18},{16,20},{1... | collective-permute-start | bytes 1572872 | tf_op jit(solution)/shard_map/ppermute | solution.py:278
  102.2 0.0 copy-start.2
  102.2 1.2 copy-done.2
  103.4 0.2 slabs.1
  103.6 0.4 collective-permute-start.2
  104.0 1.1 collective-permute-start.3
  105.2 6.8 %collective-permute-done.7.own = bf16[256,1024]{1,0:T(8,128)(2,1)S(1)} collective-permute-done((bf16[256,1024]{1,0:T(8,128)(2,1)S(1)}, bf16[256,1024]{1,0:T(8,128)(2,1)S(1)}, u32[]{:S(2)}, u32[]{:S(2)}) %collective-permute-start.7) | collective-permute-done | bytes 524320 | tf_op jit(solution)/shard_map/ppermute | solution.py:278
  112.0 3.9 %collective-permute-start.9 = (bf16[256,1024]{1,0:T(8,128)(2,1)S(1)}, bf16[256,1024]{1,0:T(8,128)(2,1)S(1)}, u32[]{:S(2)}, u32[]{:S(2)}) collective-permute-start(bf16[256,1024]{1,0:T(8,128)(2,1)S(1)} %collective-permute-done.7.own), channel_id=1, source_target_pairs={{0,4},{2,6},{4,8},{6,10},{8,12},{10,14},{12,16},{14,18},{16,20},{1... | collective-permute-start | bytes 1572872 | tf_op jit(solution)/shard_map/ppermute | solution.py:278
  115.9 0.4 collective-permute-start.14
  116.3 57.0 %collective-permute-done.3.aux_in = bf16[1024,256]{1,0:T(8,128)(2,1)S(1)} collective-permute-done((bf16[1024,256]{1,0:T(8,128)(2,1)S(1)}, bf16[1024,256]{1,0:T(8,128)(2,1)S(1)}, u32[]{:S(2)}, u32[]{:S(2)}) %collective-permute-start.3) | collective-permute-done | bytes 524320 | tf_op jit(solution)/shard_map/ppermute | solution.py:242
  173.3 1.4 collective-permute-start.4
  174.7 1.9 collective-permute-start.11
  176.7 0.1 collective-permute-start.1
  176.8 7.8 %collective-permute-done.14.w_mine = bf16[512,512]{1,0:T(8,128)(2,1)S(1)} collective-permute-done((bf16[512,512]{1,0:T(8,128)(2,1)S(1)}, bf16[512,512]{1,0:T(8,128)(2,1)S(1)}, u32[]{:S(2)}, u32[]{:S(2)}) %collective-permute-start.14) | collective-permute-done | bytes 524320 | tf_op jit(solution)/shard_map/ppermute | solution.py:243
  184.5 0.9 collective-permute-start.6
  185.5 0.5 collective-permute-start.10
  186.0 6.2 %collective-permute-done.11.own = bf16[256,1024]{1,0:T(8,128)(2,1)S(1)} collective-permute-done((bf16[256,1024]{1,0:T(8,128)(2,1)S(1)}, bf16[256,1024]{1,0:T(8,128)(2,1)S(1)}, u32[]{:S(2)}, u32[]{:S(2)}) %collective-permute-start.11) | collective-permute-done | bytes 524320 | tf_op jit(solution)/shard_map/ppermute | solution.py:278
  192.2 0.9 collective-permute-start.12
  193.1 0.3 weights.1
  193.4 0.1 collective-permute-start.15
  193.5 0.7 queries.1.q_ref
  194.2 1.2 keys.5.kv0
  195.5 1.2 keys.6.kv1
  196.7 1.2 keys.7.kv2
  198.0 1.2 keys.8.kv3
  199.2 1.2 keys.9.kv4
  200.5 0.0 copy-start.7
  200.5 19.4 %attend.1 = (f32[256,512]{1,0:T(8,128)S(1)}, f32[256,512]{1,0:T(8,128)S(1)}) custom-call(bf16[512,512]{1,0:T(8,128)(2,1)S(1)} %queries.1.q_ref, bf16[512,1024]{1,0:T(8,128)(2,1)S(1)} %keys.5.kv0, bf16[512,1024]{1,0:T(8,128)(2,1)S(1)} %keys.6.kv1, bf16[512,1024]{1,0:T(8,128)(2,1)S(1)} %keys.7.kv2, bf16[512,1024]{1,0:T(8,128)(2,1)S(1)} %keys.8.kv3, ...), custom_call_target="tpu_custom_call" | custom-call | flops 5000000000 | bytes 6291456 | tf_op jit(solution)/shard_map/attend/pallas_call | solution.py:315
  219.9 0.6 collective-permute-start.13
  220.5 1.5 collective-permute-done.13.received
  222.1 1.6 project.1
  (25 shorter events, 0.1 us)
Async XLA Ops:
  0.0 0.7 copy-start.8
  0.7 0.7 copy-start.9
  33.7 43.1 %copy-start.6 = (f32[1024]{0:T(1024)S(1)}, f32[1024]{0:T(1024)}, u32[]{:S(2)}) copy-start(f32[1024]{0:T(1024)} %param.13) | copy-start | bytes 12292
  33.7 49.1 %copy-start.5 = (bf16[7,1024]{1,0:T(8,128)(2,1)S(1)}, bf16[7,1024]{1,0:T(8,128)(2,1)}, u32[]{:S(2)}) copy-start(bf16[7,1024]{1,0:T(8,128)(2,1)} %taps.1) | copy-start | bytes 43012
  33.7 68.5 %copy-start = (bf16[1024,1536]{1,0:T(8,128)(2,1)S(1)}, bf16[1024,1536]{1,0:T(8,128)(2,1)}, u32[]{:S(2)}) copy-start(bf16[1024,1536]{1,0:T(8,128)(2,1)} %qkv.3) | copy-start | bytes 9437188
  76.8 1.2 copy-start.1
  78.0 1.0 copy-start.4
  79.7 3.1 %collective-permute-start = (bf16[8,1024]{1,0:T(8,128)(2,1)S(1)}, bf16[8,1024]{1,0:T(8,128)(2,1)S(1)}, u32[]{:S(2)}, u32[]{:S(2)}) collective-permute-start(bf16[8,1024]{1,0:T(8,128)(2,1)S(1)} %get-tuple-element.20), channel_id=1, source_target_pairs={{0,2},{2,4},{4,6},{6,8},{8,10},{10,12},{12,14},{14,16},{16,18},{18... | collective-permute-start | bytes 49160 | tf_op jit(solution)/shard_map/ppermute | solution.py:266
  83.8 14.5 %collective-permute-start.5 = (bf16[256,1024]{1,0:T(8,128)(2,1)S(1)}, bf16[256,1024]{1,0:T(8,128)(2,1)S(1)}, u32[]{:S(2)}, u32[]{:S(2)}) collective-permute-start(bf16[256,1024]{1,0:T(8,128)(2,1)S(1)} %conv.1.own), channel_id=1, source_target_pairs={{0,4},{2,6},{4,8},{6,10},{8,12},{10,14},{12,16},{14,18},{16,20},{1... | collective-permute-start | bytes 1572872 | tf_op jit(solution)/shard_map/ppermute | solution.py:278
  98.4 13.6 %collective-permute-start.7 = (bf16[256,1024]{1,0:T(8,128)(2,1)S(1)}, bf16[256,1024]{1,0:T(8,128)(2,1)S(1)}, u32[]{:S(2)}, u32[]{:S(2)}) collective-permute-start(bf16[256,1024]{1,0:T(8,128)(2,1)S(1)} %collective-permute-done.5.own), channel_id=1, source_target_pairs={{0,4},{2,6},{4,8},{6,10},{8,12},{10,14},{12,16},{14,18},{16,20},{1... | collective-permute-start | bytes 1572872 | tf_op jit(solution)/shard_map/ppermute | solution.py:278
  102.2 1.2 copy-start.2
  103.6 81.8 %collective-permute-start.2 = (bf16[1024,512]{1,0:T(8,128)(2,1)S(1)}, bf16[1024,512]{1,0:T(8,128)(2,1)S(1)}, u32[]{:S(2)}, u32[]{:S(2)}) collective-permute-start(bf16[1024,512]{1,0:T(8,128)(2,1)S(1)} %get-tuple-element.21.main), channel_id=1, source_target_pairs={{0,1},{1,0},{2,3},{3,2},{4,5},{5,4},{6,7},{7,6},{8,9},{9,8},{10,11... | collective-permute-start | bytes 3145736 | tf_op jit(solution)/shard_map/ppermute | solution.py:241
  104.0 69.3 %collective-permute-start.3 = (bf16[1024,256]{1,0:T(8,128)(2,1)S(1)}, bf16[1024,256]{1,0:T(8,128)(2,1)S(1)}, u32[]{:S(2)}, u32[]{:S(2)}) collective-permute-start(bf16[1024,256]{1,0:T(8,128)(2,1)S(1)} %get-tuple-element.22), channel_id=1, source_target_pairs={{0,1},{1,0},{2,3},{3,2},{4,5},{5,4},{6,7},{7,6},{8,9},{9,8},{10,11... | collective-permute-start | bytes 1572872 | tf_op jit(solution)/shard_map/ppermute | solution.py:242
  112.0 62.7 %collective-permute-start.9 = (bf16[256,1024]{1,0:T(8,128)(2,1)S(1)}, bf16[256,1024]{1,0:T(8,128)(2,1)S(1)}, u32[]{:S(2)}, u32[]{:S(2)}) collective-permute-start(bf16[256,1024]{1,0:T(8,128)(2,1)S(1)} %collective-permute-done.7.own), channel_id=1, source_target_pairs={{0,4},{2,6},{4,8},{6,10},{8,12},{10,14},{12,16},{14,18},{16,20},{1... | collective-permute-start | bytes 1572872 | tf_op jit(solution)/shard_map/ppermute | solution.py:278
  115.9 68.6 %collective-permute-start.14 = (bf16[512,512]{1,0:T(8,128)(2,1)S(1)}, bf16[512,512]{1,0:T(8,128)(2,1)S(1)}, u32[]{:S(2)}, u32[]{:S(2)}) collective-permute-start(bf16[512,512]{1,0:T(8,128)(2,1)S(1)} %get-tuple-element.28), channel_id=1, source_target_pairs={{0,1},{1,0},{2,3},{3,2},{4,5},{5,4},{6,7},{7,6},{8,9},{9,8},{10,11... | collective-permute-start | bytes 1572872 | tf_op jit(solution)/shard_map/ppermute | solution.py:243
  173.3 12.2 %collective-permute-start.4 = (bf16[1024,256]{1,0:T(8,128)(2,1)S(1)}, bf16[1024,256]{1,0:T(8,128)(2,1)S(1)}, u32[]{:S(2)}, u32[]{:S(2)}) collective-permute-start(bf16[1024,256]{1,0:T(8,128)(2,1)S(1)} %collective-permute-done.3.aux_in), channel_id=1, source_target_pairs={{0,2},{2,0},{4,6},{6,4},{8,10},{10,8},{12,14},{14,12},{16,18},{18,... | collective-permute-start | bytes 1572872 | tf_op jit(solution)/shard_map/ppermute | solution.py:244
  174.7 17.5 %collective-permute-start.11 = (bf16[256,1024]{1,0:T(8,128)(2,1)S(1)}, bf16[256,1024]{1,0:T(8,128)(2,1)S(1)}, u32[]{:S(2)}, u32[]{:S(2)}) collective-permute-start(bf16[256,1024]{1,0:T(8,128)(2,1)S(1)} %collective-permute-done.9.own), channel_id=1, source_target_pairs={{0,4},{2,6},{4,8},{6,10},{8,12},{10,14},{12,16},{14,18},{16,20},{1... | collective-permute-start | bytes 1572872 | tf_op jit(solution)/shard_map/ppermute | solution.py:278
  176.7 16.7 %collective-permute-start.1 = (bf16[256,1024]{1,0:T(8,128)(2,1)S(1)}, bf16[256,1024]{1,0:T(8,128)(2,1)S(1)}, u32[]{:S(2)}, u32[]{:S(2)}) collective-permute-start(bf16[256,1024]{1,0:T(8,128)(2,1)S(1)} %conv.1.own), channel_id=1, source_target_pairs={{0,2},{2,0},{4,6},{6,4},{8,10},{10,8},{12,14},{14,12},{16,18},{18,... | collective-permute-start | bytes 1572872 | tf_op jit(solution)/shard_map/ppermute | solution.py:281
  184.5 10.9 %collective-permute-start.6 = (bf16[256,1024]{1,0:T(8,128)(2,1)S(1)}, bf16[256,1024]{1,0:T(8,128)(2,1)S(1)}, u32[]{:S(2)}, u32[]{:S(2)}) collective-permute-start(bf16[256,1024]{1,0:T(8,128)(2,1)S(1)} %collective-permute-done.5.own), channel_id=1, source_target_pairs={{0,2},{2,0},{4,6},{6,4},{8,10},{10,8},{12,14},{14,12},{16,18},{18,... | collective-permute-start | bytes 1572872 | tf_op jit(solution)/shard_map/ppermute | solution.py:281
  185.5 11.2 %collective-permute-start.8 = (bf16[256,1024]{1,0:T(8,128)(2,1)S(1)}, bf16[256,1024]{1,0:T(8,128)(2,1)S(1)}, u32[]{:S(2)}, u32[]{:S(2)}) collective-permute-start(bf16[256,1024]{1,0:T(8,128)(2,1)S(1)} %collective-permute-done.7.own), channel_id=1, source_target_pairs={{0,2},{2,0},{4,6},{6,4},{8,10},{10,8},{12,14},{14,12},{16,18},{18,... | collective-permute-start | bytes 1572872 | tf_op jit(solution)/shard_map/ppermute | solution.py:281
  185.5 12.5 %collective-permute-start.10 = (bf16[256,1024]{1,0:T(8,128)(2,1)S(1)}, bf16[256,1024]{1,0:T(8,128)(2,1)S(1)}, u32[]{:S(2)}, u32[]{:S(2)}) collective-permute-start(bf16[256,1024]{1,0:T(8,128)(2,1)S(1)} %collective-permute-done.9.own), channel_id=1, source_target_pairs={{0,2},{2,0},{4,6},{6,4},{8,10},{10,8},{12,14},{14,12},{16,18},{18,... | collective-permute-start | bytes 1572872 | tf_op jit(solution)/shard_map/ppermute | solution.py:281
  192.2 7.0 %collective-permute-start.12 = (bf16[256,1024]{1,0:T(8,128)(2,1)S(1)}, bf16[256,1024]{1,0:T(8,128)(2,1)S(1)}, u32[]{:S(2)}, u32[]{:S(2)}) collective-permute-start(bf16[256,1024]{1,0:T(8,128)(2,1)S(1)} %collective-permute-done.11.own), channel_id=1, source_target_pairs={{0,2},{2,0},{4,6},{6,4},{8,10},{10,8},{12,14},{14,12},{16,18},{18,... | collective-permute-start | bytes 1572872 | tf_op jit(solution)/shard_map/ppermute | solution.py:281
  193.4 27.1 %collective-permute-start.15 = (bf16[512,512]{1,0:T(8,128)(2,1)S(1)}, bf16[512,512]{1,0:T(8,128)(2,1)S(1)}, u32[]{:S(2)}, u32[]{:S(2)}) collective-permute-start(bf16[512,512]{1,0:T(8,128)(2,1)S(1)} %collective-permute-done.14.w_mine), channel_id=1, source_target_pairs={{0,2},{2,0},{4,6},{6,4},{8,10},{10,8},{12,14},{14,12},{16,18},{18,... | collective-permute-start | bytes 1572872 | tf_op jit(solution)/shard_map/ppermute | solution.py:245
  200.5 21.6 %copy-start.3 = (bf16[1024,512]{1,0:T(8,128)(2,1)S(1)}, bf16[1024,512]{1,0:T(8,128)(2,1)}, u32[]{:S(2)}) copy-start(bf16[1024,512]{1,0:T(8,128)(2,1)} %w_here.1) | copy-start | bytes 3145732
  200.5 21.6 %copy-start.7 = (f32[1024]{0:T(1024)S(1)}, f32[1024]{0:T(1024)}, u32[]{:S(2)}) copy-start(f32[1024]{0:T(1024)} %param.17) | copy-start | bytes 12292
  219.9 2.1 collective-permute-start.13

commit v3 on v2

--- a/solution.py
+++ b/solution.py
@@ -1,3 +1,5 @@
+import functools
+
 import jax
 import jax.numpy as jnp
 from jax import lax
@@ -6,7 +8,6 @@
 from jax.sharding import PartitionSpec as P
 
 HEAD = 64
-WINDOW = 2048
 EPSILON = 1e-05
 ROWS = 256
 D = 1024
@@ -14,8 +15,9 @@
 OWNERS = 128
 SLOTS = 4
 HOPS = 4
-SPAN = WINDOW // ROWS + 1
 LOG2E = 1.4426950408889634
+SCALE = LOG2E * HEAD ** (-0.5)
+MASKED = -1e30
 
 bf16 = jnp.bfloat16
 f32 = jnp.float32
@@ -37,13 +39,14 @@
     return pl.CostEstimate(flops=flops, bytes_accessed=moved, transcendentals=0)
 
 
-def slab_kernel(qkv, out, main, aux, half, sems):
+def slab_kernel(qkv, out, main, aux, half, keys, sems):
     par = lax.rem(lax.axis_index("seq"), 2)
     f = lax.axis_index("fsdp")
     copies = (
         pltpu.make_async_copy(qkv.at[:, pl.ds(pl.multiple_of(HALF * (par + f), HALF), HALF)], main, sems.at[0]),
         pltpu.make_async_copy(qkv.at[:, pl.ds(pl.multiple_of(D * (1 - f) + 256 * par, 256), 256)], aux, sems.at[1]),
         pltpu.make_async_copy(out.at[pl.ds(pl.multiple_of(HALF * par, HALF), HALF), :], half, sems.at[2]),
+        pltpu.make_async_copy(qkv.at[:, pl.ds(pl.multiple_of(D * (1 - f), D), HALF)], keys, sems.at[3]),
     )
     for copy in copies:
         copy.start()
@@ -51,15 +54,13 @@
         copy.wait()
 
 
-def weight_kernel(qkv, main, main_in, aux_in, aux_pair, wq, wk, wv, sem):
+def weight_kernel(keys, main, main_in, aux_in, aux_pair, wq, wk, wv):
     par = lax.rem(lax.axis_index("seq"), 2)
     f = lax.axis_index("fsdp")
 
     @pl.when(par == f)
     def _():
-        copy = pltpu.make_async_copy(qkv.at[:, pl.ds(pl.multiple_of(D * (1 - f), D), HALF)], wk, sem)
-        copy.start()
-        copy.wait()
+        wk[...] = keys[...]
 
     @pl.when(par != f)
     def _():
@@ -122,14 +123,6 @@
     lax.fori_loop(0, D // 128, column, 0)
 
 
-def kv_kernel(own, other, wk, wv, kv):
-    par = lax.rem(lax.axis_index("seq"), 2)
-    for x, side in ((own, par), (other, 1 - par)):
-        at = pl.ds(pl.multiple_of(side * ROWS, ROWS), ROWS)
-        kv[at, :HALF] = jnp.dot(x[...], wk[...], preferred_element_type=f32).astype(bf16)
-        kv[at, HALF:] = jnp.dot(x[...], wv[...], preferred_element_type=f32).astype(bf16)
-
-
 def q_kernel(own, other, wq, q):
     par = lax.rem(lax.axis_index("seq"), 2)
     for x, side in ((own, par), (other, 1 - par)):
@@ -137,66 +130,113 @@
         q[at, :] = jnp.dot(x[...], wq[...], preferred_element_type=f32).astype(bf16)
 
 
-def attend_kernel(q_ref, kv0, kv1, kv2, kv3, kv4, mine, theirs, edge, bias, sc0, sc1, done):
-    kv = (kv0, kv1, kv2, kv3, kv4)
+def blocks_of(k):
+    if k == 0:
+        return ((0, 0, 1), (1, 0, 0), (1, 1, 1))
+    if k == HOPS:
+        return ((0, 0, 2), (0, 1, 0), (1, 1, 2))
+    return ((0, 0, 0), (0, 1, 0), (1, 0, 0), (1, 1, 0))
+
+
+def score_block(k, own, other, wk, wv, q_ref, v_ref, e_ref, top_ref, sum_ref, k_ref):
+    par = lax.rem(lax.axis_index("seq"), 2)
+    for x, side in ((own, par), (other, 1 - par)):
+        at = pl.ds(pl.multiple_of(side * ROWS, ROWS), ROWS)
+        k_ref[at, :] = jnp.dot(x[...], wk[...], preferred_element_type=f32).astype(bf16)
+        v_ref[at, :] = jnp.dot(x[...], wv[...], preferred_element_type=f32).astype(bf16)
+    row = lax.broadcasted_iota(jnp.int32, (ROWS, ROWS), 0)
+    col = lax.broadcasted_iota(jnp.int32, (ROWS, ROWS), 1)
+    lane = lax.broadcasted_iota(jnp.int32, (ROWS, 128), 1)
+    blocks = blocks_of(k)
+    count = len(blocks)
+    top_ref[...] = jnp.zeros((2, ROWS, 128), f32)
+    sum_ref[...] = jnp.zeros((2, ROWS, 128), f32)
+
+    def at_block(h, i):
+        return pl.ds(pl.multiple_of((h * count + i) * ROWS, ROWS), ROWS)
+
+    def pair(hp, carry):
+        lanes = pl.ds(pl.multiple_of(hp * 128, 128), 128)
+        tops = {}
+        for side in range(2):
+            h = 2 * hp + side
+            for i, (qb, half, edge) in enumerate(blocks):
+                q = q_ref[qb * ROWS : (qb + 1) * ROWS, lanes]
+                q = jnp.where((lane < HEAD) == (side == 0), q, jnp.zeros_like(q))
+                keys = k_ref[half * ROWS : (half + 1) * ROWS, lanes]
+                s = lax.dot_general(q, keys, (((1,), (1,)), ((), ())), preferred_element_type=f32)
+                if edge:
+                    s = jnp.where(col <= row if edge == 1 else col > row, s, MASKED)
+                e_ref[at_block(h, i), :] = s
+                part = jnp.maximum(s[:, :128], s[:, 128:])
+                known = tops.get((side, qb))
+                tops[side, qb] = part if known is None else jnp.maximum(known, part)
+        for side in range(2):
+            h = 2 * hp + side
+            for qb in range(2):
+                top = jnp.max(tops[side, qb], axis=1, keepdims=True)
+                total = None
+                for i, (which, half, edge) in enumerate(blocks):
+                    if which == qb:
+                        e = jnp.exp2((e_ref[at_block(h, i), :] - top) * SCALE)
+                        e_ref[at_block(h, i), :] = e
+                        part = e[:, :128] + e[:, 128:]
+                        total = part if total is None else total + part
+                total = jnp.sum(total, axis=1, keepdims=True)
+                top_ref[qb] = jnp.where(lane == h, top, top_ref[qb])
+                sum_ref[qb] = jnp.where(lane == h, total, sum_ref[qb])
+        return carry
+
+    lax.fori_loop(0, 4, pair, 0)
+
+
+def attend_kernel(*refs):
+    q_ref, own, other, wk, wv = refs[:5]
+    values, es, tops, sums = (refs[5 + HOPS * i : 5 + HOPS * (i + 1)] for i in range(4))
+    mine, theirs, v_last, e_last, top_last, sum_last, k_last, factor, done = refs[5 + 4 * HOPS :]
+    score_block(HOPS, own, other, wk, wv, q_ref, v_last, e_last, top_last, sum_last, k_last)
+    values, es = values + (v_last,), es + (e_last,)
+    tops, sums = tops + (top_last,), sums + (sum_last,)
     seq = lax.axis_index("seq")
     par = lax.rem(seq, 2)
     chip = seq // 2
-    row = lax.broadcasted_iota(jnp.int32, (ROWS, ROWS), 0)
-    col = lax.broadcasted_iota(jnp.int32, (ROWS, ROWS), 1)
-    edge[0] = jnp.where(col > row, 0.0, -jnp.inf).astype(f32)
-    edge[1] = jnp.where(col <= row, 0.0, -jnp.inf).astype(f32)
-    block = lax.broadcasted_iota(jnp.int32, (16, ROWS), 0)
-    bias[...] = jnp.where(block + 2 * (chip - HOPS) >= 0, 0.0, -jnp.inf).astype(f32)
     lane = lax.broadcasted_iota(jnp.int32, (ROWS, 128), 1)
-
-    def place(h, b, value):
-        lanes = pl.ds(pl.multiple_of(value * HALF + (h // 2) * 128, 128), 128)
-        return kv[HOPS - b // 2][(b % 2) * ROWS : (b % 2 + 1) * ROWS, lanes]
-
-    def scores(qb, h, sc):
-        lanes = pl.ds(pl.multiple_of((h // 2) * 128, 128), 128)
-        q = q_ref[qb * ROWS : (qb + 1) * ROWS, lanes]
-        q = jnp.where((lane // HEAD) == lax.rem(h, 2), q, jnp.zeros_like(q))
-        top = None
-        for kb in range(SPAN):
-            s = lax.dot_general(q, place(h, qb + kb, 0), (((1,), (1,)), ((), ())), preferred_element_type=f32)
-            if kb < SPAN - 1:
-                s = s + bias[qb + kb : qb + kb + 1, :]
-            if kb == 0:
-                s = s + edge[0]
-            if kb == SPAN - 1:
-                s = s + edge[1]
-            sc[:, kb * ROWS : (kb + 1) * ROWS] = s
-            part = jnp.maximum(s[:, :128], s[:, 128:])
-            top = part if top is None else jnp.maximum(top, part)
-        return jnp.max(top, axis=1, keepdims=True)
-
-    def weigh(qb, h, sc, top):
-        total = None
-        for kb in range(SPAN):
-            e = jnp.exp2((sc[:, kb * ROWS : (kb + 1) * ROWS] - top) * (LOG2E * HEAD ** (-0.5)))
-            sc[:, kb * ROWS : (kb + 1) * ROWS] = e
-            part = e[:, :128] + e[:, 128:]
-            total = part if total is None else total + part
-        inverse = 1.0 / jnp.sum(total, axis=1, keepdims=True)
-        acc = None
-        for kb in range(SPAN):
-            p = (sc[:, kb * ROWS : (kb + 1) * ROWS] * inverse).astype(bf16)
-            part = jnp.dot(p, place(h, qb + kb, 1), preferred_element_type=f32)
-            acc = part if acc is None else acc + part
-        lanes = pl.ds(pl.multiple_of((h // 2) * 128, 128), 128)
-        old = done[qb, :, lanes]
-        done[qb, :, lanes] = jnp.where((lane // HEAD) == lax.rem(h, 2), acc, old)
-
-    def head(h, top0):
-        top1 = scores(1, h, sc1)
-        weigh(0, h, sc0, top0)
-        after = scores(0, jnp.minimum(h + 1, 7), sc0)
-        weigh(1, h, sc1, top1)
-        return after
-
-    lax.fori_loop(0, 8, head, scores(0, 0, sc0))
+    for qb in range(2):
+        top = tops[0][qb]
+        for k in range(1, HOPS + 1):
+            top = jnp.where(chip >= k, jnp.maximum(top, tops[k][qb]), top)
+        total = jnp.zeros((ROWS, 128), f32)
+        for k in range(HOPS + 1):
+            weight = jnp.exp2((tops[k][qb] - top) * SCALE)
+            weight = jnp.where(chip >= k, weight, 0.0)
+            factor[qb, k] = weight
+            total = total + weight * sums[k][qb]
+        inverse = 1.0 / jnp.where(lane < 8, total, 1.0)
+        for k in range(HOPS + 1):
+            factor[qb, k] = factor[qb, k] * inverse
+
+    def pair(hp, carry):
+        lanes = pl.ds(pl.multiple_of(hp * 128, 128), 128)
+        for qb in range(2):
+            outs = []
+            for side in range(2):
+                h = 2 * hp + side
+                acc = None
+                for k in range(HOPS + 1):
+                    blocks = blocks_of(k)
+                    column = jnp.sum(jnp.where(lane == h, factor[qb, k], 0.0), axis=1, keepdims=True)
+                    for i, (which, half, edge) in enumerate(blocks):
+                        if which == qb:
+                            at = pl.ds(pl.multiple_of((h * len(blocks) + i) * ROWS, ROWS), ROWS)
+                            p = (es[k][at, :] * column).astype(bf16)
+                            value = values[k][half * ROWS : (half + 1) * ROWS, lanes]
+                            part = jnp.dot(p, value, preferred_element_type=f32)
+                            acc = part if acc is None else acc + part
+                outs.append(acc)
+            done[qb, :, lanes] = jnp.where(lane < HEAD, outs[0], outs[1])
+        return carry
+
+    lax.fori_loop(0, 4, pair, 0)
     mine[...] = done[par]
     theirs[...] = done[1 - par]
 
@@ -225,19 +265,20 @@
     swap = [(i, i ^ 1) for i in range(count)]
     ahead = [(i, i + 2) for i in range(count - 2)]
 
-    main, aux, half = pl.pallas_call(
+    main, aux, half, keys = pl.pallas_call(
         slab_kernel,
         out_shape=(
             jax.ShapeDtypeStruct((D, HALF), bf16),
             jax.ShapeDtypeStruct((D, 256), bf16),
             jax.ShapeDtypeStruct((HALF, HALF), bf16),
+            jax.ShapeDtypeStruct((D, HALF), bf16),
         ),
         in_specs=[anywhere()] * 2,
-        out_specs=(vmem(), vmem(), vmem()),
-        scratch_shapes=[pltpu.SemaphoreType.DMA((3,))],
-        compiler_params=limit(4),
+        out_specs=(vmem(), vmem(), vmem(), vmem()),
+        scratch_shapes=[pltpu.SemaphoreType.DMA((4,))],
+        compiler_params=limit(6),
         name="slabs",
-    )(qkv_weight, out_weight)
+    )(*(pltpu.with_memory_space_constraint(w, pltpu.HBM) for w in (qkv_weight, out_weight)))
     main_in = lax.ppermute(main, "fsdp", across)
     aux_in = lax.ppermute(aux, "fsdp", across)
     out_in = lax.ppermute(half, "fsdp", across)
@@ -283,13 +324,12 @@
     wq, wk, wv = pl.pallas_call(
         weight_kernel,
         out_shape=(jax.ShapeDtypeStruct((D, HALF), bf16),) * 3,
-        in_specs=[anywhere()] + [vmem()] * 4,
+        in_specs=[vmem()] * 5,
         out_specs=(vmem(), vmem(), vmem()),
-        scratch_shapes=[pltpu.SemaphoreType.DMA],
         compiler_params=limit(8),
         cost_estimate=cost(10**6, 6 * 2**20),
         name="weights",
-    )(qkv_weight, main, main_in, aux_in, aux_pair)
+    )(keys, main, main_in, aux_in, aux_pair)
     q = pl.pallas_call(
         q_kernel,
         out_shape=jax.ShapeDtypeStruct((2 * ROWS, HALF), bf16),
@@ -298,36 +338,49 @@
         cost_estimate=cost(2 * 512 * D * HALF, 3 * 2**20),
         compiler_params=limit(6),
     name="queries",
-    )(own[0], other[0], wq)
-    kv = []
-    for hop in range(HOPS + 1):
-        kv.append(
+    )(x, other[0], wq)
+
+    def stats():
+        return jax.ShapeDtypeStruct((2, ROWS, 128), f32)
+
+    found = []
+    for hop in range(HOPS):
+        size = len(blocks_of(hop)) * 8 * ROWS
+        found.append(
             pl.pallas_call(
-                kv_kernel,
-                out_shape=jax.ShapeDtypeStruct((2 * ROWS, D), bf16),
-                in_specs=[vmem()] * 4,
-                out_specs=vmem(),
-                cost_estimate=cost(2 * 512 * D * D, 4 * 2**20),
-                compiler_params=limit(8),
-    name="keys",
-            )(own[hop], other[hop], wk, wv)
+                functools.partial(score_block, hop),
+                out_shape=(
+                    jax.ShapeDtypeStruct((2 * ROWS, HALF), bf16),
+                    jax.ShapeDtypeStruct((size, ROWS), f32),
+                    stats(),
+                    stats(),
+                ),
+                in_specs=[vmem()] * 5,
+                out_specs=(vmem(),) * 4,
+                scratch_shapes=[pltpu.VMEM((2 * ROWS, HALF), bf16)],
+                compiler_params=limit(4),
+                cost_estimate=cost(2 * 10**9, 4 * 2**20),
+                name="near",
+            )(own[hop], other[hop], wk, wv, q)
         )
     mine, theirs = pl.pallas_call(
         attend_kernel,
         out_shape=(jax.ShapeDtypeStruct((ROWS, HALF), f32), jax.ShapeDtypeStruct((ROWS, HALF), f32)),
-        in_specs=[vmem()] * 6,
+        in_specs=[vmem()] * (5 + 4 * HOPS),
         out_specs=(vmem(), vmem()),
         scratch_shapes=[
-            pltpu.VMEM((2, ROWS, ROWS), f32),
-            pltpu.VMEM((16, ROWS), f32),
-            pltpu.VMEM((ROWS, SPAN * ROWS), f32),
-            pltpu.VMEM((ROWS, SPAN * ROWS), f32),
+            pltpu.VMEM((2 * ROWS, HALF), bf16),
+            pltpu.VMEM((len(blocks_of(HOPS)) * 8 * ROWS, ROWS), f32),
+            pltpu.VMEM((2, ROWS, 128), f32),
+            pltpu.VMEM((2, ROWS, 128), f32),
+            pltpu.VMEM((2 * ROWS, HALF), bf16),
+            pltpu.VMEM((2, HOPS + 1, ROWS, 128), f32),
             pltpu.VMEM((2, ROWS, HALF), f32),
         ],
+        compiler_params=limit(14),
         cost_estimate=cost(5 * 10**9, 6 * 2**20),
-        compiler_params=limit(16),
-    name="attend",
-    )(q, *kv)
+        name="attend",
+    )(q, own[HOPS], other[HOPS], wk, wv, *(found[k][i] for i in range(4) for k in range(HOPS)))
     received = lax.ppermute(theirs, "seq", swap)
     mixed = pl.pallas_call(
         out_kernel,

time: 224 us -> 216 us (0.964)
  local copies, waits for them, and re-layouts: 15.7 us -> 8.77 us
  Pallas kernels: 30.4 us -> 36.9 us
  waiting for transfers between devices: 91.2 us -> 86.4 us
    ppermute x1, waiting for transfers between devices: 7.78 us -> 36.8 us  [local(): out_in = lax.ppermute(half, 'fsdp', across)]
    ppermute x1, waiting for transfers between devices: 57 us -> 29.8 us  [local(): aux_in = lax.ppermute(aux, 'fsdp', across)]
    pallas_call x5 -> x4, Pallas kernels: 6.23 us -> 19.2 us  [local(): pl.pallas_call(functools.partial(score_block, hop), out_shape=(jax.ShapeD...]
    pallas_call x1, Pallas kernels: 19.4 us -> 11.1 us  [local(): pl.pallas_call(attend_kernel, out_shape=(jax.ShapeDtypeStruct((ROWS, HALF...]
    ppermute x4, waiting for transfers between devices: 23.8 us -> 17 us  [local(): own.append(lax.ppermute(own[-1], 'seq', ahead))]
    unnamed x20 -> x14, local copies, waits for them, and re-layouts: 4.87 us -> 1.39 us
    all_to_all x2, local copies, waits for them, and re-layouts: 4.55 us -> 1.76 us  [local(): lax.all_to_all(found, 'seq', split_axis=0, concat_axis=0, tiled=True)]
  transfers between devices with their start and end apart: 16 -> 16, of which waited for: 7 -> 6; matrix products, arithmetic and copies ran while one was open for 0% -> 0% of each run, Pallas kernels for 12% -> 15%
where the time goes in v3:
time: 216 us
  waiting for transfers between devices  86.4 us (40%)
  blocking collectives  63.3 us (29%)
  Pallas kernels  36.9 us (17%)
  starting transfers between devices  20.2 us (9%)
  local copies, waits for them, and re-layouts  8.77 us (4%)
    all_to_all x1, blocking collectives, local(): lax.all_to_all(found, 'seq', split_axis=0, concat_axis=0, tiled=True)  37.7 us
    ppermute x1, waiting for transfers between devices, local(): out_in = lax.ppermute(half, 'fsdp', across)  36.8 us
    ppermute x1, waiting for transfers between devices, local(): aux_in = lax.ppermute(aux, 'fsdp', across)  29.8 us
    all_to_all x1, blocking collectives, local(): lax.all_to_all(table, 'seq', split_axis=0, concat_axis=0, tiled=True)  25.6 us
    pallas_call x4, Pallas kernels, local(): pl.pallas_call(functools.partial(score_block, hop), out_shape=(jax.ShapeD...  19.2 us
    ppermute x4, waiting for transfers between devices, local(): own.append(lax.ppermute(own[-1], 'seq', ahead))  17 us
    ppermute x4, starting transfers between devices, local(): own.append(lax.ppermute(own[-1], 'seq', ahead))  13.4 us
    pallas_call x1, Pallas kernels, local(): pl.pallas_call(attend_kernel, out_shape=(jax.ShapeDtypeStruct((ROWS, HALF...  11.1 us
  transfers between devices with their start and end apart: 16, of which 6 were waited for; matrix products, arithmetic and copies ran while one was open for 0% of the time, Pallas kernels for 15%

profile of v3, /device:TPU:25, one launch (start us, length us, event | category | flops | bytes accessed | tf_op | source)
XLA Modules:
  0.0 215.8 jit_solution(252916792554669743)
XLA Ops:
  0.0 0.7 copy-done.5
  0.7 0.7 copy-done.6
  1.4 0.4 requests.1
  1.8 25.6 %all_to_all.23 = s32[128,1,128]{2,1,0:T(1,128)S(1)} all-to-all(s32[128,1,128]{2,1,0:T(1,128)S(1)} %bitcast.12), channel_id=1, replica_groups=mesh['seq'=128,'fsdp'=2] {'seq'}, dimensions={0} | all-to-all | bytes 131072 | tf_op jit(solution)/shard_map/all_to_all | solution.py:296
  27.4 0.1 reshape.45
  27.5 0.0 copy-start.1
  27.5 0.0 copy-start.3
  27.5 5.5 %gather_fusion = bf16[512,1024]{1,0:T(8,128)(2,1)S(1)} fusion(bf16[2048,1024]{1,0:T(8,128)(2,1)} %param.12, s32[1024]{0:T(1024)S(1)} %pad_clamp_fusion), kind=kCustom, calls=%fused_computation | custom fusion | bytes 2099200 | tf_op jit(solution)/shard_map/gather | solution.py:297
  33.0 0.0 copy-start.2
  33.1 0.4 all_to_all.18
  33.5 37.7 %all_to_all.24 = bf16[128,4,1024]{2,1,0:T(4,128)(2,1)} all-to-all(bf16[128,4,1024]{2,1,0:T(4,128)(2,1)S(1)} %all_to_all.18), channel_id=1, replica_groups=mesh['seq'=128,'fsdp'=2] {'seq'}, dimensions={0} | all-to-all | bytes 2097152 | tf_op jit(solution)/shard_map/all_to_all | solution.py:298
  71.2 1.3 all_to_all.20.fetched
  72.5 0.6 norm.1
  73.1 2.0 collective-permute-start
  75.2 1.1 collective-permute-done.rim
  76.2 1.0 conv.1.own
  77.3 3.8 %collective-permute-start.5 = (bf16[256,1024]{1,0:T(8,128)(2,1)S(1)}, bf16[256,1024]{1,0:T(8,128)(2,1)S(1)}, u32[]{:S(2)}, u32[]{:S(2)}) collective-permute-start(bf16[256,1024]{1,0:T(8,128)(2,1)S(1)} %conv.1.own), channel_id=1, source_target_pairs={{0,4},{2,6},{4,8},{6,10},{8,12},{10,14},{12,16},{14,18},{16,20},{1... | collective-permute-start | bytes 1572872 | tf_op jit(solution)/shard_map/ppermute | solution.py:319
  81.1 10.7 %collective-permute-done.5.own = bf16[256,1024]{1,0:T(8,128)(2,1)S(1)} collective-permute-done((bf16[256,1024]{1,0:T(8,128)(2,1)S(1)}, bf16[256,1024]{1,0:T(8,128)(2,1)S(1)}, u32[]{:S(2)}, u32[]{:S(2)}) %collective-permute-start.5) | collective-permute-done | bytes 524320 | tf_op jit(solution)/shard_map/ppermute | solution.py:319
  91.8 3.8 %collective-permute-start.6 = (bf16[256,1024]{1,0:T(8,128)(2,1)S(1)}, bf16[256,1024]{1,0:T(8,128)(2,1)S(1)}, u32[]{:S(2)}, u32[]{:S(2)}) collective-permute-start(bf16[256,1024]{1,0:T(8,128)(2,1)S(1)} %collective-permute-done.5.own), channel_id=1, source_target_pairs={{0,4},{2,6},{4,8},{6,10},{8,12},{10,14},{12,16},{14,18},{16,20},{1... | collective-permute-start | bytes 1572872 | tf_op jit(solution)/shard_map/ppermute | solution.py:319
  95.6 1.9 slabs.1
  97.6 0.4 collective-permute-start.3
  98.0 1.2 collective-permute-start.2
  99.1 6.3 %collective-permute-done.6.own = bf16[256,1024]{1,0:T(8,128)(2,1)S(1)} collective-permute-done((bf16[256,1024]{1,0:T(8,128)(2,1)S(1)}, bf16[256,1024]{1,0:T(8,128)(2,1)S(1)}, u32[]{:S(2)}, u32[]{:S(2)}) %collective-permute-start.6) | collective-permute-done | bytes 524320 | tf_op jit(solution)/shard_map/ppermute | solution.py:319
  105.4 3.9 %collective-permute-start.7 = (bf16[256,1024]{1,0:T(8,128)(2,1)S(1)}, bf16[256,1024]{1,0:T(8,128)(2,1)S(1)}, u32[]{:S(2)}, u32[]{:S(2)}) collective-permute-start(bf16[256,1024]{1,0:T(8,128)(2,1)S(1)} %collective-permute-done.6.own), channel_id=1, source_target_pairs={{0,4},{2,6},{4,8},{6,10},{8,12},{10,14},{12,16},{14,18},{16,20},{1... | collective-permute-start | bytes 1572872 | tf_op jit(solution)/shard_map/ppermute | solution.py:319
  109.3 0.4 collective-permute-start.14
  109.7 29.8 %collective-permute-done.3.aux_in = bf16[1024,256]{1,0:T(8,128)(2,1)S(1)} collective-permute-done((bf16[1024,256]{1,0:T(8,128)(2,1)S(1)}, bf16[1024,256]{1,0:T(8,128)(2,1)S(1)}, u32[]{:S(2)}, u32[]{:S(2)}) %collective-permute-start.3) | collective-permute-done | bytes 524320 | tf_op jit(solution)/shard_map/ppermute | solution.py:283
  139.5 0.6 collective-permute-start.4
  140.1 0.0 collective-permute-start.1
  140.1 1.9 collective-permute-start.8
  142.0 36.8 %collective-permute-done.14.w_mine = bf16[512,512]{1,0:T(8,128)(2,1)S(1)} collective-permute-done((bf16[512,512]{1,0:T(8,128)(2,1)S(1)}, bf16[512,512]{1,0:T(8,128)(2,1)S(1)}, u32[]{:S(2)}, u32[]{:S(2)}) %collective-permute-start.14) | collective-permute-done | bytes 524320 | tf_op jit(solution)/shard_map/ppermute | solution.py:284
  178.8 0.5 collective-permute-start.10
  179.3 0.0 collective-permute-done.4.aux_pair
  179.3 0.0 collective-permute-start.11
  179.3 0.5 collective-permute-start.15
  179.8 0.3 weights.1
  180.1 0.7 queries.1.q_ref.refs_0_
  180.8 0.3 collective-permute-start.12
  181.1 4.4 %near.4 = (bf16[512,512]{1,0:T(8,128)(2,1)S(1)}, f32[6144,256]{1,0:T(8,128)S(1)}, f32[2,256,128]{2,1,0:T(8,128)S(1)}, f32[2,256,128]{2,1,0:T(8,128)S(1)}) custom-call(bf16[256,1024]{1,0:T(8,128)(2,1)S(1)} %conv.1.own, bf16[256,1024]{1,0:T(8,128)(2,1)S(1)} %collective-permute-done.1.other, bf16[1024,512]{1,0:T(8,128)(2,1)S(1)} %get-tuple-element.42.wk.refs_3_, ...), custom_call_target="tpu_custom_call" | custom-call | flops 2000000000 | bytes 4194304 | tf_op jit(solution)/shard_map/near/pallas_call | solution.py:350
  185.5 0.6 collective-permute-start.9
  186.1 4.9 %near.5 = (bf16[512,512]{1,0:T(8,128)(2,1)S(1)}, f32[8192,256]{1,0:T(8,128)S(1)}, f32[2,256,128]{2,1,0:T(8,128)S(1)}, f32[2,256,128]{2,1,0:T(8,128)S(1)}) custom-call(bf16[256,1024]{1,0:T(8,128)(2,1)S(1)} %collective-permute-done.5.own, bf16[256,1024]{1,0:T(8,128)(2,1)S(1)} %collective-permute-done.10.other, ...), custom_call_target="tpu_custom_call" | custom-call | flops 2000000000 | bytes 4194304 | tf_op jit(solution)/shard_map/near/pallas_call | solution.py:350
  191.1 5.0 %near.6 = (bf16[512,512]{1,0:T(8,128)(2,1)S(1)}, f32[8192,256]{1,0:T(8,128)S(1)}, f32[2,256,128]{2,1,0:T(8,128)S(1)}, f32[2,256,128]{2,1,0:T(8,128)S(1)}) custom-call(bf16[256,1024]{1,0:T(8,128)(2,1)S(1)} %collective-permute-done.6.own, bf16[256,1024]{1,0:T(8,128)(2,1)S(1)} %collective-permute-done.11.other, ...), custom_call_target="tpu_custom_call" | custom-call | flops 2000000000 | bytes 4194304 | tf_op jit(solution)/shard_map/near/pallas_call | solution.py:350
  196.1 5.0 %near.7 = (bf16[512,512]{1,0:T(8,128)(2,1)S(1)}, f32[8192,256]{1,0:T(8,128)S(1)}, f32[2,256,128]{2,1,0:T(8,128)S(1)}, f32[2,256,128]{2,1,0:T(8,128)S(1)}) custom-call(bf16[256,1024]{1,0:T(8,128)(2,1)S(1)} %collective-permute-done.7.own, bf16[256,1024]{1,0:T(8,128)(2,1)S(1)} %collective-permute-done.12.other, ...), custom_call_target="tpu_custom_call" | custom-call | flops 2000000000 | bytes 4194304 | tf_op jit(solution)/shard_map/near/pallas_call | solution.py:350
  201.0 0.0 copy-start
  201.0 0.0 copy-start.4
  201.1 11.1 %attend.1 = (f32[256,512]{1,0:T(8,128)S(1)}, f32[256,512]{1,0:T(8,128)S(1)}) custom-call(bf16[512,512]{1,0:T(8,128)(2,1)S(1)} %queries.1.q_ref.refs_0_, bf16[256,1024]{1,0:T(8,128)(2,1)S(1)} %collective-permute-done.8.refs_1_, bf16[256,1024]{1,0:T(8,128)(2,1)S(1)} %collective-permute-done.9.refs_2_, bf16[1024,512]{1,0:T(8,128)(2,1)S(1)} %get-tuple-element.42.wk.refs_3_, ...), custom_call_target="tpu_custom_call" | custom-call | flops 5000000000 | bytes 6291456 | tf_op jit(solution)/shard_map/attend/pallas_call | solution.py:366
  212.2 0.3 collective-permute-start.13
  212.5 1.7 collective-permute-done.13.received
  214.2 1.6 project.1
  (18 shorter events, 0.0 us)
Async XLA Ops:
  0.0 0.7 copy-start.5
  0.7 0.7 copy-start.6
  27.5 45.0 %copy-start.1 = (bf16[1,256,1024]{2,1,0:T(8,128)(2,1)S(1)}, bf16[1,256,1024]{2,1,0:T(8,128)(2,1)}, u32[]{:S(2)}) copy-start(bf16[1,256,1024]{2,1,0:T(8,128)(2,1)} %param.9) | copy-start | bytes 1572868
  27.5 45.0 %copy-start.3 = (f32[1024]{0:T(1024)S(1)}, f32[1024]{0:T(1024)}, u32[]{:S(2)}) copy-start(f32[1024]{0:T(1024)} %param.13) | copy-start | bytes 12292
  33.0 43.2 %copy-start.2 = (bf16[7,1024]{1,0:T(8,128)(2,1)S(1)}, bf16[7,1024]{1,0:T(8,128)(2,1)}, u32[]{:S(2)}) copy-start(bf16[7,1024]{1,0:T(8,128)(2,1)} %taps.1) | copy-start | bytes 43012
  73.1 3.1 %collective-permute-start = (bf16[8,1024]{1,0:T(8,128)(2,1)S(1)}, bf16[8,1024]{1,0:T(8,128)(2,1)S(1)}, u32[]{:S(2)}, u32[]{:S(2)}) collective-permute-start(bf16[8,1024]{1,0:T(8,128)(2,1)S(1)} %get-tuple-element.37), channel_id=1, source_target_pairs={{0,2},{2,4},{4,6},{6,8},{8,10},{10,12},{12,14},{14,16},{16,18},{18... | collective-permute-start | bytes 49160 | tf_op jit(solution)/shard_map/ppermute | solution.py:307
  77.3 14.5 %collective-permute-start.5 = (bf16[256,1024]{1,0:T(8,128)(2,1)S(1)}, bf16[256,1024]{1,0:T(8,128)(2,1)S(1)}, u32[]{:S(2)}, u32[]{:S(2)}) collective-permute-start(bf16[256,1024]{1,0:T(8,128)(2,1)S(1)} %conv.1.own), channel_id=1, source_target_pairs={{0,4},{2,6},{4,8},{6,10},{8,12},{10,14},{12,16},{14,18},{16,20},{1... | collective-permute-start | bytes 1572872 | tf_op jit(solution)/shard_map/ppermute | solution.py:319
  91.8 13.7 %collective-permute-start.6 = (bf16[256,1024]{1,0:T(8,128)(2,1)S(1)}, bf16[256,1024]{1,0:T(8,128)(2,1)S(1)}, u32[]{:S(2)}, u32[]{:S(2)}) collective-permute-start(bf16[256,1024]{1,0:T(8,128)(2,1)S(1)} %collective-permute-done.5.own), channel_id=1, source_target_pairs={{0,4},{2,6},{4,8},{6,10},{8,12},{10,14},{12,16},{14,18},{16,20},{1... | collective-permute-start | bytes 1572872 | tf_op jit(solution)/shard_map/ppermute | solution.py:319
  97.6 41.9 %collective-permute-start.3 = (bf16[1024,256]{1,0:T(8,128)(2,1)S(1)}, bf16[1024,256]{1,0:T(8,128)(2,1)S(1)}, u32[]{:S(2)}, u32[]{:S(2)}) collective-permute-start(bf16[1024,256]{1,0:T(8,128)(2,1)S(1)} %get-tuple-element.40), channel_id=1, source_target_pairs={{0,1},{1,0},{2,3},{3,2},{4,5},{5,4},{6,7},{7,6},{8,9},{9,8},{10,11... | collective-permute-start | bytes 1572872 | tf_op jit(solution)/shard_map/ppermute | solution.py:283
  98.0 81.4 %collective-permute-start.2 = (bf16[1024,512]{1,0:T(8,128)(2,1)S(1)}, bf16[1024,512]{1,0:T(8,128)(2,1)S(1)}, u32[]{:S(2)}, u32[]{:S(2)}) collective-permute-start(bf16[1024,512]{1,0:T(8,128)(2,1)S(1)} %get-tuple-element.39.main), channel_id=1, source_target_pairs={{0,1},{1,0},{2,3},{3,2},{4,5},{5,4},{6,7},{7,6},{8,9},{9,8},{10,11... | collective-permute-start | bytes 3145736 | tf_op jit(solution)/shard_map/ppermute | solution.py:282
  105.4 34.6 %collective-permute-start.7 = (bf16[256,1024]{1,0:T(8,128)(2,1)S(1)}, bf16[256,1024]{1,0:T(8,128)(2,1)S(1)}, u32[]{:S(2)}, u32[]{:S(2)}) collective-permute-start(bf16[256,1024]{1,0:T(8,128)(2,1)S(1)} %collective-permute-done.6.own), channel_id=1, source_target_pairs={{0,4},{2,6},{4,8},{6,10},{8,12},{10,14},{12,16},{14,18},{16,20},{1... | collective-permute-start | bytes 1572872 | tf_op jit(solution)/shard_map/ppermute | solution.py:319
  109.3 69.5 %collective-permute-start.14 = (bf16[512,512]{1,0:T(8,128)(2,1)S(1)}, bf16[512,512]{1,0:T(8,128)(2,1)S(1)}, u32[]{:S(2)}, u32[]{:S(2)}) collective-permute-start(bf16[512,512]{1,0:T(8,128)(2,1)S(1)} %get-tuple-element.62), channel_id=1, source_target_pairs={{0,1},{1,0},{2,3},{3,2},{4,5},{5,4},{6,7},{7,6},{8,9},{9,8},{10,11... | collective-permute-start | bytes 1572872 | tf_op jit(solution)/shard_map/ppermute | solution.py:284
  139.5 39.8 %collective-permute-start.4 = (bf16[1024,256]{1,0:T(8,128)(2,1)S(1)}, bf16[1024,256]{1,0:T(8,128)(2,1)S(1)}, u32[]{:S(2)}, u32[]{:S(2)}) collective-permute-start(bf16[1024,256]{1,0:T(8,128)(2,1)S(1)} %collective-permute-done.3.aux_in), channel_id=1, source_target_pairs={{0,2},{2,0},{4,6},{6,4},{8,10},{10,8},{12,14},{14,12},{16,18},{18,... | collective-permute-start | bytes 1572872 | tf_op jit(solution)/shard_map/ppermute | solution.py:285
  140.1 40.0 %collective-permute-start.1 = (bf16[256,1024]{1,0:T(8,128)(2,1)S(1)}, bf16[256,1024]{1,0:T(8,128)(2,1)S(1)}, u32[]{:S(2)}, u32[]{:S(2)}) collective-permute-start(bf16[256,1024]{1,0:T(8,128)(2,1)S(1)} %conv.1.own), channel_id=1, source_target_pairs={{0,2},{2,0},{4,6},{6,4},{8,10},{10,8},{12,14},{14,12},{16,18},{18,... | collective-permute-start | bytes 1572872 | tf_op jit(solution)/shard_map/ppermute | solution.py:322
  140.1 45.4 %collective-permute-start.8 = (bf16[256,1024]{1,0:T(8,128)(2,1)S(1)}, bf16[256,1024]{1,0:T(8,128)(2,1)S(1)}, u32[]{:S(2)}, u32[]{:S(2)}) collective-permute-start(bf16[256,1024]{1,0:T(8,128)(2,1)S(1)} %collective-permute-done.7.own), channel_id=1, source_target_pairs={{0,4},{2,6},{4,8},{6,10},{8,12},{10,14},{12,16},{14,18},{16,20},{1... | collective-permute-start | bytes 1572872 | tf_op jit(solution)/shard_map/ppermute | solution.py:319
  178.8 7.3 %collective-permute-start.10 = (bf16[256,1024]{1,0:T(8,128)(2,1)S(1)}, bf16[256,1024]{1,0:T(8,128)(2,1)S(1)}, u32[]{:S(2)}, u32[]{:S(2)}) collective-permute-start(bf16[256,1024]{1,0:T(8,128)(2,1)S(1)} %collective-permute-done.5.own), channel_id=1, source_target_pairs={{0,2},{2,0},{4,6},{6,4},{8,10},{10,8},{12,14},{14,12},{16,18},{18,... | collective-permute-start | bytes 1572872 | tf_op jit(solution)/shard_map/ppermute | solution.py:322
  179.3 11.8 %collective-permute-start.11 = (bf16[256,1024]{1,0:T(8,128)(2,1)S(1)}, bf16[256,1024]{1,0:T(8,128)(2,1)S(1)}, u32[]{:S(2)}, u32[]{:S(2)}) collective-permute-start(bf16[256,1024]{1,0:T(8,128)(2,1)S(1)} %collective-permute-done.6.own), channel_id=1, source_target_pairs={{0,2},{2,0},{4,6},{6,4},{8,10},{10,8},{12,14},{14,12},{16,18},{18,... | collective-permute-start | bytes 1572872 | tf_op jit(solution)/shard_map/ppermute | solution.py:322
  179.3 33.1 %collective-permute-start.15 = (bf16[512,512]{1,0:T(8,128)(2,1)S(1)}, bf16[512,512]{1,0:T(8,128)(2,1)S(1)}, u32[]{:S(2)}, u32[]{:S(2)}) collective-permute-start(bf16[512,512]{1,0:T(8,128)(2,1)S(1)} %collective-permute-done.14.w_mine), channel_id=1, source_target_pairs={{0,2},{2,0},{4,6},{6,4},{8,10},{10,8},{12,14},{14,12},{16,18},{18,... | collective-permute-start | bytes 1572872 | tf_op jit(solution)/shard_map/ppermute | solution.py:286
  180.8 15.2 %collective-permute-start.12 = (bf16[256,1024]{1,0:T(8,128)(2,1)S(1)}, bf16[256,1024]{1,0:T(8,128)(2,1)S(1)}, u32[]{:S(2)}, u32[]{:S(2)}) collective-permute-start(bf16[256,1024]{1,0:T(8,128)(2,1)S(1)} %collective-permute-done.7.own), channel_id=1, source_target_pairs={{0,2},{2,0},{4,6},{6,4},{8,10},{10,8},{12,14},{14,12},{16,18},{18,... | collective-permute-start | bytes 1572872 | tf_op jit(solution)/shard_map/ppermute | solution.py:322
  185.5 15.5 %collective-permute-start.9 = (bf16[256,1024]{1,0:T(8,128)(2,1)S(1)}, bf16[256,1024]{1,0:T(8,128)(2,1)S(1)}, u32[]{:S(2)}, u32[]{:S(2)}) collective-permute-start(bf16[256,1024]{1,0:T(8,128)(2,1)S(1)} %collective-permute-done.8.refs_1_), channel_id=1, source_target_pairs={{0,2},{2,0},{4,6},{6,4},{8,10},{10,8},{12,14},{14,12},{16,18},{18,... | collective-permute-start | bytes 1572872 | tf_op jit(solution)/shard_map/ppermute | solution.py:322
  201.0 13.1 %copy-start = (bf16[1024,512]{1,0:T(8,128)(2,1)S(1)}, bf16[1024,512]{1,0:T(8,128)(2,1)}, u32[]{:S(2)}) copy-start(bf16[1024,512]{1,0:T(8,128)(2,1)} %w_here.1) | copy-start | bytes 3145732
  201.0 13.1 %copy-start.4 = (f32[1024]{0:T(1024)S(1)}, f32[1024]{0:T(1024)}, u32[]{:S(2)}) copy-start(f32[1024]{0:T(1024)} %param.17) | copy-start | bytes 12292
  212.2 2.0 collective-permute-start.13

commit v4 on v3

--- a/solution.py
+++ b/solution.py
@@ -96,10 +96,13 @@
     slot[...] = ocol * SLOTS + rank_col
 
 
-def norm_kernel(fetched, slot, dna, gain, normed, rim):
+def norm_kernel(fetched, slot, dna, gain, normed, rim, staged, sem):
+    copy = pltpu.make_async_copy(dna, staged, sem)
+    copy.start()
     pick = (lax.broadcasted_iota(jnp.int32, (ROWS, OWNERS * SLOTS), 1) == slot[...]).astype(f32).astype(bf16)
     site = jnp.dot(pick, fetched[...], preferred_element_type=f32)
-    resid = dna[...].astype(f32) + site
+    copy.wait()
+    resid = staged[...].astype(f32) + site
     mean = jnp.mean(resid * resid, axis=1, keepdims=True)
     out = (resid * lax.rsqrt(mean + EPSILON) * gain[...]).astype(bf16)
     normed[...] = out
@@ -138,7 +141,7 @@
     return ((0, 0, 0), (0, 1, 0), (1, 0, 0), (1, 1, 0))
 
 
-def score_block(k, own, other, wk, wv, q_ref, v_ref, e_ref, top_ref, sum_ref, k_ref):
+def score_block(k, own, other, wk, wv, q_ref, v_ref, e_ref, top_ref, sum_ref, k_ref, sc0, sc1):
     par = lax.rem(lax.axis_index("seq"), 2)
     for x, side in ((own, par), (other, 1 - par)):
         at = pl.ds(pl.multiple_of(side * ROWS, ROWS), ROWS)
@@ -152,49 +155,49 @@
     top_ref[...] = jnp.zeros((2, ROWS, 128), f32)
     sum_ref[...] = jnp.zeros((2, ROWS, 128), f32)
 
-    def at_block(h, i):
-        return pl.ds(pl.multiple_of((h * count + i) * ROWS, ROWS), ROWS)
-
-    def pair(hp, carry):
+    def scores(hp, side, sc):
         lanes = pl.ds(pl.multiple_of(hp * 128, 128), 128)
-        tops = {}
-        for side in range(2):
-            h = 2 * hp + side
-            for i, (qb, half, edge) in enumerate(blocks):
-                q = q_ref[qb * ROWS : (qb + 1) * ROWS, lanes]
-                q = jnp.where((lane < HEAD) == (side == 0), q, jnp.zeros_like(q))
-                keys = k_ref[half * ROWS : (half + 1) * ROWS, lanes]
-                s = lax.dot_general(q, keys, (((1,), (1,)), ((), ())), preferred_element_type=f32)
-                if edge:
-                    s = jnp.where(col <= row if edge == 1 else col > row, s, MASKED)
-                e_ref[at_block(h, i), :] = s
-                part = jnp.maximum(s[:, :128], s[:, 128:])
-                known = tops.get((side, qb))
-                tops[side, qb] = part if known is None else jnp.maximum(known, part)
-        for side in range(2):
-            h = 2 * hp + side
-            for qb in range(2):
-                top = jnp.max(tops[side, qb], axis=1, keepdims=True)
-                total = None
-                for i, (which, half, edge) in enumerate(blocks):
-                    if which == qb:
-                        e = jnp.exp2((e_ref[at_block(h, i), :] - top) * SCALE)
-                        e_ref[at_block(h, i), :] = e
-                        part = e[:, :128] + e[:, 128:]
-                        total = part if total is None else total + part
-                total = jnp.sum(total, axis=1, keepdims=True)
-                top_ref[qb] = jnp.where(lane == h, top, top_ref[qb])
-                sum_ref[qb] = jnp.where(lane == h, total, sum_ref[qb])
-        return carry
-
-    lax.fori_loop(0, 4, pair, 0)
+        tops = [None, None]
+        for i, (qb, half, edge) in enumerate(blocks):
+            q = q_ref[qb * ROWS : (qb + 1) * ROWS, lanes]
+            q = jnp.where((lane < HEAD) == (side == 0), q, jnp.zeros_like(q))
+            keys = k_ref[half * ROWS : (half + 1) * ROWS, lanes]
+            s = lax.dot_general(q, keys, (((1,), (1,)), ((), ())), preferred_element_type=f32)
+            if edge:
+                s = jnp.where(col <= row if edge == 1 else col > row, s, MASKED)
+            sc[i] = s
+            part = jnp.maximum(s[:, :128], s[:, 128:])
+            tops[qb] = part if tops[qb] is None else jnp.maximum(tops[qb], part)
+        return tuple(jnp.max(top, axis=1, keepdims=True) for top in tops)
+
+    def weigh(h, sc, tops):
+        for qb in range(2):
+            total = None
+            for i, (which, half, edge) in enumerate(blocks):
+                if which == qb:
+                    e = jnp.exp2((sc[i] - tops[qb]) * SCALE)
+                    e_ref[pl.ds(pl.multiple_of((h * count + i) * ROWS, ROWS), ROWS), :] = e
+                    part = e[:, :128] + e[:, 128:]
+                    total = part if total is None else total + part
+            total = jnp.sum(total, axis=1, keepdims=True)
+            top_ref[qb] = jnp.where(lane == h, tops[qb], top_ref[qb])
+            sum_ref[qb] = jnp.where(lane == h, total, sum_ref[qb])
+
+    def pair(hp, even):
+        odd = scores(hp, 1, sc1)
+        weigh(2 * hp, sc0, even)
+        after_it = scores(jnp.minimum(hp + 1, 3), 0, sc0)
+        weigh(2 * hp + 1, sc1, odd)
+        return after_it
+
+    lax.fori_loop(0, 4, pair, scores(0, 0, sc0))
 
 
 def attend_kernel(*refs):
     q_ref, own, other, wk, wv = refs[:5]
     values, es, tops, sums = (refs[5 + HOPS * i : 5 + HOPS * (i + 1)] for i in range(4))
-    mine, theirs, v_last, e_last, top_last, sum_last, k_last, factor, done = refs[5 + 4 * HOPS :]
-    score_block(HOPS, own, other, wk, wv, q_ref, v_last, e_last, top_last, sum_last, k_last)
+    mine, theirs, v_last, e_last, top_last, sum_last, k_last, sc0, sc1, factor, done = refs[5 + 4 * HOPS :]
+    score_block(HOPS, own, other, wk, wv, q_ref, v_last, e_last, top_last, sum_last, k_last, sc0, sc1)
     values, es = values + (v_last,), es + (e_last,)
     tops, sums = tops + (top_last,), sums + (sum_last,)
     seq = lax.axis_index("seq")
@@ -262,6 +265,7 @@
 def local(dna_embed, site_owner, site_row, variant_table, norm_gain, conv_weight, qkv_weight, out_weight, attn_gain):
     count = lax.axis_size("seq")
     across = [(0, 1), (1, 0)]
+    beyond = [(i, i ^ (count + 1)) for i in range(2 * count)]
     swap = [(i, i ^ 1) for i in range(count)]
     ahead = [(i, i + 2) for i in range(count - 2)]
 
@@ -274,14 +278,14 @@
             jax.ShapeDtypeStruct((D, HALF), bf16),
         ),
         in_specs=[anywhere()] * 2,
-        out_specs=(vmem(), vmem(), vmem(), vmem()),
+        out_specs=(vmem(),) * 4,
         scratch_shapes=[pltpu.SemaphoreType.DMA((4,))],
         compiler_params=limit(6),
         name="slabs",
     )(*(pltpu.with_memory_space_constraint(w, pltpu.HBM) for w in (qkv_weight, out_weight)))
     main_in = lax.ppermute(main, "fsdp", across)
-    aux_in = lax.ppermute(aux, "fsdp", across)
-    out_in = lax.ppermute(half, "fsdp", across)
+    aux_in = lax.ppermute(aux, ("seq", "fsdp"), beyond)
+    out_in = lax.ppermute(half, ("seq", "fsdp"), beyond)
     aux_pair = lax.ppermute(aux_in, "seq", swap)
     out_pair = lax.ppermute(out_in, "seq", swap)
 
@@ -299,11 +303,12 @@
     normed, edge = pl.pallas_call(
         norm_kernel,
         out_shape=(jax.ShapeDtypeStruct((ROWS, D), bf16), jax.ShapeDtypeStruct((8, D), bf16)),
-        in_specs=[vmem()] * 4,
+        in_specs=[vmem(), vmem(), anywhere(), vmem()],
         out_specs=(vmem(), vmem()),
+        scratch_shapes=[pltpu.VMEM((ROWS, D), bf16), pltpu.SemaphoreType.DMA],
         compiler_params=limit(10),
     name="norm",
-    )(fetched, slot, dna_embed[0], norm_gain.reshape(1, D))
+    )(fetched, slot, pltpu.with_memory_space_constraint(dna_embed[0], pltpu.HBM), norm_gain.reshape(1, D))
     rim = lax.ppermute(edge, "seq", [(i, i + 1) for i in range(count - 1)])
     x = pl.pallas_call(
         conv_kernel,
@@ -357,8 +362,8 @@
                 ),
                 in_specs=[vmem()] * 5,
                 out_specs=(vmem(),) * 4,
-                scratch_shapes=[pltpu.VMEM((2 * ROWS, HALF), bf16)],
-                compiler_params=limit(4),
+                scratch_shapes=[pltpu.VMEM((2 * ROWS, HALF), bf16)] + [pltpu.VMEM((4, ROWS, ROWS), f32)] * 2,
+                compiler_params=limit(5),
                 cost_estimate=cost(2 * 10**9, 4 * 2**20),
                 name="near",
             )(own[hop], other[hop], wk, wv, q)
@@ -374,10 +379,12 @@
             pltpu.VMEM((2, ROWS, 128), f32),
             pltpu.VMEM((2, ROWS, 128), f32),
             pltpu.VMEM((2 * ROWS, HALF), bf16),
+            pltpu.VMEM((4, ROWS, ROWS), f32),
+            pltpu.VMEM((4, ROWS, ROWS), f32),
             pltpu.VMEM((2, HOPS + 1, ROWS, 128), f32),
             pltpu.VMEM((2, ROWS, HALF), f32),
         ],
-        compiler_params=limit(14),
+        compiler_params=limit(15),
         cost_estimate=cost(5 * 10**9, 6 * 2**20),
         name="attend",
     )(q, own[HOPS], other[HOPS], wk, wv, *(found[k][i] for i in range(4) for k in range(HOPS)))

time: 216 us -> 191 us (0.88)
  waiting for transfers between devices: 86.4 us -> 50.4 us
  starting transfers between devices: 20.2 us -> 33.2 us
    ppermute x2, waiting for transfers between devices: 66.6 us -> 27.8 us  [the longest x1 15.6 us: local(): aux_in = lax.ppermute(aux, ('seq', 'fsdp'), beyond)]
    ppermute x1, starting transfers between devices: 0.59 us -> 14 us  [local(): aux_pair = lax.ppermute(aux_in, 'seq', swap)]
    pallas_call x4, Pallas kernels: 19.2 us -> 16.8 us  [local(): pl.pallas_call(functools.partial(score_block, hop), out_shape=(jax.ShapeD...]
  transfers between devices with their start and end apart: 16 -> 16, of which waited for: 6 -> 7; matrix products, arithmetic and copies ran while one was open for 0% -> 0% of each run, Pallas kernels for 15% -> 16%
where the time goes in v4:
time: 191 us
  blocking collectives  63.3 us (33%)
  waiting for transfers between devices  50.4 us (26%)
  Pallas kernels  35 us (18%)
  starting transfers between devices  33.2 us (17%)
  local copies, waits for them, and re-layouts  8.71 us (5%)
    all_to_all x1, blocking collectives, local(): lax.all_to_all(found, 'seq', split_axis=0, concat_axis=0, tiled=True)  37.7 us
    all_to_all x1, blocking collectives, local(): lax.all_to_all(table, 'seq', split_axis=0, concat_axis=0, tiled=True)  25.6 us
    ppermute x4, waiting for transfers between devices, local(): own.append(lax.ppermute(own[-1], 'seq', ahead))  18.1 us
    pallas_call x4, Pallas kernels, local(): pl.pallas_call(functools.partial(score_block, hop), out_shape=(jax.ShapeD...  16.8 us
    ppermute x1, waiting for transfers between devices, local(): aux_in = lax.ppermute(aux, ('seq', 'fsdp'), beyond)  15.6 us
    ppermute x1, starting transfers between devices, local(): aux_pair = lax.ppermute(aux_in, 'seq', swap)  14 us
    ppermute x4, starting transfers between devices, local(): own.append(lax.ppermute(own[-1], 'seq', ahead))  13.4 us
    ppermute x1, waiting for transfers between devices, local(): out_in = lax.ppermute(half, ('seq', 'fsdp'), beyond)  12.2 us
  transfers between devices with their start and end apart: 16, of which 7 were waited for; matrix products, arithmetic and copies ran while one was open for 0% of the time, Pallas kernels for 16%

profile of v4, /device:TPU:25, one launch (start us, length us, event | category | flops | bytes accessed | tf_op | source)
XLA Modules:
  0.0 190.8 jit_solution(1315639983135101075)
XLA Ops:
  0.0 0.7 copy-done.4
  0.7 0.7 copy-done.5
  1.4 0.4 requests.1
  1.8 25.6 %all_to_all.23 = s32[128,1,128]{2,1,0:T(1,128)S(1)} all-to-all(s32[128,1,128]{2,1,0:T(1,128)S(1)} %bitcast.11), channel_id=1, replica_groups=mesh['seq'=128,'fsdp'=2] {'seq'}, dimensions={0} | all-to-all | bytes 131072 | tf_op jit(solution)/shard_map/all_to_all | solution.py:300
  27.4 0.1 reshape.45
  27.5 0.0 copy-start.2
  27.5 5.5 %gather_fusion = bf16[512,1024]{1,0:T(8,128)(2,1)S(1)} fusion(bf16[2048,1024]{1,0:T(8,128)(2,1)} %param.12, s32[1024]{0:T(1024)S(1)} %pad_clamp_fusion), kind=kCustom, calls=%fused_computation | custom fusion | bytes 2099200 | tf_op jit(solution)/shard_map/gather | solution.py:301
  33.0 0.0 copy-start.1
  33.0 0.4 all_to_all.18
  33.4 37.7 %all_to_all.24 = bf16[128,4,1024]{2,1,0:T(4,128)(2,1)} all-to-all(bf16[128,4,1024]{2,1,0:T(4,128)(2,1)S(1)} %all_to_all.18), channel_id=1, replica_groups=mesh['seq'=128,'fsdp'=2] {'seq'}, dimensions={0} | all-to-all | bytes 2097152 | tf_op jit(solution)/shard_map/all_to_all | solution.py:302
  71.1 1.3 all_to_all.20.fetched
  72.4 1.6 norm.1
  74.0 2.0 %collective-permute-start = (bf16[8,1024]{1,0:T(8,128)(2,1)S(1)}, bf16[8,1024]{1,0:T(8,128)(2,1)S(1)}, u32[]{:S(2)}, u32[]{:S(2)}) collective-permute-start(bf16[8,1024]{1,0:T(8,128)(2,1)S(1)} %get-tuple-element.37), channel_id=1, source_target_pairs={{0,2},{2,4},{4,6},{6,8},{8,10},{10,12},{12,14},{14,16},{16,18},{18... | collective-permute-start | bytes 49160 | tf_op jit(solution)/shard_map/ppermute | solution.py:312
  76.0 1.1 collective-permute-done.rim
  77.1 1.0 conv.1.own
  78.1 3.8 %collective-permute-start.5 = (bf16[256,1024]{1,0:T(8,128)(2,1)S(1)}, bf16[256,1024]{1,0:T(8,128)(2,1)S(1)}, u32[]{:S(2)}, u32[]{:S(2)}) collective-permute-start(bf16[256,1024]{1,0:T(8,128)(2,1)S(1)} %conv.1.own), channel_id=1, source_target_pairs={{0,4},{2,6},{4,8},{6,10},{8,12},{10,14},{12,16},{14,18},{16,20},{1... | collective-permute-start | bytes 1572872 | tf_op jit(solution)/shard_map/ppermute | solution.py:324
  81.9 10.7 %collective-permute-done.5.own = bf16[256,1024]{1,0:T(8,128)(2,1)S(1)} collective-permute-done((bf16[256,1024]{1,0:T(8,128)(2,1)S(1)}, bf16[256,1024]{1,0:T(8,128)(2,1)S(1)}, u32[]{:S(2)}, u32[]{:S(2)}) %collective-permute-start.5) | collective-permute-done | bytes 524320 | tf_op jit(solution)/shard_map/ppermute | solution.py:324
  92.7 3.8 %collective-permute-start.6 = (bf16[256,1024]{1,0:T(8,128)(2,1)S(1)}, bf16[256,1024]{1,0:T(8,128)(2,1)S(1)}, u32[]{:S(2)}, u32[]{:S(2)}) collective-permute-start(bf16[256,1024]{1,0:T(8,128)(2,1)S(1)} %collective-permute-done.5.own), channel_id=1, source_target_pairs={{0,4},{2,6},{4,8},{6,10},{8,12},{10,14},{12,16},{14,18},{16,20},{1... | collective-permute-start | bytes 1572872 | tf_op jit(solution)/shard_map/ppermute | solution.py:324
  96.5 1.9 %slabs.1 = (bf16[1024,512]{1,0:T(8,128)(2,1)S(1)}, bf16[1024,256]{1,0:T(8,128)(2,1)S(1)}, bf16[512,512]{1,0:T(8,128)(2,1)S(1)}, bf16[1024,512]{1,0:T(8,128)(2,1)S(1)}) custom-call(bf16[1024,1536]{1,0:T(8,128)(2,1)} %qkv.1, bf16[1024,512]{1,0:T(8,128)(2,1)} %w_here.1), custom_call_target="tpu_custom_call" | custom-call | tf_op jit(solution)/shard_map/slabs/pallas_call | solution.py:272
  98.4 0.1 collective-permute-start.3
  98.5 0.4 collective-permute-start.2
  98.9 7.4 %collective-permute-done.6.own = bf16[256,1024]{1,0:T(8,128)(2,1)S(1)} collective-permute-done((bf16[256,1024]{1,0:T(8,128)(2,1)S(1)}, bf16[256,1024]{1,0:T(8,128)(2,1)S(1)}, u32[]{:S(2)}, u32[]{:S(2)}) %collective-permute-start.6) | collective-permute-done | bytes 524320 | tf_op jit(solution)/shard_map/ppermute | solution.py:324
  106.3 3.9 %collective-permute-start.7 = (bf16[256,1024]{1,0:T(8,128)(2,1)S(1)}, bf16[256,1024]{1,0:T(8,128)(2,1)S(1)}, u32[]{:S(2)}, u32[]{:S(2)}) collective-permute-start(bf16[256,1024]{1,0:T(8,128)(2,1)S(1)} %collective-permute-done.6.own), channel_id=1, source_target_pairs={{0,4},{2,6},{4,8},{6,10},{8,12},{10,14},{12,16},{14,18},{16,20},{1... | collective-permute-start | bytes 1572872 | tf_op jit(solution)/shard_map/ppermute | solution.py:324
  110.2 0.1 collective-permute-start.14
  110.3 15.6 %collective-permute-done.3.aux_in = bf16[1024,256]{1,0:T(8,128)(2,1)S(1)} collective-permute-done((bf16[1024,256]{1,0:T(8,128)(2,1)S(1)}, bf16[1024,256]{1,0:T(8,128)(2,1)S(1)}, u32[]{:S(2)}, u32[]{:S(2)}) %collective-permute-start.3) | collective-permute-done | bytes 524320 | tf_op jit(solution)/shard_map/ppermute | solution.py:287
  125.9 14.0 %collective-permute-start.4 = (bf16[1024,256]{1,0:T(8,128)(2,1)S(1)}, bf16[1024,256]{1,0:T(8,128)(2,1)S(1)}, u32[]{:S(2)}, u32[]{:S(2)}) collective-permute-start(bf16[1024,256]{1,0:T(8,128)(2,1)S(1)} %collective-permute-done.3.aux_in), channel_id=1, source_target_pairs={{0,2},{2,0},{4,6},{6,4},{8,10},{10,8},{12,14},{14,12},{16,18},{18,... | collective-permute-start | bytes 1572872 | tf_op jit(solution)/shard_map/ppermute | solution.py:289
  139.9 0.0 collective-permute-done.7.own
  139.9 1.9 %collective-permute-start.8 = (bf16[256,1024]{1,0:T(8,128)(2,1)S(1)}, bf16[256,1024]{1,0:T(8,128)(2,1)S(1)}, u32[]{:S(2)}, u32[]{:S(2)}) collective-permute-start(bf16[256,1024]{1,0:T(8,128)(2,1)S(1)} %collective-permute-done.7.own), channel_id=1, source_target_pairs={{0,4},{2,6},{4,8},{6,10},{8,12},{10,14},{12,16},{14,18},{16,20},{1... | collective-permute-start | bytes 1572872 | tf_op jit(solution)/shard_map/ppermute | solution.py:324
  141.9 12.2 %collective-permute-done.14.w_mine = bf16[512,512]{1,0:T(8,128)(2,1)S(1)} collective-permute-done((bf16[512,512]{1,0:T(8,128)(2,1)S(1)}, bf16[512,512]{1,0:T(8,128)(2,1)S(1)}, u32[]{:S(2)}, u32[]{:S(2)}) %collective-permute-start.14) | collective-permute-done | bytes 524320 | tf_op jit(solution)/shard_map/ppermute | solution.py:288
  154.0 1.6 collective-permute-start.10
  155.6 0.0 collective-permute-start.11
  155.6 1.6 collective-permute-done.2.main_in
  157.2 0.5 collective-permute-start.15
  157.7 0.3 weights.1
  158.0 0.0 collective-permute-done.1.other
  158.0 0.7 queries.1.q_ref.refs_0_
  158.7 0.1 collective-permute-start.12
  158.8 3.8 %near.4 = (bf16[512,512]{1,0:T(8,128)(2,1)S(1)}, f32[6144,256]{1,0:T(8,128)S(1)}, f32[2,256,128]{2,1,0:T(8,128)S(1)}, f32[2,256,128]{2,1,0:T(8,128)S(1)}) custom-call(bf16[256,1024]{1,0:T(8,128)(2,1)S(1)} %conv.1.own, bf16[256,1024]{1,0:T(8,128)(2,1)S(1)} %collective-permute-done.1.other, bf16[1024,512]{1,0:T(8,128)(2,1)S(1)} %get-tuple-element.42.wk.refs_3_, ...), custom_call_target="tpu_custom_call" | custom-call | flops 2000000000 | bytes 4194304 | tf_op jit(solution)/shard_map/near/pallas_call | solution.py:355
  162.7 0.8 collective-permute-start.9
  163.5 4.3 %near.5 = (bf16[512,512]{1,0:T(8,128)(2,1)S(1)}, f32[8192,256]{1,0:T(8,128)S(1)}, f32[2,256,128]{2,1,0:T(8,128)S(1)}, f32[2,256,128]{2,1,0:T(8,128)S(1)}) custom-call(bf16[256,1024]{1,0:T(8,128)(2,1)S(1)} %collective-permute-done.5.own, bf16[256,1024]{1,0:T(8,128)(2,1)S(1)} %collective-permute-done.10.other, ...), custom_call_target="tpu_custom_call" | custom-call | flops 2000000000 | bytes 4194304 | tf_op jit(solution)/shard_map/near/pallas_call | solution.py:355
  167.8 4.3 %near.6 = (bf16[512,512]{1,0:T(8,128)(2,1)S(1)}, f32[8192,256]{1,0:T(8,128)S(1)}, f32[2,256,128]{2,1,0:T(8,128)S(1)}, f32[2,256,128]{2,1,0:T(8,128)S(1)}) custom-call(bf16[256,1024]{1,0:T(8,128)(2,1)S(1)} %collective-permute-done.6.own, bf16[256,1024]{1,0:T(8,128)(2,1)S(1)} %collective-permute-done.11.other, ...), custom_call_target="tpu_custom_call" | custom-call | flops 2000000000 | bytes 4194304 | tf_op jit(solution)/shard_map/near/pallas_call | solution.py:355
  172.2 4.3 %near.7 = (bf16[512,512]{1,0:T(8,128)(2,1)S(1)}, f32[8192,256]{1,0:T(8,128)S(1)}, f32[2,256,128]{2,1,0:T(8,128)S(1)}, f32[2,256,128]{2,1,0:T(8,128)S(1)}) custom-call(bf16[256,1024]{1,0:T(8,128)(2,1)S(1)} %collective-permute-done.7.own, bf16[256,1024]{1,0:T(8,128)(2,1)S(1)} %collective-permute-done.12.other, ...), custom_call_target="tpu_custom_call" | custom-call | flops 2000000000 | bytes 4194304 | tf_op jit(solution)/shard_map/near/pallas_call | solution.py:355
  176.5 0.0 copy-start
  176.5 0.0 copy-start.3
  176.5 10.7 %attend.1 = (f32[256,512]{1,0:T(8,128)S(1)}, f32[256,512]{1,0:T(8,128)S(1)}) custom-call(bf16[512,512]{1,0:T(8,128)(2,1)S(1)} %queries.1.q_ref.refs_0_, bf16[256,1024]{1,0:T(8,128)(2,1)S(1)} %collective-permute-done.8.refs_1_, bf16[256,1024]{1,0:T(8,128)(2,1)S(1)} %collective-permute-done.9.refs_2_, bf16[1024,512]{1,0:T(8,128)(2,1)S(1)} %get-tuple-element.42.wk.refs_3_, ...), custom_call_target="tpu_custom_call" | custom-call | flops 5000000000 | bytes 6291456 | tf_op jit(solution)/shard_map/attend/pallas_call | solution.py:371
  187.3 0.1 collective-permute-start.13
  187.4 1.9 collective-permute-done.13.received
  189.3 1.6 project.1
  (16 shorter events, 0.0 us)
Async XLA Ops:
  0.0 0.7 copy-start.4
  0.7 0.7 copy-start.5
  27.5 44.9 %copy-start.2 = (f32[1024]{0:T(1024)S(1)}, f32[1024]{0:T(1024)}, u32[]{:S(2)}) copy-start(f32[1024]{0:T(1024)} %param.13) | copy-start | bytes 12292
  33.0 44.1 %copy-start.1 = (bf16[7,1024]{1,0:T(8,128)(2,1)S(1)}, bf16[7,1024]{1,0:T(8,128)(2,1)}, u32[]{:S(2)}) copy-start(bf16[7,1024]{1,0:T(8,128)(2,1)} %taps.1) | copy-start | bytes 43012
  74.0 3.1 %collective-permute-start = (bf16[8,1024]{1,0:T(8,128)(2,1)S(1)}, bf16[8,1024]{1,0:T(8,128)(2,1)S(1)}, u32[]{:S(2)}, u32[]{:S(2)}) collective-permute-start(bf16[8,1024]{1,0:T(8,128)(2,1)S(1)} %get-tuple-element.37), channel_id=1, source_target_pairs={{0,2},{2,4},{4,6},{6,8},{8,10},{10,12},{12,14},{14,16},{16,18},{18... | collective-permute-start | bytes 49160 | tf_op jit(solution)/shard_map/ppermute | solution.py:312
  78.1 14.5 %collective-permute-start.5 = (bf16[256,1024]{1,0:T(8,128)(2,1)S(1)}, bf16[256,1024]{1,0:T(8,128)(2,1)S(1)}, u32[]{:S(2)}, u32[]{:S(2)}) collective-permute-start(bf16[256,1024]{1,0:T(8,128)(2,1)S(1)} %conv.1.own), channel_id=1, source_target_pairs={{0,4},{2,6},{4,8},{6,10},{8,12},{10,14},{12,16},{14,18},{16,20},{1... | collective-permute-start | bytes 1572872 | tf_op jit(solution)/shard_map/ppermute | solution.py:324
  92.7 13.7 %collective-permute-start.6 = (bf16[256,1024]{1,0:T(8,128)(2,1)S(1)}, bf16[256,1024]{1,0:T(8,128)(2,1)S(1)}, u32[]{:S(2)}, u32[]{:S(2)}) collective-permute-start(bf16[256,1024]{1,0:T(8,128)(2,1)S(1)} %collective-permute-done.5.own), channel_id=1, source_target_pairs={{0,4},{2,6},{4,8},{6,10},{8,12},{10,14},{12,16},{14,18},{16,20},{1... | collective-permute-start | bytes 1572872 | tf_op jit(solution)/shard_map/ppermute | solution.py:324
  98.4 27.5 %collective-permute-start.3 = (bf16[1024,256]{1,0:T(8,128)(2,1)S(1)}, bf16[1024,256]{1,0:T(8,128)(2,1)S(1)}, u32[]{:S(2)}, u32[]{:S(2)}) collective-permute-start(bf16[1024,256]{1,0:T(8,128)(2,1)S(1)} %get-tuple-element.40), channel_id=1, source_target_pairs={{0,129},{1,128},{2,131},{3,130},{4,133},{5,132},{6,135},{7,134},{8... | collective-permute-start | bytes 1572872 | tf_op jit(solution)/shard_map/ppermute | solution.py:287
  98.5 58.7 %collective-permute-start.2 = (bf16[1024,512]{1,0:T(8,128)(2,1)S(1)}, bf16[1024,512]{1,0:T(8,128)(2,1)S(1)}, u32[]{:S(2)}, u32[]{:S(2)}) collective-permute-start(bf16[1024,512]{1,0:T(8,128)(2,1)S(1)} %get-tuple-element.39.main), channel_id=1, source_target_pairs={{0,1},{1,0},{2,3},{3,2},{4,5},{5,4},{6,7},{7,6},{8,9},{9,8},{10,11... | collective-permute-start | bytes 3145736 | tf_op jit(solution)/shard_map/ppermute | solution.py:286
  106.3 33.6 %collective-permute-start.7 = (bf16[256,1024]{1,0:T(8,128)(2,1)S(1)}, bf16[256,1024]{1,0:T(8,128)(2,1)S(1)}, u32[]{:S(2)}, u32[]{:S(2)}) collective-permute-start(bf16[256,1024]{1,0:T(8,128)(2,1)S(1)} %collective-permute-done.6.own), channel_id=1, source_target_pairs={{0,4},{2,6},{4,8},{6,10},{8,12},{10,14},{12,16},{14,18},{16,20},{1... | collective-permute-start | bytes 1572872 | tf_op jit(solution)/shard_map/ppermute | solution.py:324
  110.2 43.8 %collective-permute-start.14 = (bf16[512,512]{1,0:T(8,128)(2,1)S(1)}, bf16[512,512]{1,0:T(8,128)(2,1)S(1)}, u32[]{:S(2)}, u32[]{:S(2)}) collective-permute-start(bf16[512,512]{1,0:T(8,128)(2,1)S(1)} %get-tuple-element.62), channel_id=1, source_target_pairs={{0,129},{1,128},{2,131},{3,130},{4,133},{5,132},{6,135},{7,134},{8... | collective-permute-start | bytes 1572872 | tf_op jit(solution)/shard_map/ppermute | solution.py:288
  125.9 29.7 %collective-permute-start.4 = (bf16[1024,256]{1,0:T(8,128)(2,1)S(1)}, bf16[1024,256]{1,0:T(8,128)(2,1)S(1)}, u32[]{:S(2)}, u32[]{:S(2)}) collective-permute-start(bf16[1024,256]{1,0:T(8,128)(2,1)S(1)} %collective-permute-done.3.aux_in), channel_id=1, source_target_pairs={{0,2},{2,0},{4,6},{6,4},{8,10},{10,8},{12,14},{14,12},{16,18},{18,... | collective-permute-start | bytes 1572872 | tf_op jit(solution)/shard_map/ppermute | solution.py:289
  139.9 18.1 %collective-permute-start.1 = (bf16[256,1024]{1,0:T(8,128)(2,1)S(1)}, bf16[256,1024]{1,0:T(8,128)(2,1)S(1)}, u32[]{:S(2)}, u32[]{:S(2)}) collective-permute-start(bf16[256,1024]{1,0:T(8,128)(2,1)S(1)} %conv.1.own), channel_id=1, source_target_pairs={{0,2},{2,0},{4,6},{6,4},{8,10},{10,8},{12,14},{14,12},{16,18},{18,... | collective-permute-start | bytes 1572872 | tf_op jit(solution)/shard_map/ppermute | solution.py:327
  139.9 22.7 %collective-permute-start.8 = (bf16[256,1024]{1,0:T(8,128)(2,1)S(1)}, bf16[256,1024]{1,0:T(8,128)(2,1)S(1)}, u32[]{:S(2)}, u32[]{:S(2)}) collective-permute-start(bf16[256,1024]{1,0:T(8,128)(2,1)S(1)} %collective-permute-done.7.own), channel_id=1, source_target_pairs={{0,4},{2,6},{4,8},{6,10},{8,12},{10,14},{12,16},{14,18},{16,20},{1... | collective-permute-start | bytes 1572872 | tf_op jit(solution)/shard_map/ppermute | solution.py:324
  154.0 9.5 %collective-permute-start.10 = (bf16[256,1024]{1,0:T(8,128)(2,1)S(1)}, bf16[256,1024]{1,0:T(8,128)(2,1)S(1)}, u32[]{:S(2)}, u32[]{:S(2)}) collective-permute-start(bf16[256,1024]{1,0:T(8,128)(2,1)S(1)} %collective-permute-done.5.own), channel_id=1, source_target_pairs={{0,2},{2,0},{4,6},{6,4},{8,10},{10,8},{12,14},{14,12},{16,18},{18,... | collective-permute-start | bytes 1572872 | tf_op jit(solution)/shard_map/ppermute | solution.py:327
  155.6 12.2 %collective-permute-start.11 = (bf16[256,1024]{1,0:T(8,128)(2,1)S(1)}, bf16[256,1024]{1,0:T(8,128)(2,1)S(1)}, u32[]{:S(2)}, u32[]{:S(2)}) collective-permute-start(bf16[256,1024]{1,0:T(8,128)(2,1)S(1)} %collective-permute-done.6.own), channel_id=1, source_target_pairs={{0,2},{2,0},{4,6},{6,4},{8,10},{10,8},{12,14},{14,12},{16,18},{18,... | collective-permute-start | bytes 1572872 | tf_op jit(solution)/shard_map/ppermute | solution.py:327
  157.2 30.2 %collective-permute-start.15 = (bf16[512,512]{1,0:T(8,128)(2,1)S(1)}, bf16[512,512]{1,0:T(8,128)(2,1)S(1)}, u32[]{:S(2)}, u32[]{:S(2)}) collective-permute-start(bf16[512,512]{1,0:T(8,128)(2,1)S(1)} %collective-permute-done.14.w_mine), channel_id=1, source_target_pairs={{0,2},{2,0},{4,6},{6,4},{8,10},{10,8},{12,14},{14,12},{16,18},{18,... | collective-permute-start | bytes 1572872 | tf_op jit(solution)/shard_map/ppermute | solution.py:290
  158.7 13.4 %collective-permute-start.12 = (bf16[256,1024]{1,0:T(8,128)(2,1)S(1)}, bf16[256,1024]{1,0:T(8,128)(2,1)S(1)}, u32[]{:S(2)}, u32[]{:S(2)}) collective-permute-start(bf16[256,1024]{1,0:T(8,128)(2,1)S(1)} %collective-permute-done.7.own), channel_id=1, source_target_pairs={{0,2},{2,0},{4,6},{6,4},{8,10},{10,8},{12,14},{14,12},{16,18},{18,... | collective-permute-start | bytes 1572872 | tf_op jit(solution)/shard_map/ppermute | solution.py:327
  162.7 13.8 %collective-permute-start.9 = (bf16[256,1024]{1,0:T(8,128)(2,1)S(1)}, bf16[256,1024]{1,0:T(8,128)(2,1)S(1)}, u32[]{:S(2)}, u32[]{:S(2)}) collective-permute-start(bf16[256,1024]{1,0:T(8,128)(2,1)S(1)} %collective-permute-done.8.refs_1_), channel_id=1, source_target_pairs={{0,2},{2,0},{4,6},{6,4},{8,10},{10,8},{12,14},{14,12},{16,18},{18,... | collective-permute-start | bytes 1572872 | tf_op jit(solution)/shard_map/ppermute | solution.py:327
  176.5 12.8 %copy-start = (bf16[1024,512]{1,0:T(8,128)(2,1)S(1)}, bf16[1024,512]{1,0:T(8,128)(2,1)}, u32[]{:S(2)}) copy-start(bf16[1024,512]{1,0:T(8,128)(2,1)} %w_here.1) | copy-start | bytes 3145732
  176.5 12.8 %copy-start.3 = (f32[1024]{0:T(1024)S(1)}, f32[1024]{0:T(1024)}, u32[]{:S(2)}) copy-start(f32[1024]{0:T(1024)} %param.17) | copy-start | bytes 12292
  187.3 2.0 %collective-permute-start.13 = (f32[256,512]{1,0:T(8,128)S(1)}, f32[256,512]{1,0:T(8,128)S(1)}, u32[]{:S(2)}, u32[]{:S(2)}) collective-permute-start(f32[256,512]{1,0:T(8,128)S(1)} %get-tuple-element.61), channel_id=1, source_target_pairs={{0,2},{2,0},{4,6},{6,4},{8,10},{10,8},{12,14},{14,12},{16,18},{18,... | collective-permute-start | bytes 1572872 | tf_op jit(solution)/shard_map/ppermute | solution.py:391

commit v5 on v4

--- a/solution.py
+++ b/solution.py
@@ -15,6 +15,7 @@
 OWNERS = 128
 SLOTS = 4
 HOPS = 4
+Z = 8
 LOG2E = 1.4426950408889634
 SCALE = LOG2E * HEAD ** (-0.5)
 MASKED = -1e30
@@ -78,8 +79,14 @@
         wv[...] = main[...]
 
 
-def request_kernel(owner, rows, table, slot):
-    orow = owner[...]
+def request_kernel(owner, rows_in, table, slot, owners, rows, sems):
+    first = pltpu.make_async_copy(owner, owners, sems.at[0])
+    second = pltpu.make_async_copy(rows_in, rows, sems.at[1])
+    first.start()
+    second.start()
+    first.wait()
+    second.wait()
+    orow = owners[...]
     above = lax.broadcasted_iota(jnp.int32, (ROWS, ROWS), 0)
     along = lax.broadcasted_iota(jnp.int32, (ROWS, ROWS), 1)
     ocol = jnp.sum(jnp.where(above == along, orow, 0), axis=1, keepdims=True)
@@ -292,11 +299,12 @@
     table, slot = pl.pallas_call(
         request_kernel,
         out_shape=(jax.ShapeDtypeStruct((OWNERS, 128), jnp.int32), jax.ShapeDtypeStruct((ROWS, 1), jnp.int32)),
-        in_specs=[vmem()] * 2,
+        in_specs=[anywhere()] * 2,
         out_specs=(vmem(), vmem()),
+        scratch_shapes=[pltpu.VMEM((1, ROWS), jnp.int32)] * 2 + [pltpu.SemaphoreType.DMA((2,))],
         compiler_params=limit(4),
         name="requests",
-    )(site_owner.reshape(1, ROWS), site_row)
+    )(*(pltpu.with_memory_space_constraint(v, pltpu.HBM) for v in (site_owner.reshape(1, ROWS), site_row)))
     wanted = lax.all_to_all(table, "seq", split_axis=0, concat_axis=0, tiled=True)
     found = variant_table[wanted[:, :SLOTS].reshape(OWNERS * SLOTS)]
     fetched = lax.all_to_all(found, "seq", split_axis=0, concat_axis=0, tiled=True)
@@ -320,8 +328,12 @@
         name="conv",
     )(normed, rim, conv_weight)
     own = [x]
-    for _ in range(HOPS):
+    for _ in range(HOPS - 1):
         own.append(lax.ppermute(own[-1], "seq", ahead))
+    ring, reach = 2 * Z, 2 * HOPS
+    behind = [i // ring * ring + (i - 6) % ring for i in range(count - reach)]
+    far = lax.ppermute(x, "seq", list(enumerate(behind)))
+    own.append(lax.ppermute(far, "seq", [(b, i + reach) for i, b in enumerate(behind)]))
     other = []
     for hop in range(HOPS + 1):
         other.append(lax.ppermute(own[hop], "seq", swap))

time: 191 us -> 210 us (1.099)
  waiting for transfers between devices: 50.4 us -> 77.8 us
  starting transfers between devices: 33.2 us -> 24.2 us
    ppermute x1, waiting for transfers between devices: 12.2 us -> 27.6 us  [local(): out_in = lax.ppermute(half, ('seq', 'fsdp'), beyond)]
    ppermute x1, starting transfers between devices: 14 us -> 0.67 us  [local(): aux_pair = lax.ppermute(aux_in, 'seq', swap)]
    ppermute x1, waiting for transfers between devices: 15.6 us -> 23.3 us  [local(): aux_in = lax.ppermute(aux, ('seq', 'fsdp'), beyond)]
    ppermute x4 -> x3, waiting for transfers between devices: 18.1 us -> 24.3 us  [local(): own.append(lax.ppermute(own[-1], 'seq', ahead))]
    ppermute x0 -> x2, starting transfers between devices: none -> 5.63 us  [the longest x1 3.71 us: local(): far = lax.ppermute(x, 'seq', list(enumerate(behind)))]
    ppermute x4 -> x3, starting transfers between devices: 13.4 us -> 9.56 us  [local(): own.append(lax.ppermute(own[-1], 'seq', ahead))]
    ppermute x1, starting transfers between devices: 0.09 us -> 2.27 us  [local(): out_in = lax.ppermute(half, ('seq', 'fsdp'), beyond)]
  transfers between devices with their start and end apart: 16 -> 17, of which waited for: 7 -> 6; matrix products, arithmetic and copies ran while one was open for 0% -> 0% of each run, Pallas kernels for 16% -> 15%
where the time goes in v5:
time: 210 us; the launch traced here: 209 us
  waiting for transfers between devices  77.8 us (37%)
  blocking collectives  63.3 us (30%)
  Pallas kernels  35.7 us (17%)
  starting transfers between devices  24.2 us (12%)
  local copies, waits for them, and re-layouts  7.35 us (4%)
    all_to_all x1, blocking collectives, local(): lax.all_to_all(found, 'seq', split_axis=0, concat_axis=0, tiled=True)  37.7 us
    ppermute x1, waiting for transfers between devices, local(): out_in = lax.ppermute(half, ('seq', 'fsdp'), beyond)  27.6 us
    all_to_all x1, blocking collectives, local(): lax.all_to_all(table, 'seq', split_axis=0, concat_axis=0, tiled=True)  25.6 us
    ppermute x3, waiting for transfers between devices, local(): own.append(lax.ppermute(own[-1], 'seq', ahead))  24.3 us
    ppermute x1, waiting for transfers between devices, local(): aux_in = lax.ppermute(aux, ('seq', 'fsdp'), beyond)  23.3 us
    pallas_call x4, Pallas kernels, local(): pl.pallas_call(functools.partial(score_block, hop), out_shape=(jax.ShapeD...  16.8 us
    pallas_call x1, Pallas kernels, local(): pl.pallas_call(attend_kernel, out_shape=(jax.ShapeDtypeStruct((ROWS, HALF...  10.7 us
    ppermute x3, starting transfers between devices, local(): own.append(lax.ppermute(own[-1], 'seq', ahead))  9.56 us
  transfers between devices with their start and end apart: 17, of which 6 were waited for; matrix products, arithmetic and copies ran while one was open for 0% of the time, Pallas kernels for 15%

profile of v5, /device:TPU:25, one launch (start us, length us, event | category | flops | bytes accessed | tf_op | source)
XLA Modules:
  0.0 208.6 jit_solution(7373511624946031220)
XLA Ops:
  0.0 1.1 requests.1
  1.1 25.6 %all_to_all.23 = s32[128,1,128]{2,1,0:T(1,128)S(1)} all-to-all(s32[128,1,128]{2,1,0:T(1,128)S(1)} %bitcast.11), channel_id=1, replica_groups=mesh['seq'=128,'fsdp'=2] {'seq'}, dimensions={0} | all-to-all | bytes 131072 | tf_op jit(solution)/shard_map/all_to_all | solution.py:308
  26.7 0.1 reshape.45
  26.9 0.0 copy-start.2
  26.9 5.5 %gather_fusion = bf16[512,1024]{1,0:T(8,128)(2,1)S(1)} fusion(bf16[2048,1024]{1,0:T(8,128)(2,1)} %param.12, s32[1024]{0:T(1024)S(1)} %pad_clamp_fusion), kind=kCustom, calls=%fused_computation | custom fusion | bytes 2099200 | tf_op jit(solution)/shard_map/gather | solution.py:309
  32.3 0.0 copy-start.1
  32.3 0.4 all_to_all.18
  32.8 37.7 %all_to_all.24 = bf16[128,4,1024]{2,1,0:T(4,128)(2,1)} all-to-all(bf16[128,4,1024]{2,1,0:T(4,128)(2,1)S(1)} %all_to_all.18), channel_id=1, replica_groups=mesh['seq'=128,'fsdp'=2] {'seq'}, dimensions={0} | all-to-all | bytes 2097152 | tf_op jit(solution)/shard_map/all_to_all | solution.py:310
  70.5 1.3 all_to_all.20.fetched
  71.8 1.6 norm.1
  73.4 2.0 collective-permute-start
  75.4 1.0 collective-permute-done.rim
  76.4 1.0 conv.1.own
  77.5 3.8 %collective-permute-start.8 = (bf16[256,1024]{1,0:T(8,128)(2,1)S(1)}, bf16[256,1024]{1,0:T(8,128)(2,1)S(1)}, u32[]{:S(2)}, u32[]{:S(2)}) collective-permute-start(bf16[256,1024]{1,0:T(8,128)(2,1)S(1)} %conv.1.own), channel_id=1, source_target_pairs={{0,4},{2,6},{4,8},{6,10},{8,12},{10,14},{12,16},{14,18},{16,20},{1... | collective-permute-start | bytes 1572872 | tf_op jit(solution)/shard_map/ppermute | solution.py:332
  81.3 1.9 slabs.1
  83.2 0.1 collective-permute-start.3
  83.3 0.4 collective-permute-start.2
  83.7 2.3 %collective-permute-start.15 = (bf16[512,512]{1,0:T(8,128)(2,1)S(1)}, bf16[512,512]{1,0:T(8,128)(2,1)S(1)}, u32[]{:S(2)}, u32[]{:S(2)}) collective-permute-start(bf16[512,512]{1,0:T(8,128)(2,1)S(1)} %get-tuple-element.62), channel_id=1, source_target_pairs={{0,129},{1,128},{2,131},{3,130},{4,133},{5,132},{6,135},{7,134},{8... | collective-permute-start | bytes 1572872 | tf_op jit(solution)/shard_map/ppermute | solution.py:295
  86.0 6.0 %collective-permute-done.8.own = bf16[256,1024]{1,0:T(8,128)(2,1)S(1)} collective-permute-done((bf16[256,1024]{1,0:T(8,128)(2,1)S(1)}, bf16[256,1024]{1,0:T(8,128)(2,1)S(1)}, u32[]{:S(2)}, u32[]{:S(2)}) %collective-permute-start.8) | collective-permute-done | bytes 524320 | tf_op jit(solution)/shard_map/ppermute | solution.py:332
  92.0 3.8 %collective-permute-start.10 = (bf16[256,1024]{1,0:T(8,128)(2,1)S(1)}, bf16[256,1024]{1,0:T(8,128)(2,1)S(1)}, u32[]{:S(2)}, u32[]{:S(2)}) collective-permute-start(bf16[256,1024]{1,0:T(8,128)(2,1)S(1)} %collective-permute-done.8.own), channel_id=1, source_target_pairs={{0,4},{2,6},{4,8},{6,10},{8,12},{10,14},{12,16},{14,18},{16,20},{1... | collective-permute-start | bytes 1572872 | tf_op jit(solution)/shard_map/ppermute | solution.py:332
  95.9 3.7 %collective-permute-start.5 = (bf16[256,1024]{1,0:T(8,128)(2,1)S(1)}, bf16[256,1024]{1,0:T(8,128)(2,1)S(1)}, u32[]{:S(2)}, u32[]{:S(2)}) collective-permute-start(bf16[256,1024]{1,0:T(8,128)(2,1)S(1)} %conv.1.own), channel_id=1, source_target_pairs={{0,20},{2,22},{4,24},{6,26},{8,28},{10,30},{12,0},{14,2},{16,4},{1... | collective-permute-start | bytes 1572872 | tf_op jit(solution)/shard_map/ppermute | solution.py:335
  99.6 23.3 %collective-permute-done.3.aux_in = bf16[1024,256]{1,0:T(8,128)(2,1)S(1)} collective-permute-done((bf16[1024,256]{1,0:T(8,128)(2,1)S(1)}, bf16[1024,256]{1,0:T(8,128)(2,1)S(1)}, u32[]{:S(2)}, u32[]{:S(2)}) %collective-permute-start.3) | collective-permute-done | bytes 524320 | tf_op jit(solution)/shard_map/ppermute | solution.py:294
  122.9 0.7 collective-permute-start.4
  123.6 27.6 %collective-permute-done.15.w_mine = bf16[512,512]{1,0:T(8,128)(2,1)S(1)} collective-permute-done((bf16[512,512]{1,0:T(8,128)(2,1)S(1)}, bf16[512,512]{1,0:T(8,128)(2,1)S(1)}, u32[]{:S(2)}, u32[]{:S(2)}) %collective-permute-start.15) | collective-permute-done | bytes 524320 | tf_op jit(solution)/shard_map/ppermute | solution.py:295
  151.2 0.5 collective-permute-start.1
  151.6 0.0 collective-permute-done.10.own
  151.7 1.9 collective-permute-start.12
  153.6 1.9 collective-permute-start.6
  155.5 0.0 collective-permute-done.4.aux_pair
  155.5 0.1 collective-permute-start.9
  155.6 0.0 collective-permute-done.2.main_in
  155.6 0.5 collective-permute-start.11
  156.1 0.3 weights.1
  156.4 0.3 collective-permute-start.16
  156.7 0.7 queries.1.q_ref.refs_0_
  157.4 18.2 %collective-permute-done.12.own = bf16[256,1024]{1,0:T(8,128)(2,1)S(1)} collective-permute-done((bf16[256,1024]{1,0:T(8,128)(2,1)S(1)}, bf16[256,1024]{1,0:T(8,128)(2,1)S(1)}, u32[]{:S(2)}, u32[]{:S(2)}) %collective-permute-start.12) | collective-permute-done | bytes 524320 | tf_op jit(solution)/shard_map/ppermute | solution.py:332
  175.7 1.5 collective-permute-start.13
  177.2 3.8 %near.4 = (bf16[512,512]{1,0:T(8,128)(2,1)S(1)}, f32[6144,256]{1,0:T(8,128)S(1)}, f32[2,256,128]{2,1,0:T(8,128)S(1)}, f32[2,256,128]{2,1,0:T(8,128)S(1)}) custom-call(bf16[256,1024]{1,0:T(8,128)(2,1)S(1)} %conv.1.own, bf16[256,1024]{1,0:T(8,128)(2,1)S(1)} %collective-permute-done.1.other, bf16[1024,512]{1,0:T(8,128)(2,1)S(1)} %get-tuple-element.42.wk.refs_3_, ...), custom_call_target="tpu_custom_call" | custom-call | flops 2000000000 | bytes 4194304 | tf_op jit(solution)/shard_map/near/pallas_call | solution.py:367
  181.1 0.2 collective-permute-start.7
  181.2 4.3 %near.5 = (bf16[512,512]{1,0:T(8,128)(2,1)S(1)}, f32[8192,256]{1,0:T(8,128)S(1)}, f32[2,256,128]{2,1,0:T(8,128)S(1)}, f32[2,256,128]{2,1,0:T(8,128)S(1)}) custom-call(bf16[256,1024]{1,0:T(8,128)(2,1)S(1)} %collective-permute-done.8.own, bf16[256,1024]{1,0:T(8,128)(2,1)S(1)} %collective-permute-done.9.other, ...), custom_call_target="tpu_custom_call" | custom-call | flops 2000000000 | bytes 4194304 | tf_op jit(solution)/shard_map/near/pallas_call | solution.py:367
  185.6 4.3 %near.6 = (bf16[512,512]{1,0:T(8,128)(2,1)S(1)}, f32[8192,256]{1,0:T(8,128)S(1)}, f32[2,256,128]{2,1,0:T(8,128)S(1)}, f32[2,256,128]{2,1,0:T(8,128)S(1)}) custom-call(bf16[256,1024]{1,0:T(8,128)(2,1)S(1)} %collective-permute-done.10.own, bf16[256,1024]{1,0:T(8,128)(2,1)S(1)} %collective-permute-done.11.other, ...), custom_call_target="tpu_custom_call" | custom-call | flops 2000000000 | bytes 4194304 | tf_op jit(solution)/shard_map/near/pallas_call | solution.py:367
  189.9 4.3 %near.7 = (bf16[512,512]{1,0:T(8,128)(2,1)S(1)}, f32[8192,256]{1,0:T(8,128)S(1)}, f32[2,256,128]{2,1,0:T(8,128)S(1)}, f32[2,256,128]{2,1,0:T(8,128)S(1)}) custom-call(bf16[256,1024]{1,0:T(8,128)(2,1)S(1)} %collective-permute-done.12.own, bf16[256,1024]{1,0:T(8,128)(2,1)S(1)} %collective-permute-done.13.other, ...), custom_call_target="tpu_custom_call" | custom-call | flops 2000000000 | bytes 4194304 | tf_op jit(solution)/shard_map/near/pallas_call | solution.py:367
  194.2 0.0 copy-start
  194.2 0.0 copy-start.3
  194.3 10.7 %attend.1 = (f32[256,512]{1,0:T(8,128)S(1)}, f32[256,512]{1,0:T(8,128)S(1)}) custom-call(bf16[512,512]{1,0:T(8,128)(2,1)S(1)} %queries.1.q_ref.refs_0_, bf16[256,1024]{1,0:T(8,128)(2,1)S(1)} %collective-permute-done.6.refs_1_, bf16[256,1024]{1,0:T(8,128)(2,1)S(1)} %collective-permute-done.7.refs_2_, bf16[1024,512]{1,0:T(8,128)(2,1)S(1)} %get-tuple-element.42.wk.refs_3_, ...), custom_call_target="tpu_custom_call" | custom-call | flops 5000000000 | bytes 6291456 | tf_op jit(solution)/shard_map/attend/pallas_call | solution.py:383
  205.0 0.5 collective-permute-start.14
  205.5 1.5 collective-permute-done.14.received
  207.1 1.6 project.1
  (14 shorter events, 0.0 us)
Async XLA Ops:
  26.9 44.9 %copy-start.2 = (f32[1024]{0:T(1024)S(1)}, f32[1024]{0:T(1024)}, u32[]{:S(2)}) copy-start(f32[1024]{0:T(1024)} %param.13) | copy-start | bytes 12292
  32.3 44.1 %copy-start.1 = (bf16[7,1024]{1,0:T(8,128)(2,1)S(1)}, bf16[7,1024]{1,0:T(8,128)(2,1)}, u32[]{:S(2)}) copy-start(bf16[7,1024]{1,0:T(8,128)(2,1)} %taps.1) | copy-start | bytes 43012
  73.4 3.1 %collective-permute-start = (bf16[8,1024]{1,0:T(8,128)(2,1)S(1)}, bf16[8,1024]{1,0:T(8,128)(2,1)S(1)}, u32[]{:S(2)}, u32[]{:S(2)}) collective-permute-start(bf16[8,1024]{1,0:T(8,128)(2,1)S(1)} %get-tuple-element.37), channel_id=1, source_target_pairs={{0,2},{2,4},{4,6},{6,8},{8,10},{10,12},{12,14},{14,16},{16,18},{18... | collective-permute-start | bytes 49160 | tf_op jit(solution)/shard_map/ppermute | solution.py:320
  77.5 14.5 %collective-permute-start.8 = (bf16[256,1024]{1,0:T(8,128)(2,1)S(1)}, bf16[256,1024]{1,0:T(8,128)(2,1)S(1)}, u32[]{:S(2)}, u32[]{:S(2)}) collective-permute-start(bf16[256,1024]{1,0:T(8,128)(2,1)S(1)} %conv.1.own), channel_id=1, source_target_pairs={{0,4},{2,6},{4,8},{6,10},{8,12},{10,14},{12,16},{14,18},{16,20},{1... | collective-permute-start | bytes 1572872 | tf_op jit(solution)/shard_map/ppermute | solution.py:332
  83.2 39.7 %collective-permute-start.3 = (bf16[1024,256]{1,0:T(8,128)(2,1)S(1)}, bf16[1024,256]{1,0:T(8,128)(2,1)S(1)}, u32[]{:S(2)}, u32[]{:S(2)}) collective-permute-start(bf16[1024,256]{1,0:T(8,128)(2,1)S(1)} %get-tuple-element.40), channel_id=1, source_target_pairs={{0,129},{1,128},{2,131},{3,130},{4,133},{5,132},{6,135},{7,134},{8... | collective-permute-start | bytes 1572872 | tf_op jit(solution)/shard_map/ppermute | solution.py:294
  83.3 72.3 %collective-permute-start.2 = (bf16[1024,512]{1,0:T(8,128)(2,1)S(1)}, bf16[1024,512]{1,0:T(8,128)(2,1)S(1)}, u32[]{:S(2)}, u32[]{:S(2)}) collective-permute-start(bf16[1024,512]{1,0:T(8,128)(2,1)S(1)} %get-tuple-element.39.main), channel_id=1, source_target_pairs={{0,1},{1,0},{2,3},{3,2},{4,5},{5,4},{6,7},{7,6},{8,9},{9,8},{10,11... | collective-permute-start | bytes 3145736 | tf_op jit(solution)/shard_map/ppermute | solution.py:293
  83.7 67.4 %collective-permute-start.15 = (bf16[512,512]{1,0:T(8,128)(2,1)S(1)}, bf16[512,512]{1,0:T(8,128)(2,1)S(1)}, u32[]{:S(2)}, u32[]{:S(2)}) collective-permute-start(bf16[512,512]{1,0:T(8,128)(2,1)S(1)} %get-tuple-element.62), channel_id=1, source_target_pairs={{0,129},{1,128},{2,131},{3,130},{4,133},{5,132},{6,135},{7,134},{8... | collective-permute-start | bytes 1572872 | tf_op jit(solution)/shard_map/ppermute | solution.py:295
  92.0 59.6 %collective-permute-start.10 = (bf16[256,1024]{1,0:T(8,128)(2,1)S(1)}, bf16[256,1024]{1,0:T(8,128)(2,1)S(1)}, u32[]{:S(2)}, u32[]{:S(2)}) collective-permute-start(bf16[256,1024]{1,0:T(8,128)(2,1)S(1)} %collective-permute-done.8.own), channel_id=1, source_target_pairs={{0,4},{2,6},{4,8},{6,10},{8,12},{10,14},{12,16},{14,18},{16,20},{1... | collective-permute-start | bytes 1572872 | tf_op jit(solution)/shard_map/ppermute | solution.py:332
  95.9 57.7 %collective-permute-start.5 = (bf16[256,1024]{1,0:T(8,128)(2,1)S(1)}, bf16[256,1024]{1,0:T(8,128)(2,1)S(1)}, u32[]{:S(2)}, u32[]{:S(2)}) collective-permute-start(bf16[256,1024]{1,0:T(8,128)(2,1)S(1)} %conv.1.own), channel_id=1, source_target_pairs={{0,20},{2,22},{4,24},{6,26},{8,28},{10,30},{12,0},{14,2},{16,4},{1... | collective-permute-start | bytes 1572872 | tf_op jit(solution)/shard_map/ppermute | solution.py:335
  122.9 32.6 %collective-permute-start.4 = (bf16[1024,256]{1,0:T(8,128)(2,1)S(1)}, bf16[1024,256]{1,0:T(8,128)(2,1)S(1)}, u32[]{:S(2)}, u32[]{:S(2)}) collective-permute-start(bf16[1024,256]{1,0:T(8,128)(2,1)S(1)} %collective-permute-done.3.aux_in), channel_id=1, source_target_pairs={{0,2},{2,0},{4,6},{6,4},{8,10},{10,8},{12,14},{14,12},{16,18},{18,... | collective-permute-start | bytes 1572872 | tf_op jit(solution)/shard_map/ppermute | solution.py:296
  151.2 5.2 %collective-permute-start.1 = (bf16[256,1024]{1,0:T(8,128)(2,1)S(1)}, bf16[256,1024]{1,0:T(8,128)(2,1)S(1)}, u32[]{:S(2)}, u32[]{:S(2)}) collective-permute-start(bf16[256,1024]{1,0:T(8,128)(2,1)S(1)} %conv.1.own), channel_id=1, source_target_pairs={{0,2},{2,0},{4,6},{6,4},{8,10},{10,8},{12,14},{14,12},{16,18},{18,... | collective-permute-start | bytes 1572872 | tf_op jit(solution)/shard_map/ppermute | solution.py:339
  151.7 24.0 %collective-permute-start.12 = (bf16[256,1024]{1,0:T(8,128)(2,1)S(1)}, bf16[256,1024]{1,0:T(8,128)(2,1)S(1)}, u32[]{:S(2)}, u32[]{:S(2)}) collective-permute-start(bf16[256,1024]{1,0:T(8,128)(2,1)S(1)} %collective-permute-done.10.own), channel_id=1, source_target_pairs={{0,4},{2,6},{4,8},{6,10},{8,12},{10,14},{12,16},{14,18},{16,20},{1... | collective-permute-start | bytes 1572872 | tf_op jit(solution)/shard_map/ppermute | solution.py:332
  153.6 27.5 %collective-permute-start.6 = (bf16[256,1024]{1,0:T(8,128)(2,1)S(1)}, bf16[256,1024]{1,0:T(8,128)(2,1)S(1)}, u32[]{:S(2)}, u32[]{:S(2)}) collective-permute-start(bf16[256,1024]{1,0:T(8,128)(2,1)S(1)} %collective-permute-done.5), channel_id=1, source_target_pairs={{20,16},{22,18},{24,20},{26,22},{28,24},{30,26},{0,28},{2,30},{4,3... | collective-permute-start | bytes 1572872 | tf_op jit(solution)/shard_map/ppermute | solution.py:336
  155.5 25.7 %collective-permute-start.9 = (bf16[256,1024]{1,0:T(8,128)(2,1)S(1)}, bf16[256,1024]{1,0:T(8,128)(2,1)S(1)}, u32[]{:S(2)}, u32[]{:S(2)}) collective-permute-start(bf16[256,1024]{1,0:T(8,128)(2,1)S(1)} %collective-permute-done.8.own), channel_id=1, source_target_pairs={{0,2},{2,0},{4,6},{6,4},{8,10},{10,8},{12,14},{14,12},{16,18},{18,... | collective-permute-start | bytes 1572872 | tf_op jit(solution)/shard_map/ppermute | solution.py:339
  155.6 29.9 %collective-permute-start.11 = (bf16[256,1024]{1,0:T(8,128)(2,1)S(1)}, bf16[256,1024]{1,0:T(8,128)(2,1)S(1)}, u32[]{:S(2)}, u32[]{:S(2)}) collective-permute-start(bf16[256,1024]{1,0:T(8,128)(2,1)S(1)} %collective-permute-done.10.own), channel_id=1, source_target_pairs={{0,2},{2,0},{4,6},{6,4},{8,10},{10,8},{12,14},{14,12},{16,18},{18,... | collective-permute-start | bytes 1572872 | tf_op jit(solution)/shard_map/ppermute | solution.py:339
  156.4 49.1 %collective-permute-start.16 = (bf16[512,512]{1,0:T(8,128)(2,1)S(1)}, bf16[512,512]{1,0:T(8,128)(2,1)S(1)}, u32[]{:S(2)}, u32[]{:S(2)}) collective-permute-start(bf16[512,512]{1,0:T(8,128)(2,1)S(1)} %collective-permute-done.15.w_mine), channel_id=1, source_target_pairs={{0,2},{2,0},{4,6},{6,4},{8,10},{10,8},{12,14},{14,12},{16,18},{18,... | collective-permute-start | bytes 1572872 | tf_op jit(solution)/shard_map/ppermute | solution.py:297
  175.7 14.2 %collective-permute-start.13 = (bf16[256,1024]{1,0:T(8,128)(2,1)S(1)}, bf16[256,1024]{1,0:T(8,128)(2,1)S(1)}, u32[]{:S(2)}, u32[]{:S(2)}) collective-permute-start(bf16[256,1024]{1,0:T(8,128)(2,1)S(1)} %collective-permute-done.12.own), channel_id=1, source_target_pairs={{0,2},{2,0},{4,6},{6,4},{8,10},{10,8},{12,14},{14,12},{16,18},{18,... | collective-permute-start | bytes 1572872 | tf_op jit(solution)/shard_map/ppermute | solution.py:339
  181.1 13.2 %collective-permute-start.7 = (bf16[256,1024]{1,0:T(8,128)(2,1)S(1)}, bf16[256,1024]{1,0:T(8,128)(2,1)S(1)}, u32[]{:S(2)}, u32[]{:S(2)}) collective-permute-start(bf16[256,1024]{1,0:T(8,128)(2,1)S(1)} %collective-permute-done.6.refs_1_), channel_id=1, source_target_pairs={{0,2},{2,0},{4,6},{6,4},{8,10},{10,8},{12,14},{14,12},{16,18},{18,... | collective-permute-start | bytes 1572872 | tf_op jit(solution)/shard_map/ppermute | solution.py:339
  194.2 12.8 %copy-start = (bf16[1024,512]{1,0:T(8,128)(2,1)S(1)}, bf16[1024,512]{1,0:T(8,128)(2,1)}, u32[]{:S(2)}) copy-start(bf16[1024,512]{1,0:T(8,128)(2,1)} %w_here.1) | copy-start | bytes 3145732
  194.2 12.8 %copy-start.3 = (f32[1024]{0:T(1024)S(1)}, f32[1024]{0:T(1024)}, u32[]{:S(2)}) copy-start(f32[1024]{0:T(1024)} %param.17) | copy-start | bytes 12292
  205.0 2.1 collective-permute-start.14

commit v6 on v5

--- a/solution.py
+++ b/solution.py
@@ -103,17 +103,17 @@
     slot[...] = ocol * SLOTS + rank_col
 
 
-def norm_kernel(fetched, slot, dna, gain, normed, rim, staged, sem):
-    copy = pltpu.make_async_copy(dna, staged, sem)
+def norm_kernel(first, fetched, slot, dna, gain, normed, staged, sem):
+    rows = ROWS - first
+    copy = pltpu.make_async_copy(dna.at[pl.ds(first, rows), :], staged, sem)
     copy.start()
-    pick = (lax.broadcasted_iota(jnp.int32, (ROWS, OWNERS * SLOTS), 1) == slot[...]).astype(f32).astype(bf16)
+    index = slot[pl.ds(first, rows), :]
+    pick = (lax.broadcasted_iota(jnp.int32, (rows, OWNERS * SLOTS), 1) == index).astype(f32).astype(bf16)
     site = jnp.dot(pick, fetched[...], preferred_element_type=f32)
     copy.wait()
     resid = staged[...].astype(f32) + site
     mean = jnp.mean(resid * resid, axis=1, keepdims=True)
-    out = (resid * lax.rsqrt(mean + EPSILON) * gain[...]).astype(bf16)
-    normed[...] = out
-    rim[...] = out[ROWS - 8 :]
+    normed[...] = (resid * lax.rsqrt(mean + EPSILON) * gain[...]).astype(bf16)
 
 
 def conv_kernel(normed, rim, taps, out, padded):
@@ -308,15 +308,20 @@
     wanted = lax.all_to_all(table, "seq", split_axis=0, concat_axis=0, tiled=True)
     found = variant_table[wanted[:, :SLOTS].reshape(OWNERS * SLOTS)]
     fetched = lax.all_to_all(found, "seq", split_axis=0, concat_axis=0, tiled=True)
-    normed, edge = pl.pallas_call(
-        norm_kernel,
-        out_shape=(jax.ShapeDtypeStruct((ROWS, D), bf16), jax.ShapeDtypeStruct((8, D), bf16)),
-        in_specs=[vmem(), vmem(), anywhere(), vmem()],
-        out_specs=(vmem(), vmem()),
-        scratch_shapes=[pltpu.VMEM((ROWS, D), bf16), pltpu.SemaphoreType.DMA],
-        compiler_params=limit(10),
-    name="norm",
-    )(fetched, slot, pltpu.with_memory_space_constraint(dna_embed[0], pltpu.HBM), norm_gain.reshape(1, D))
+
+    def norm(first):
+        return pl.pallas_call(
+            functools.partial(norm_kernel, first),
+            out_shape=jax.ShapeDtypeStruct((ROWS - first, D), bf16),
+            in_specs=[vmem(), vmem(), anywhere(), vmem()],
+            out_specs=vmem(),
+            scratch_shapes=[pltpu.VMEM((ROWS - first, D), bf16), pltpu.SemaphoreType.DMA],
+            compiler_params=limit(10),
+            name="norm",
+        )(fetched, slot, pltpu.with_memory_space_constraint(dna_embed[0], pltpu.HBM), norm_gain.reshape(1, D))
+
+    edge = norm(ROWS - 8)
+    normed = norm(0)
     rim = lax.ppermute(edge, "seq", [(i, i + 1) for i in range(count - 1)])
     x = pl.pallas_call(
         conv_kernel,

time: 210 us -> 210 us (level)
  transfers between devices with their start and end apart: 17 -> 17, of which waited for: 6 -> 5; matrix products, arithmetic and copies ran while one was open for 0% -> 0% of each run, Pallas kernels for 15% -> 15%
where the time goes in v6:
time: 210 us; the launch traced here: 209 us
  waiting for transfers between devices  76.5 us (36%)
  blocking collectives  63.3 us (30%)
  Pallas kernels  36.7 us (17%)
  starting transfers between devices  24.7 us (12%)
  local copies, waits for them, and re-layouts  7.35 us (4%)
    all_to_all x1, blocking collectives, local(): lax.all_to_all(found, 'seq', split_axis=0, concat_axis=0, tiled=True)  37.7 us
    ppermute x1, waiting for transfers between devices, local(): out_in = lax.ppermute(half, ('seq', 'fsdp'), beyond)  27.6 us
    all_to_all x1, blocking collectives, local(): lax.all_to_all(table, 'seq', split_axis=0, concat_axis=0, tiled=True)  25.6 us
    ppermute x3, waiting for transfers between devices, local(): own.append(lax.ppermute(own[-1], 'seq', ahead))  24.7 us
    ppermute x1, waiting for transfers between devices, local(): aux_in = lax.ppermute(aux, ('seq', 'fsdp'), beyond)  22.6 us
    pallas_call x4, Pallas kernels, local(): pl.pallas_call(functools.partial(score_block, hop), out_shape=(jax.ShapeD...  16.8 us
    pallas_call x1, Pallas kernels, local(): pl.pallas_call(attend_kernel, out_shape=(jax.ShapeDtypeStruct((ROWS, HALF...  10.7 us
    ppermute x3, starting transfers between devices, local(): own.append(lax.ppermute(own[-1], 'seq', ahead))  10 us
  transfers between devices with their start and end apart: 17, of which 5 were waited for; matrix products, arithmetic and copies ran while one was open for 0% of the time, Pallas kernels for 15%

profile of v6, /device:TPU:25, one launch (start us, length us, event | category | flops | bytes accessed | tf_op | source)
XLA Modules:
  0.0 208.8 jit_solution(2817579627757591092)
XLA Ops:
  0.0 1.1 requests.1
  1.1 25.6 %all_to_all.23 = s32[128,1,128]{2,1,0:T(1,128)S(1)} all-to-all(s32[128,1,128]{2,1,0:T(1,128)S(1)} %bitcast.11), channel_id=1, replica_groups=mesh['seq'=128,'fsdp'=2] {'seq'}, dimensions={0} | all-to-all | bytes 131072 | tf_op jit(solution)/shard_map/all_to_all | solution.py:308
  26.7 0.1 reshape.46
  26.9 0.0 copy-start.2
  26.9 5.5 %gather_fusion = bf16[512,1024]{1,0:T(8,128)(2,1)S(1)} fusion(bf16[2048,1024]{1,0:T(8,128)(2,1)} %param.12, s32[1024]{0:T(1024)S(1)} %pad_clamp_fusion), kind=kCustom, calls=%fused_computation | custom fusion | bytes 2099200 | tf_op jit(solution)/shard_map/gather | solution.py:309
  32.3 0.0 copy-start.1
  32.3 0.4 all_to_all.18
  32.8 37.7 %all_to_all.24 = bf16[128,4,1024]{2,1,0:T(4,128)(2,1)} all-to-all(bf16[128,4,1024]{2,1,0:T(4,128)(2,1)S(1)} %all_to_all.18), channel_id=1, replica_groups=mesh['seq'=128,'fsdp'=2] {'seq'}, dimensions={0} | all-to-all | bytes 2097152 | tf_op jit(solution)/shard_map/all_to_all | solution.py:310
  70.4 1.3 all_to_all.20.fetched
  71.8 1.0 norm.3
  72.8 2.0 collective-permute-start
  74.8 1.6 norm.2.normed
  76.4 1.1 conv.1.own
  77.4 4.0 %collective-permute-start.8 = (bf16[256,1024]{1,0:T(8,128)(2,1)S(1)}, bf16[256,1024]{1,0:T(8,128)(2,1)S(1)}, u32[]{:S(2)}, u32[]{:S(2)}) collective-permute-start(bf16[256,1024]{1,0:T(8,128)(2,1)S(1)} %conv.1.own), channel_id=1, source_target_pairs={{0,4},{2,6},{4,8},{6,10},{8,12},{10,14},{12,16},{14,18},{16,20},{1... | collective-permute-start | bytes 1572872 | tf_op jit(solution)/shard_map/ppermute | solution.py:337
  81.5 1.9 slabs.1
  83.4 0.1 collective-permute-start.3
  83.5 0.4 collective-permute-start.2
  83.9 2.3 %collective-permute-start.15 = (bf16[512,512]{1,0:T(8,128)(2,1)S(1)}, bf16[512,512]{1,0:T(8,128)(2,1)S(1)}, u32[]{:S(2)}, u32[]{:S(2)}) collective-permute-start(bf16[512,512]{1,0:T(8,128)(2,1)S(1)} %get-tuple-element.58), channel_id=1, source_target_pairs={{0,129},{1,128},{2,131},{3,130},{4,133},{5,132},{6,135},{7,134},{8... | collective-permute-start | bytes 1572872 | tf_op jit(solution)/shard_map/ppermute | solution.py:295
  86.2 6.5 %collective-permute-done.8.own = bf16[256,1024]{1,0:T(8,128)(2,1)S(1)} collective-permute-done((bf16[256,1024]{1,0:T(8,128)(2,1)S(1)}, bf16[256,1024]{1,0:T(8,128)(2,1)S(1)}, u32[]{:S(2)}, u32[]{:S(2)}) %collective-permute-start.8) | collective-permute-done | bytes 524320 | tf_op jit(solution)/shard_map/ppermute | solution.py:337
  92.7 4.1 %collective-permute-start.10 = (bf16[256,1024]{1,0:T(8,128)(2,1)S(1)}, bf16[256,1024]{1,0:T(8,128)(2,1)S(1)}, u32[]{:S(2)}, u32[]{:S(2)}) collective-permute-start(bf16[256,1024]{1,0:T(8,128)(2,1)S(1)} %collective-permute-done.8.own), channel_id=1, source_target_pairs={{0,4},{2,6},{4,8},{6,10},{8,12},{10,14},{12,16},{14,18},{16,20},{1... | collective-permute-start | bytes 1572872 | tf_op jit(solution)/shard_map/ppermute | solution.py:337
  96.8 3.7 %collective-permute-start.5 = (bf16[256,1024]{1,0:T(8,128)(2,1)S(1)}, bf16[256,1024]{1,0:T(8,128)(2,1)S(1)}, u32[]{:S(2)}, u32[]{:S(2)}) collective-permute-start(bf16[256,1024]{1,0:T(8,128)(2,1)S(1)} %conv.1.own), channel_id=1, source_target_pairs={{0,20},{2,22},{4,24},{6,26},{8,28},{10,30},{12,0},{14,2},{16,4},{1... | collective-permute-start | bytes 1572872 | tf_op jit(solution)/shard_map/ppermute | solution.py:340
  100.5 22.6 %collective-permute-done.3.aux_in = bf16[1024,256]{1,0:T(8,128)(2,1)S(1)} collective-permute-done((bf16[1024,256]{1,0:T(8,128)(2,1)S(1)}, bf16[1024,256]{1,0:T(8,128)(2,1)S(1)}, u32[]{:S(2)}, u32[]{:S(2)}) %collective-permute-start.3) | collective-permute-done | bytes 524320 | tf_op jit(solution)/shard_map/ppermute | solution.py:294
  123.1 0.7 collective-permute-start.4
  123.7 27.6 %collective-permute-done.15.w_mine = bf16[512,512]{1,0:T(8,128)(2,1)S(1)} collective-permute-done((bf16[512,512]{1,0:T(8,128)(2,1)S(1)}, bf16[512,512]{1,0:T(8,128)(2,1)S(1)}, u32[]{:S(2)}, u32[]{:S(2)}) %collective-permute-start.15) | collective-permute-done | bytes 524320 | tf_op jit(solution)/shard_map/ppermute | solution.py:295
  151.3 0.5 collective-permute-start.1
  151.8 0.0 collective-permute-done.10.own
  151.8 1.9 collective-permute-start.12
  153.7 1.9 collective-permute-start.6
  155.7 0.0 collective-permute-done.4.aux_pair
  155.7 0.1 collective-permute-start.9
  155.8 0.0 collective-permute-done.2.main_in
  155.8 0.5 collective-permute-start.11
  156.3 0.3 weights.1
  156.6 0.3 collective-permute-start.16
  156.9 0.7 queries.1.q_ref.refs_0_
  157.6 18.2 %collective-permute-done.12.own = bf16[256,1024]{1,0:T(8,128)(2,1)S(1)} collective-permute-done((bf16[256,1024]{1,0:T(8,128)(2,1)S(1)}, bf16[256,1024]{1,0:T(8,128)(2,1)S(1)}, u32[]{:S(2)}, u32[]{:S(2)}) %collective-permute-start.12) | collective-permute-done | bytes 524320 | tf_op jit(solution)/shard_map/ppermute | solution.py:337
  175.8 1.5 collective-permute-start.13
  177.3 3.8 %near.4 = (bf16[512,512]{1,0:T(8,128)(2,1)S(1)}, f32[6144,256]{1,0:T(8,128)S(1)}, f32[2,256,128]{2,1,0:T(8,128)S(1)}, f32[2,256,128]{2,1,0:T(8,128)S(1)}) custom-call(bf16[256,1024]{1,0:T(8,128)(2,1)S(1)} %conv.1.own, bf16[256,1024]{1,0:T(8,128)(2,1)S(1)} %collective-permute-done.1.other, bf16[1024,512]{1,0:T(8,128)(2,1)S(1)} %get-tuple-element.38.wk.refs_3_, ...), custom_call_target="tpu_custom_call" | custom-call | flops 2000000000 | bytes 4194304 | tf_op jit(solution)/shard_map/near/pallas_call | solution.py:372
  181.2 0.2 collective-permute-start.7
  181.4 4.3 %near.5 = (bf16[512,512]{1,0:T(8,128)(2,1)S(1)}, f32[8192,256]{1,0:T(8,128)S(1)}, f32[2,256,128]{2,1,0:T(8,128)S(1)}, f32[2,256,128]{2,1,0:T(8,128)S(1)}) custom-call(bf16[256,1024]{1,0:T(8,128)(2,1)S(1)} %collective-permute-done.8.own, bf16[256,1024]{1,0:T(8,128)(2,1)S(1)} %collective-permute-done.9.other, ...), custom_call_target="tpu_custom_call" | custom-call | flops 2000000000 | bytes 4194304 | tf_op jit(solution)/shard_map/near/pallas_call | solution.py:372
  185.7 4.3 %near.6 = (bf16[512,512]{1,0:T(8,128)(2,1)S(1)}, f32[8192,256]{1,0:T(8,128)S(1)}, f32[2,256,128]{2,1,0:T(8,128)S(1)}, f32[2,256,128]{2,1,0:T(8,128)S(1)}) custom-call(bf16[256,1024]{1,0:T(8,128)(2,1)S(1)} %collective-permute-done.10.own, bf16[256,1024]{1,0:T(8,128)(2,1)S(1)} %collective-permute-done.11.other, ...), custom_call_target="tpu_custom_call" | custom-call | flops 2000000000 | bytes 4194304 | tf_op jit(solution)/shard_map/near/pallas_call | solution.py:372
  190.1 4.3 %near.7 = (bf16[512,512]{1,0:T(8,128)(2,1)S(1)}, f32[8192,256]{1,0:T(8,128)S(1)}, f32[2,256,128]{2,1,0:T(8,128)S(1)}, f32[2,256,128]{2,1,0:T(8,128)S(1)}) custom-call(bf16[256,1024]{1,0:T(8,128)(2,1)S(1)} %collective-permute-done.12.own, bf16[256,1024]{1,0:T(8,128)(2,1)S(1)} %collective-permute-done.13.other, ...), custom_call_target="tpu_custom_call" | custom-call | flops 2000000000 | bytes 4194304 | tf_op jit(solution)/shard_map/near/pallas_call | solution.py:372
  194.4 0.0 copy-start
  194.4 0.0 copy-start.3
  194.4 10.7 %attend.1 = (f32[256,512]{1,0:T(8,128)S(1)}, f32[256,512]{1,0:T(8,128)S(1)}) custom-call(bf16[512,512]{1,0:T(8,128)(2,1)S(1)} %queries.1.q_ref.refs_0_, bf16[256,1024]{1,0:T(8,128)(2,1)S(1)} %collective-permute-done.6.refs_1_, bf16[256,1024]{1,0:T(8,128)(2,1)S(1)} %collective-permute-done.7.refs_2_, bf16[1024,512]{1,0:T(8,128)(2,1)S(1)} %get-tuple-element.38.wk.refs_3_, ...), custom_call_target="tpu_custom_call" | custom-call | flops 5000000000 | bytes 6291456 | tf_op jit(solution)/shard_map/attend/pallas_call | solution.py:388
  205.2 0.5 collective-permute-start.14
  205.7 1.5 collective-permute-done.14.received
  207.2 1.6 project.1
  (15 shorter events, 0.0 us)
Async XLA Ops:
  26.9 44.9 %copy-start.2 = (f32[1024]{0:T(1024)S(1)}, f32[1024]{0:T(1024)}, u32[]{:S(2)}) copy-start(f32[1024]{0:T(1024)} %param.13) | copy-start | bytes 12292
  32.3 44.0 %copy-start.1 = (bf16[7,1024]{1,0:T(8,128)(2,1)S(1)}, bf16[7,1024]{1,0:T(8,128)(2,1)}, u32[]{:S(2)}) copy-start(bf16[7,1024]{1,0:T(8,128)(2,1)} %taps.1) | copy-start | bytes 43012
  72.8 3.6 %collective-permute-start = (bf16[8,1024]{1,0:T(8,128)(2,1)S(1)}, bf16[8,1024]{1,0:T(8,128)(2,1)S(1)}, u32[]{:S(2)}, u32[]{:S(2)}) collective-permute-start(bf16[8,1024]{1,0:T(8,128)(2,1)S(1)} %norm.3), channel_id=1, source_target_pairs={{0,2},{2,4},{4,6},{6,8},{8,10},{10,12},{12,14},{14,16},{16,18},{18... | collective-permute-start | bytes 49160 | tf_op jit(solution)/shard_map/ppermute | solution.py:325
  77.4 15.2 %collective-permute-start.8 = (bf16[256,1024]{1,0:T(8,128)(2,1)S(1)}, bf16[256,1024]{1,0:T(8,128)(2,1)S(1)}, u32[]{:S(2)}, u32[]{:S(2)}) collective-permute-start(bf16[256,1024]{1,0:T(8,128)(2,1)S(1)} %conv.1.own), channel_id=1, source_target_pairs={{0,4},{2,6},{4,8},{6,10},{8,12},{10,14},{12,16},{14,18},{16,20},{1... | collective-permute-start | bytes 1572872 | tf_op jit(solution)/shard_map/ppermute | solution.py:337
  83.4 39.7 %collective-permute-start.3 = (bf16[1024,256]{1,0:T(8,128)(2,1)S(1)}, bf16[1024,256]{1,0:T(8,128)(2,1)S(1)}, u32[]{:S(2)}, u32[]{:S(2)}) collective-permute-start(bf16[1024,256]{1,0:T(8,128)(2,1)S(1)} %get-tuple-element.36), channel_id=1, source_target_pairs={{0,129},{1,128},{2,131},{3,130},{4,133},{5,132},{6,135},{7,134},{8... | collective-permute-start | bytes 1572872 | tf_op jit(solution)/shard_map/ppermute | solution.py:294
  83.5 72.3 %collective-permute-start.2 = (bf16[1024,512]{1,0:T(8,128)(2,1)S(1)}, bf16[1024,512]{1,0:T(8,128)(2,1)S(1)}, u32[]{:S(2)}, u32[]{:S(2)}) collective-permute-start(bf16[1024,512]{1,0:T(8,128)(2,1)S(1)} %get-tuple-element.35.main), channel_id=1, source_target_pairs={{0,1},{1,0},{2,3},{3,2},{4,5},{5,4},{6,7},{7,6},{8,9},{9,8},{10,11... | collective-permute-start | bytes 3145736 | tf_op jit(solution)/shard_map/ppermute | solution.py:293
  83.9 67.4 %collective-permute-start.15 = (bf16[512,512]{1,0:T(8,128)(2,1)S(1)}, bf16[512,512]{1,0:T(8,128)(2,1)S(1)}, u32[]{:S(2)}, u32[]{:S(2)}) collective-permute-start(bf16[512,512]{1,0:T(8,128)(2,1)S(1)} %get-tuple-element.58), channel_id=1, source_target_pairs={{0,129},{1,128},{2,131},{3,130},{4,133},{5,132},{6,135},{7,134},{8... | collective-permute-start | bytes 1572872 | tf_op jit(solution)/shard_map/ppermute | solution.py:295
  92.7 59.1 %collective-permute-start.10 = (bf16[256,1024]{1,0:T(8,128)(2,1)S(1)}, bf16[256,1024]{1,0:T(8,128)(2,1)S(1)}, u32[]{:S(2)}, u32[]{:S(2)}) collective-permute-start(bf16[256,1024]{1,0:T(8,128)(2,1)S(1)} %collective-permute-done.8.own), channel_id=1, source_target_pairs={{0,4},{2,6},{4,8},{6,10},{8,12},{10,14},{12,16},{14,18},{16,20},{1... | collective-permute-start | bytes 1572872 | tf_op jit(solution)/shard_map/ppermute | solution.py:337
  96.8 57.0 %collective-permute-start.5 = (bf16[256,1024]{1,0:T(8,128)(2,1)S(1)}, bf16[256,1024]{1,0:T(8,128)(2,1)S(1)}, u32[]{:S(2)}, u32[]{:S(2)}) collective-permute-start(bf16[256,1024]{1,0:T(8,128)(2,1)S(1)} %conv.1.own), channel_id=1, source_target_pairs={{0,20},{2,22},{4,24},{6,26},{8,28},{10,30},{12,0},{14,2},{16,4},{1... | collective-permute-start | bytes 1572872 | tf_op jit(solution)/shard_map/ppermute | solution.py:340
  123.1 32.6 %collective-permute-start.4 = (bf16[1024,256]{1,0:T(8,128)(2,1)S(1)}, bf16[1024,256]{1,0:T(8,128)(2,1)S(1)}, u32[]{:S(2)}, u32[]{:S(2)}) collective-permute-start(bf16[1024,256]{1,0:T(8,128)(2,1)S(1)} %collective-permute-done.3.aux_in), channel_id=1, source_target_pairs={{0,2},{2,0},{4,6},{6,4},{8,10},{10,8},{12,14},{14,12},{16,18},{18,... | collective-permute-start | bytes 1572872 | tf_op jit(solution)/shard_map/ppermute | solution.py:296
  151.3 5.2 %collective-permute-start.1 = (bf16[256,1024]{1,0:T(8,128)(2,1)S(1)}, bf16[256,1024]{1,0:T(8,128)(2,1)S(1)}, u32[]{:S(2)}, u32[]{:S(2)}) collective-permute-start(bf16[256,1024]{1,0:T(8,128)(2,1)S(1)} %conv.1.own), channel_id=1, source_target_pairs={{0,2},{2,0},{4,6},{6,4},{8,10},{10,8},{12,14},{14,12},{16,18},{18,... | collective-permute-start | bytes 1572872 | tf_op jit(solution)/shard_map/ppermute | solution.py:344
  151.8 24.0 %collective-permute-start.12 = (bf16[256,1024]{1,0:T(8,128)(2,1)S(1)}, bf16[256,1024]{1,0:T(8,128)(2,1)S(1)}, u32[]{:S(2)}, u32[]{:S(2)}) collective-permute-start(bf16[256,1024]{1,0:T(8,128)(2,1)S(1)} %collective-permute-done.10.own), channel_id=1, source_target_pairs={{0,4},{2,6},{4,8},{6,10},{8,12},{10,14},{12,16},{14,18},{16,20},{1... | collective-permute-start | bytes 1572872 | tf_op jit(solution)/shard_map/ppermute | solution.py:337
  153.7 27.5 %collective-permute-start.6 = (bf16[256,1024]{1,0:T(8,128)(2,1)S(1)}, bf16[256,1024]{1,0:T(8,128)(2,1)S(1)}, u32[]{:S(2)}, u32[]{:S(2)}) collective-permute-start(bf16[256,1024]{1,0:T(8,128)(2,1)S(1)} %collective-permute-done.5), channel_id=1, source_target_pairs={{20,16},{22,18},{24,20},{26,22},{28,24},{30,26},{0,28},{2,30},{4,3... | collective-permute-start | bytes 1572872 | tf_op jit(solution)/shard_map/ppermute | solution.py:341
  155.7 25.7 %collective-permute-start.9 = (bf16[256,1024]{1,0:T(8,128)(2,1)S(1)}, bf16[256,1024]{1,0:T(8,128)(2,1)S(1)}, u32[]{:S(2)}, u32[]{:S(2)}) collective-permute-start(bf16[256,1024]{1,0:T(8,128)(2,1)S(1)} %collective-permute-done.8.own), channel_id=1, source_target_pairs={{0,2},{2,0},{4,6},{6,4},{8,10},{10,8},{12,14},{14,12},{16,18},{18,... | collective-permute-start | bytes 1572872 | tf_op jit(solution)/shard_map/ppermute | solution.py:344
  155.8 29.9 %collective-permute-start.11 = (bf16[256,1024]{1,0:T(8,128)(2,1)S(1)}, bf16[256,1024]{1,0:T(8,128)(2,1)S(1)}, u32[]{:S(2)}, u32[]{:S(2)}) collective-permute-start(bf16[256,1024]{1,0:T(8,128)(2,1)S(1)} %collective-permute-done.10.own), channel_id=1, source_target_pairs={{0,2},{2,0},{4,6},{6,4},{8,10},{10,8},{12,14},{14,12},{16,18},{18,... | collective-permute-start | bytes 1572872 | tf_op jit(solution)/shard_map/ppermute | solution.py:344
  156.6 49.1 %collective-permute-start.16 = (bf16[512,512]{1,0:T(8,128)(2,1)S(1)}, bf16[512,512]{1,0:T(8,128)(2,1)S(1)}, u32[]{:S(2)}, u32[]{:S(2)}) collective-permute-start(bf16[512,512]{1,0:T(8,128)(2,1)S(1)} %collective-permute-done.15.w_mine), channel_id=1, source_target_pairs={{0,2},{2,0},{4,6},{6,4},{8,10},{10,8},{12,14},{14,12},{16,18},{18,... | collective-permute-start | bytes 1572872 | tf_op jit(solution)/shard_map/ppermute | solution.py:297
  175.8 14.2 %collective-permute-start.13 = (bf16[256,1024]{1,0:T(8,128)(2,1)S(1)}, bf16[256,1024]{1,0:T(8,128)(2,1)S(1)}, u32[]{:S(2)}, u32[]{:S(2)}) collective-permute-start(bf16[256,1024]{1,0:T(8,128)(2,1)S(1)} %collective-permute-done.12.own), channel_id=1, source_target_pairs={{0,2},{2,0},{4,6},{6,4},{8,10},{10,8},{12,14},{14,12},{16,18},{18,... | collective-permute-start | bytes 1572872 | tf_op jit(solution)/shard_map/ppermute | solution.py:344
  181.2 13.2 %collective-permute-start.7 = (bf16[256,1024]{1,0:T(8,128)(2,1)S(1)}, bf16[256,1024]{1,0:T(8,128)(2,1)S(1)}, u32[]{:S(2)}, u32[]{:S(2)}) collective-permute-start(bf16[256,1024]{1,0:T(8,128)(2,1)S(1)} %collective-permute-done.6.refs_1_), channel_id=1, source_target_pairs={{0,2},{2,0},{4,6},{6,4},{8,10},{10,8},{12,14},{14,12},{16,18},{18,... | collective-permute-start | bytes 1572872 | tf_op jit(solution)/shard_map/ppermute | solution.py:344
  194.4 12.8 %copy-start = (bf16[1024,512]{1,0:T(8,128)(2,1)S(1)}, bf16[1024,512]{1,0:T(8,128)(2,1)}, u32[]{:S(2)}) copy-start(bf16[1024,512]{1,0:T(8,128)(2,1)} %w_here.1) | copy-start | bytes 3145732
  194.4 12.8 %copy-start.3 = (f32[1024]{0:T(1024)S(1)}, f32[1024]{0:T(1024)}, u32[]{:S(2)}) copy-start(f32[1024]{0:T(1024)} %param.17) | copy-start | bytes 12292
  205.2 2.1 collective-permute-start.14
